TPU v7x, 256 devices: a whole 4x4x8 slice. The times are simulated.
256 devices in a mesh: rows: 8 (over z_lo, x), cols: 32 (over y, z_hi, core).
Axes of the slice: x: 4, y: 4, z: 8 (z_hi: 4, z_lo: 2; z = z_hi * 2 + z_lo), core: 2. Of those that a mesh axis runs over, the one named last changes fastest.
Arguments:
- queries: bfloat16 [65536, 1024], P(('rows', 'cols')), may hold values from -1 to 1
- attn_out: bfloat16 [65536, 1024], P(('rows', 'cols')), may hold values from -6 to 6
- out_grad: bfloat16 [65536, 1024], P(('rows', 'cols')), may hold values from -96 to 96
- log_norm: float32 [65536, 8], P(('rows', 'cols')), may hold values from 7.5 to 8.5
- leaf_kv: bfloat16 [65536, 256], P(('rows', 'cols')), may hold values from -1 to 1
- root_kv: bfloat16 [2048, 256], P('cols'), may hold values from -1 to 1
- branch_kv: bfloat16 [16, 1024, 256], P('rows', 'cols'), may hold values from -1 to 1
- branch_len: int32 [16], replicated, may hold values from 256 to 1024, as said below
- segment_ids: int32 [256, 256], P(('rows', 'cols')), may hold values from 0 to 7, never falling along the last dimension, each value on 1 to 128 neighbouring positions
- segment_branch: int32 [256, 8], P(('rows', 'cols')), may hold values from 0 to 1
Outputs:
- query_grad: bfloat16 [65536, 1024], P(('rows', 'cols'))
- leaf_kv_grad: float32 [65536, 256], P(('rows', 'cols'))
- root_kv_grad: float32 [2048, 256], P('cols')
- branch_kv_grad: float32 [16, 1024, 256], P('rows', 'cols')
Inputs may be any that keep to these rules, and one draw needn't show every extreme that they name: `branch_len`: every branch has between 256 and 1024 live slots; some branch has exactly 1024 and some exactly 256. `segment_ids`: never falling along a device's tokens; each segment has 1 to 128 tokens, one exactly 128. `segment_branch`: a segment on row r extends branch r * 2 + value.
All inputs are finite; a program needn't handle non-finite values.
Results may differ from a plain program's by a relative error of at most 0.0041.
Values may be sent and summed in bfloat16 or wider, within the bound.
No kernel may reach another device: no remote copies, remote signals or barrier semaphores. Data moves between devices by JAX's collectives and lax.ppermute only.
A program may use at most 64 MiB of HBM per device.

v0:
```python
from functools import partial

import jax
import jax.numpy as jnp
from jax import lax
from jax.sharding import PartitionSpec as P

HEADS = 8
HD = 128
BR_DEV = 2
SEGS = 8


def block_grads(query_heads, grad_heads, log_norm, row_delta, key_rows, allowed):
    scale = HD ** (-0.5)
    keys_part = key_rows[:, :HD]
    values_part = key_rows[:, HD:]
    scores = (
        jnp.einsum("thd,kd->thk", query_heads, keys_part, preferred_element_type=jnp.float32)
        * scale
    )
    weights = jnp.where(allowed[:, None, :], jnp.exp(scores - log_norm[:, :, None]), 0.0)
    dweight = jnp.einsum("thd,kd->thk", grad_heads, values_part, preferred_element_type=jnp.float32)
    dscore = weights * (dweight - row_delta[:, :, None])
    weight_b = weights.astype(jnp.bfloat16)
    dscore_b = dscore.astype(jnp.bfloat16)
    query_part = (
        jnp.einsum("thk,kd->thd", dscore_b, keys_part, preferred_element_type=jnp.float32) * scale
    )
    key_grad = (
        jnp.einsum("thk,thd->kd", dscore_b, query_heads, preferred_element_type=jnp.float32) * scale
    )
    value_grad = jnp.einsum("thk,thd->kd", weight_b, grad_heads, preferred_element_type=jnp.float32)
    return (query_part, jnp.concatenate([key_grad, value_grad], axis=1))


def sweep_keys(query_heads, grad_heads, log_norm, row_delta, key_rows, allowed_of):
    count_rows = key_rows.shape[0]
    block_rows = 512 if count_rows % 512 == 0 else count_rows

    def visit_block(query_sum, block_index):
        offset = block_index * block_rows
        key_block = lax.dynamic_slice_in_dim(key_rows, offset, block_rows, 0)
        query_part, key_grads = block_grads(
            query_heads, grad_heads, log_norm, row_delta, key_block, allowed_of(offset, block_rows)
        )
        return (query_sum + query_part, key_grads)

    start_sum = jnp.zeros(query_heads.shape, jnp.float32)
    query_sum, key_grads = lax.scan(
        visit_block, start_sum, jnp.arange(count_rows // block_rows, dtype=jnp.int32)
    )
    return (query_sum, key_grads.reshape(count_rows, key_rows.shape[1]))


def shards(
    queries,
    attn_out,
    out_grad,
    log_norm,
    leaf_kv,
    root_kv,
    branch_kv,
    branch_len,
    segment_ids,
    segment_branch,
):
    tokens = queries.shape[0]
    query_heads = queries.reshape(tokens, HEADS, HD)
    grad_heads = out_grad.reshape(tokens, HEADS, HD)
    out_heads = attn_out.reshape(tokens, HEADS, HD)
    row_delta = jnp.sum(grad_heads.astype(jnp.float32) * out_heads.astype(jnp.float32), axis=2)
    segment = segment_ids[0]
    seg_branch = segment_branch[0]
    token_branch = jnp.sum(
        jnp.where(
            segment[:, None] == jnp.arange(SEGS, dtype=jnp.int32)[None, :], seg_branch[None, :], 0
        ),
        axis=1,
    )
    row_index = lax.axis_index("rows")
    lengths = lax.dynamic_slice_in_dim(branch_len, row_index * BR_DEV, BR_DEV, 0)
    run_keys = partial(sweep_keys, query_heads, grad_heads, log_norm, row_delta)

    def every_key(offset, count_rows):
        return jnp.ones((tokens, count_rows), dtype=bool)

    query_part, piece_grads = run_keys(
        lax.all_gather(root_kv, "cols", axis=0, tiled=True), every_key
    )
    root_grads = piece_grads
    query_grad = query_part
    piece = lax.all_gather(branch_kv, "cols", axis=1, tiled=True)
    branch_query_grad = query_grad
    updates = []
    for slot in range(BR_DEV):

        def slot_allowed(offset, count_rows, slot=slot):
            slot_pos = offset + jnp.arange(count_rows, dtype=jnp.int32)
            return (token_branch == slot)[:, None] & (slot_pos < lengths[slot])[None, :]

        query_part, piece_grads = run_keys(piece[slot], slot_allowed)
        branch_query_grad = branch_query_grad + query_part
        updates.append(piece_grads)
    branch_grads = jnp.stack(updates)
    query_grad = branch_query_grad
    positions = jnp.arange(tokens, dtype=jnp.int32)

    def leaf_allowed(offset, count_rows):
        key_pos = offset + jnp.arange(count_rows, dtype=jnp.int32)
        return (segment[:, None] == segment[None, :]) & (key_pos[None, :] <= positions[:, None])

    leaf_part, leaf_grads = run_keys(leaf_kv, leaf_allowed)
    query_grad = query_grad + leaf_part
    branch_grad = lax.psum_scatter(branch_grads, "cols", scatter_dimension=1, tiled=True)
    row_whole = lax.psum(root_grads, "rows")
    root_grad = lax.psum_scatter(row_whole, "cols", scatter_dimension=0, tiled=True)
    return (
        query_grad.reshape(tokens, HEADS * HD).astype(jnp.bfloat16),
        leaf_grads,
        root_grad,
        branch_grad,
    )


def solution(mesh):
    in_specs = (
        P(("rows", "cols"), None),
        P(("rows", "cols"), None),
        P(("rows", "cols"), None),
        P(("rows", "cols"), None),
        P(("rows", "cols"), None),
        P("cols", None),
        P("rows", "cols", None),
        P(),
        P(("rows", "cols"), None),
        P(("rows", "cols"), None),
    )
    out_specs = (
        P(("rows", "cols"), None),
        P(("rows", "cols"), None),
        P("cols", None),
        P("rows", "cols", None),
    )
    return jax.shard_map(shards, mesh=mesh, in_specs=in_specs, out_specs=out_specs, check_vma=False)
```

profile of v0, /device:TPU:2, one launch (start us, length us, event | category | flops | bytes accessed | tf_op | source)
XLA Modules:
  0.0 426.6 jit_solution(11022365119326840742)
XLA Ops:
  8.8 1.2 copy.59
  10.0 1.2 copy.58
  11.3 1.2 copy.60
  14.1 51.6 %all-gather.5.cloned.1.call-done = bf16[2,1024,256]{2,1,0:T(8,128)(2,1)} async-done(((bf16[2,32,256]{2,1,0:T(8,128)(2,1)}), bf16[2,1024,256]{2,1,0:T(8,128)(2,1)}) %all-gather.5.cloned.1.call-update) | async-done | bytes 1048592 | tf_op jit(solution)/shard_map/all_gather | solution.py:93
  65.8 2.2 slice_bitcast_fusion.1
  68.0 1.1 broadcast.152.clone2
  69.1 24.8 %while.46 = (s32[]{:T(128)}, f32[256,8,128]{2,0,1:T(8,128)}, f32[2,512,256]{2,1,0:T(8,128)}, s32[256]{0:T(256)S(1)}, s32[2]{0:T(128)S(1)}, /*index=5*/s32[2]{0:T...) while((s32[]{:T(128)}, f32[256,8,128]{2,0,1:T(8,128)}, ...), condition=%wide.region_7.8_spmd.clone, body=%wide.region_6.7_spmd.clone.sunk | while | flops 1353778432 | bytes 27552528 | solution.py:50
  71.7 1.6 fusion.157
  73.3 1.0 fusion.160
  74.4 2.3 fusion.158
  77.5 2.7 fusion.159
  80.4 0.8 constant_dynamic-update-slice_fusion.8
  83.9 1.6 fusion.157
  85.5 1.0 fusion.160
  86.6 2.3 fusion.158
  89.7 3.1 fusion.159
  93.0 0.8 constant_dynamic-update-slice_fusion.8
  93.9 23.9 %all-gather.3.cloned.1.call-done = bf16[2048,256]{1,0:T(8,128)(2,1)} async-done(((bf16[64,256]{1,0:T(8,128)(2,1)}), bf16[2048,256]{1,0:T(8,128)(2,1)}) %all-gather.3.cloned.1.call-update) | async-done | bytes 1048592 | tf_op jit(solution)/shard_map/all_gather | solution.py:89
  117.8 42.4 %while.44 = (s32[]{:T(128)}, f32[256,8,128]{2,0,1:T(8,128)}, f32[4,512,256]{2,1,0:T(8,128)}, s32[4]{0:T(128)S(1)}, bf16[2048,256]{1,0:T(8,128)(2,1)}, /*index=5*...) while((s32[]{:T(128)}, f32[256,8,128]{2,0,1:T(8,128)}, ...), condition=%wide.region_2.3_spmd.clone, body=%wide.region_1.2_spmd.clone.sunk | while | flops 1351548928 | bytes 27156720 | solution.py:50
  119.1 1.6 fusion.134
  120.7 0.9 fusion.136
  121.6 2.0 multiply_convert_fusion.3
  124.4 2.6 fusion.135
  127.3 0.8 constant_dynamic-update-slice_fusion.6
  129.3 1.6 fusion.134
  130.9 0.9 fusion.136
  131.9 2.0 multiply_convert_fusion.3
  133.9 0.8 fusion.137
  134.7 3.0 fusion.135
  138.0 0.8 constant_dynamic-update-slice_fusion.6
  140.0 1.6 fusion.134
  141.6 0.9 fusion.136
  142.6 2.0 multiply_convert_fusion.3
  144.6 0.8 fusion.137
  145.4 3.0 fusion.135
  148.7 0.8 constant_dynamic-update-slice_fusion.6
  150.7 1.6 fusion.134
  152.3 0.9 fusion.136
  153.3 2.0 multiply_convert_fusion.3
  156.1 3.0 fusion.135
  159.4 0.8 constant_dynamic-update-slice_fusion.6
  160.5 1.1 broadcast.152.clone2.1
  161.5 17.1 %while.45 = (s32[]{:T(128)}, f32[256,8,128]{2,0,1:T(8,128)S(1)}, f32[2,512,256]{2,1,0:T(8,128)}, s32[256]{0:T(256)S(1)}, s32[2]{0:T(128)S(1)}, /*index=5*/s32[2]...) while((s32[]{:T(128)}, f32[256,8,128]{2,0,1:T(8,128)S(1)}, ...), condition=%wide.region_5.6_spmd.clone, body=%wide.region_4.5_spmd.clone.sunk | while | flops 1353778432 | bytes 29649700 | solution.py:50
  163.0 1.6 fusion.145
  164.6 1.0 fusion.148
  165.6 1.4 fusion.146
  167.8 1.1 fusion.147
  169.2 0.8 constant_dynamic-update-slice_fusion.7
  171.5 1.6 fusion.145
  173.1 1.0 fusion.148
  174.2 1.4 fusion.146
  176.4 1.1 fusion.147
  177.7 0.9 constant_dynamic-update-slice_fusion.7
  178.6 3.1 pad_maximum_fusion
  183.8 0.8 copy.71
  184.7 1.6 copy.63
  186.3 1.3 copy.62
  187.6 1.6 copy.61
  189.2 60.1 %reduce-scatter.5.cloned.1.call-done = f32[64,256]{1,0:T(8,128)} async-done(((f32[2048,256]{1,0:T(8,128)}), f32[64,256]{1,0:T(8,128)}) %reduce-scatter.5.cloned.1.call-update) | async-done | bytes 65552 | tf_op jit(solution)/shard_map/reduce_scatter | solution.py:117
  249.3 2.5 fusion.60
  251.8 2.0 copy.70
  253.9 88.7 %reduce-scatter.3.cloned.1.call-done = f32[2,32,256]{2,1,0:T(8,128)} async-done(((f32[2,1024,256]{2,1,0:T(8,128)}), f32[2,32,256]{2,1,0:T(8,128)}) %reduce-scatter.3.cloned.1.call-update) | async-done | bytes 65552 | tf_op jit(solution)/shard_map/reduce_scatter | solution.py:115
  342.6 76.0 %all-reduce.2.cloned.1.call-done = f32[64,256]{1,0:T(8,128)} async-done(((f32[64,256]{1,0:T(8,128)}), f32[64,256]{1,0:T(8,128)}) %all-reduce.2.cloned.1.call-update) | async-done | bytes 65552 | tf_op jit(solution)/shard_map/psum | solution.py:116
  418.6 1.5 copy.135
  (80 shorter events, 20.1 us)
Async XLA Ops:
  7.2 58.6 %all-gather.5.cloned.1.call-start = ((), (), s32[]{:S(2)}) async-start(), calls=%async_computation.3 | async-start | bytes 1081344 | tf_op jit(solution)/shard_map/all_gather | solution.py:93
  7.9 109.9 %all-gather.3.cloned.1.call-start = ((), (), s32[]{:S(2)}) async-start(), calls=%async_computation.2 | async-start | bytes 1081344 | tf_op jit(solution)/shard_map/all_gather | solution.py:89
  8.6 240.6 %reduce-scatter.5.cloned.1.call-start = ((), (), s32[]{:S(2)}) async-start(), calls=%async_computation.5 | async-start | bytes 2162688 | tf_op jit(solution)/shard_map/reduce_scatter | solution.py:117
  8.7 60.3 %copy-start.1 = (f32[256,8]{0,1:T(8,128)S(1)}, f32[256,8]{0,1:T(8,128)}, u32[]{:S(2)}) copy-start(f32[256,8]{0,1:T(8,128)} %param.19) | copy-start | bytes 24580
  160.2 182.4 %reduce-scatter.3.cloned.1.call-start = ((), (), s32[]{:S(2)}) async-start(), calls=%async_computation.4 | async-start | bytes 2162688 | tf_op jit(solution)/shard_map/reduce_scatter | solution.py:115
  164.6 1.1 copy-start
  173.1 1.1 copy-start
  178.6 3.1 copy-start.3
  178.6 3.2 copy-start.2
  181.7 236.8 %all-reduce.2.cloned.1.call-start = ((), (), s32[]{:S(2)}) async-start(), calls=%async_computation.6 | async-start | bytes 131072 | tf_op jit(solution)/shard_map/psum | solution.py:116
Sparse Core Ops, SparseCore 0:
  10.7 55.0 all-gather.4
  68.3 49.4 all-gather.2
  160.3 88.8 reduce-scatter.4
  253.5 89.0 reduce-scatter.2
  345.0 73.4 all-reduce.1
where the time goes:
time: 430 us; the launch traced here: 427 us
  waiting for transfers between devices  302 us (70%)
  matrix products  66.5 us (15%)
  local copies, waits for them, and re-layouts  32 us (7%)
  between operations  13.9 us (3%)
  other arithmetic  6.29 us (1%)
  loops' own time  5.65 us (1%)
    reduce_scatter x1, waiting for transfers between devices, shards(): lax.psum_scatter(branch_grads, 'cols', scatter_dimension=1, tiled=True)  88.7 us
    psum x1, waiting for transfers between devices, shards(): row_whole = lax.psum(root_grads, 'rows')  76 us
    reduce_scatter x1, waiting for transfers between devices, shards(): lax.psum_scatter(row_whole, 'cols', scatter_dimension=0, tiled=True)  60.1 us
    all_gather x1, waiting for transfers between devices, shards(): piece = lax.all_gather(branch_kv, 'cols', axis=1, tiled=True)  51.6 us
    all_gather x1, waiting for transfers between devices, shards(): lax.all_gather(root_kv, 'cols', axis=0, tiled=True)  23.9 us
    dot_general x9, matrix products, block_grads(): jnp.einsum('thk,kd->thd', dscore_b, keys_part, preferred_element_type=jnp...  22.3 us
    dot_general x9, matrix products, block_grads(): jnp.einsum('thd,kd->thk', grad_heads, values_part, preferred_element_type...  15.8 us
    dot_general x9, matrix products, block_grads(): jnp.einsum('thd,kd->thk', query_heads, keys_part, preferred_element_type=...  13.5 us
  transfers between devices with their start and end apart: 5, of which 5 were waited for; matrix products, arithmetic and copies ran while one was open for 15% of the time, Pallas kernels for 0%

commit v1 on v0

v1 whole, which is shorter than its diff:
```python
import math

import jax
import jax.numpy as jnp
from jax import lax
from jax.experimental import pallas as pl
from jax.experimental.pallas import tpu as pltpu
from jax.sharding import Mesh
from jax.sharding import PartitionSpec as P

HEADS = 8
HD = 128
TOK = 256
SEGS = 8
TILE = 128
TILES = TOK // TILE
TROWS = TILE * HEADS
ROWS = TOK * HEADS
ROOT_SH = 64
BR_SH = 32
NY = 4
NZ = 4
KEYS = NY * NZ * ROOT_SH
BKEYS = NY * NZ * BR_SH
KB = 512
SCALE = HD ** (-0.5)
LOG2E = math.log2(math.e)
BIG = 1e30
BF = jnp.bfloat16
F32 = jnp.float32
VMEM = pl.BlockSpec(memory_space=pltpu.VMEM)
SMEM = pl.BlockSpec(memory_space=pltpu.SMEM)
PARAMS = pltpu.CompilerParams(vmem_limit_bytes=48 << 20)


def dot(a, b, ca, cb):
    return lax.dot_general(a, b, (((ca,), (cb,)), ((), ())), preferred_element_type=F32)


def move(rows, onehot):
    total = None
    for _ in range(3):
        part = rows.astype(BF)
        rows = rows - part.astype(F32)
        term = dot(part, onehot, 1, 1)
        total = term if total is None else total + term
    return total


def pair_terms(keys, values, q, g, norm, delta, mask=None):
    weight = jnp.exp2(dot(keys, q, 1, 1) * (SCALE * LOG2E) - norm)
    if mask is not None:
        weight = jnp.where(mask, weight, 0.0)
    dscore = weight * (dot(values, g, 1, 1) - delta)
    return weight.astype(BF), dscore.astype(BF)


def prepare_kernel(
    seg_branch, q_ref, o_ref, g_ref, norm_ref, leaf_ref, seg_ref, qs_ref, gs_ref, stat_ref, onehot_ref, grad_ref, dq_ref
):
    segment = seg_ref[...]
    lane = lax.broadcasted_iota(jnp.int32, (1, TOK), 1)
    branch = jnp.zeros((1, TOK), jnp.int32)
    first = jnp.zeros((1, TOK), jnp.int32)
    for s in range(SEGS):
        here = segment == s
        branch = jnp.where(here, seg_branch[0, s], branch)
        ahead = jnp.sum((segment < s).astype(F32), axis=1, keepdims=True).astype(jnp.int32)
        first = jnp.where(here, ahead, first)
    zero_branch = (branch == 0).astype(F32)
    row = lax.broadcasted_iota(jnp.int32, (TOK, TOK), 0)
    col = lax.broadcasted_iota(jnp.int32, (TOK, TOK), 1)
    before = (row < col).astype(F32).astype(BF)
    count = dot(jnp.broadcast_to(zero_branch, (8, TOK)).astype(BF), before, 1, 0)[:1].astype(jnp.int32)
    zeros = jnp.sum(zero_branch, axis=1, keepdims=True).astype(jnp.int32)
    rank = jnp.where(branch == 0, count, zeros + lane - count)
    onehot = (row == rank).astype(F32).astype(BF)
    onehot_ref[...] = onehot

    for source, target in ((q_ref, qs_ref), (g_ref, gs_ref)):
        for h in range(HEADS):
            moved = dot(onehot, source[:, h * HD : (h + 1) * HD], 1, 0).astype(BF)
            for t in range(TILES):
                target[pl.ds((t * HEADS + h) * TILE, TILE), :] = moved[t * TILE : (t + 1) * TILE]

    columns = []
    for h in range(HEADS):
        at = slice(h * HD, (h + 1) * HD)
        columns.append(
            jnp.sum(g_ref[:, at].astype(F32) * o_ref[:, at].astype(F32), axis=1, keepdims=True)
        )
    delta = move(jnp.concatenate(columns, axis=1).T, onehot)
    norm = move(norm_ref[...].T, onehot) * LOG2E
    place = jnp.concatenate([lane, first, branch, lane, lane, lane, lane, lane], axis=0)
    place = dot(place.astype(F32).astype(BF), onehot, 1, 1).astype(jnp.int32)
    norm0 = jnp.where(place[2:3] == 0, norm, BIG)
    norm1 = jnp.where(place[2:3] == 0, BIG, norm)
    for t in range(TILES):
        for h in range(HEADS):
            at = pl.ds((t * HEADS + h) * TILE, TILE)
            tok = slice(t * TILE, (t + 1) * TILE)
            for r, value in enumerate((norm, norm0, norm1, delta)):
                stat_ref[r : r + 1, at] = value[h : h + 1, tok]

    keys = leaf_ref[:, :HD]
    values = leaf_ref[:, HD:]
    keys_t = keys.T
    slot = lax.broadcasted_iota(jnp.int32, (TOK, TILE), 0)
    dkey = jnp.zeros((TOK, HD), F32)
    dvalue = jnp.zeros((TOK, HD), F32)
    for t in range(TILES):
        tok = slice(t * TILE, (t + 1) * TILE)
        mask = ((slot >= place[1:2, tok]) & (slot <= place[0:1, tok])).astype(F32)
        mask = jnp.concatenate([mask] * HEADS, axis=1) > 0.0
        at = pl.ds(t * TROWS, TROWS)
        q = qs_ref[at, :]
        g = gs_ref[at, :]
        weight, dscore = pair_terms(keys, values, q, g, stat_ref[0:1, at], stat_ref[3:4, at], mask)
        dkey += dot(dscore, q, 1, 0)
        dvalue += dot(weight, g, 1, 0)
        dq_ref[:, at] = dot(keys_t, dscore, 1, 0)
    grad_ref[:, :HD] = dkey * SCALE
    grad_ref[:, HD:] = dvalue


def sweep(kv_ref, sources, norm_row, grads, base, rows_at):
    keys = kv_ref[rows_at, :HD]
    values = kv_ref[rows_at, HD:]
    keys_t = keys.T
    grads[...] = jnp.zeros_like(grads)
    for q_ref, g_ref, stat_ref, dq_ref in sources:

        def visit(t, carry):
            at = pl.ds(pl.multiple_of(t * TROWS, TROWS), TROWS)
            norm = stat_ref[norm_row : norm_row + 1, at]

            def work():
                q = q_ref[at, :]
                g = g_ref[at, :]
                weight, dscore = pair_terms(keys, values, q, g, norm, stat_ref[3:4, at])
                grads[:, :HD] += dot(dscore, q, 1, 0)
                grads[:, HD:] += dot(weight, g, 1, 0)
                dq_ref[:, at] += dot(keys_t, dscore, 1, 0)

            if norm_row == 0:
                work()
            else:
                pl.when(jnp.min(norm) < 0.5 * BIG)(work)
            return carry

        lax.fori_loop(0, TILES, visit, 0)


def root_kernel(
    kv0, kv1, kv2, kv3, q0, g0, s0, q1, g1, s1, dq_in, dq0, dq1, grad_ref, kv_ref, total
):
    dq0[...] = dq_in[...]
    dq1[...] = jnp.zeros_like(dq1)
    part = KEYS // NY
    for i, piece in enumerate((kv0, kv1, kv2, kv3)):
        kv_ref[pl.ds(i * part, part), :] = piece[...]
    sources = ((q0, g0, s0, dq0), (q1, g1, s1, dq1))

    def block(i, carry):
        at = pl.ds(pl.multiple_of(i * KB, KB), KB)
        sweep(kv_ref, sources, 0, total, 0, at)
        grad_ref[at, :HD] = (total[:, :HD] * SCALE).astype(BF)
        grad_ref[at, HD:] = total[:, HD:].astype(BF)
        return carry

    lax.fori_loop(0, KEYS // KB, block, 0)


def branch_kernel(
    place, lengths, kv0, kv1, kv2, kv3, q0, g0, s0, q1, g1, s1, dq0_in, dq1_in, dq0, dq1, grad_ref, kv_ref, total
):
    dq0[...] = dq0_in[...]
    dq1[...] = dq1_in[...]
    sources = ((q0, g0, s0, dq0), (q1, g1, s1, dq1))
    inner = lax.broadcasted_iota(jnp.int32, (BR_SH, 1), 0)

    def live(b, dy, dz):
        y = lax.rem(place[0] + dy, NY)
        z = lax.rem(place[1] + dz, NZ)
        start = ((y * NZ + z) * 2 + place[2]) * BR_SH
        return inner + start < lengths[b]

    for b in range(2):
        for dy, piece in enumerate((kv0, kv1, kv2, kv3)):
            for dz in range(NZ):
                rows = piece[pl.ds((dz * 2 + b) * BR_SH, BR_SH), :]
                rows = jnp.where(live(b, dy, dz), rows.astype(F32), 0.0).astype(BF)
                kv_ref[pl.ds((dy * NZ + dz) * BR_SH, BR_SH), :] = rows
        sweep(kv_ref, sources, 1 + b, total, 0, pl.ds(0, BKEYS))
        for dy in range(NY):
            for dz in range(NZ):
                at = pl.ds((dy * NZ + dz) * BR_SH, BR_SH)
                to = pl.ds(((dy * NZ + dz) * 2 + b) * BR_SH, BR_SH)
                ok = live(b, dy, dz)
                grad_ref[to, :HD] = jnp.where(ok, total[at, :HD] * SCALE, 0.0).astype(BF)
                grad_ref[to, HD:] = jnp.where(ok, total[at, HD:], 0.0).astype(BF)


def finish_kernel(onehot_ref, mine, other, out_ref):
    for h in range(HEADS):
        parts = []
        for t in range(TILES):
            at = pl.ds((t * HEADS + h) * TILE, TILE)
            parts.append((((mine[:, at] + other[:, at]) * SCALE).T).astype(BF))
        column = jnp.concatenate(parts, axis=0)
        out_ref[:, h * HD : (h + 1) * HD] = dot(onehot_ref[...], column, 0, 0).astype(BF)


def shape(dims, dtype):
    return jax.ShapeDtypeStruct(dims, dtype)


def shift(value, axis, size, by):
    return lax.ppermute(value, axis, [(i, (i + by) % size) for i in range(size)])


def gather(value, axis, size):
    return [value] + [shift(value, axis, size, -k) for k in range(1, size)]


def scatter_sum(blocks, axis, size):
    total = blocks[0].astype(F32)
    for k in range(1, size):
        total = total + shift(blocks[k], axis, size, k).astype(F32)
    return total


def shards(
    queries, attn_out, out_grad, log_norm, leaf_kv, root_kv, branch_kv, branch_len, segment_ids, segment_branch
):
    row_index = lax.axis_index("zl") * 4 + lax.axis_index("x")
    lengths = lax.dynamic_slice_in_dim(branch_len, row_index * 2, 2, 0)
    place = jnp.stack([lax.axis_index("y"), lax.axis_index("zh"), lax.axis_index("c")]).astype(jnp.int32)

    root_z = jnp.concatenate(gather(root_kv, "zh", NZ), axis=0)
    branch_z = jnp.concatenate(gather(branch_kv.reshape(2 * BR_SH, 2 * HD), "zh", NZ), axis=0)
    roots = gather(root_z, "y", NY)
    branches = gather(branch_z, "y", NY)

    q0, g0, s0, onehot, leaf_grad, dq_leaf = pl.pallas_call(
        prepare_kernel,
        out_shape=(
            shape((ROWS, HD), BF),
            shape((ROWS, HD), BF),
            shape((4, ROWS), F32),
            shape((TOK, TOK), BF),
            shape((TOK, 2 * HD), F32),
            shape((HD, ROWS), F32),
        ),
        in_specs=[SMEM] + [VMEM] * 6,
        out_specs=(VMEM,) * 6,
        compiler_params=PARAMS,
        cost_estimate=pl.CostEstimate(flops=4_000_000_000, bytes_accessed=5_000_000, transcendentals=0),
        name="prepare",
    )(segment_branch, queries, attn_out, out_grad, log_norm, leaf_kv, segment_ids)
    q1 = shift(q0, "c", 2, 1)
    g1 = shift(g0, "c", 2, 1)
    s1 = shift(s0, "c", 2, 1)

    dq0, dq1, root_terms = pl.pallas_call(
        root_kernel,
        out_shape=(shape((HD, ROWS), F32), shape((HD, ROWS), F32), shape((KEYS, 2 * HD), BF)),
        in_specs=[VMEM] * 11,
        out_specs=(VMEM,) * 3,
        scratch_shapes=[pltpu.VMEM((KEYS, 2 * HD), BF), pltpu.VMEM((KB, 2 * HD), F32)],
        compiler_params=PARAMS,
        cost_estimate=pl.CostEstimate(flops=10_000_000_000, bytes_accessed=8_000_000, transcendentals=0),
        name="root",
    )(*roots, q0, g0, s0, q1, g1, s1, dq_leaf)

    dq0, dq1, branch_terms = pl.pallas_call(
        branch_kernel,
        out_shape=(shape((HD, ROWS), F32), shape((HD, ROWS), F32), shape((2 * BKEYS, 2 * HD), BF)),
        in_specs=[SMEM] * 2 + [VMEM] * 12,
        out_specs=(VMEM,) * 3,
        scratch_shapes=[pltpu.VMEM((BKEYS, 2 * HD), BF), pltpu.VMEM((BKEYS, 2 * HD), F32)],
        compiler_params=PARAMS,
        cost_estimate=pl.CostEstimate(flops=8_000_000_000, bytes_accessed=8_000_000, transcendentals=0),
        name="branch",
    )(place, lengths, *branches, q0, g0, s0, q1, g1, s1, dq0, dq1)

    root_y = scatter_sum(root_terms.reshape(NY, NZ * ROOT_SH, 2 * HD), "y", NY).astype(BF)
    root_one = scatter_sum(root_y.reshape(NZ, ROOT_SH, 2 * HD), "zh", NZ)
    for axis, size in (("x", 4), ("zl", 2)):
        root_one = root_one + sum(shift(root_one, axis, size, k) for k in range(1, size))

    branch_y = scatter_sum(branch_terms.reshape(NY, NZ * 2 * BR_SH, 2 * HD), "y", NY).astype(BF)
    branch_one = scatter_sum(branch_y.reshape(NZ, 2 * BR_SH, 2 * HD), "zh", NZ)

    query_grad = pl.pallas_call(
        finish_kernel,
        out_shape=shape((TOK, HEADS * HD), BF),
        in_specs=[VMEM] * 3,
        out_specs=VMEM,
        compiler_params=PARAMS,
        cost_estimate=pl.CostEstimate(flops=200_000_000, bytes_accessed=3_000_000, transcendentals=0),
        name="finish",
    )(onehot, dq0, shift(dq1, "c", 2, 1))
    return query_grad, leaf_grad, root_one, branch_one.reshape(2, BR_SH, 2 * HD)


def solution(mesh):
    fine = Mesh(mesh.devices.reshape(2, 4, NY, NZ, 2), ("zl", "x", "y", "zh", "c"))
    rows, cols = ("zl", "x"), ("y", "zh", "c")
    both = rows + cols
    in_specs = (
        P(both, None),
        P(both, None),
        P(both, None),
        P(both, None),
        P(both, None),
        P(cols, None),
        P(rows, cols, None),
        P(),
        P(both, None),
        P(both, None),
    )
    out_specs = (P(both, None), P(both, None), P(cols, None), P(rows, cols, None))
    return jax.shard_map(shards, mesh=fine, in_specs=in_specs, out_specs=out_specs, check_vma=False)
```

time: 430 us -> 112 us (0.26)
  waiting for transfers between devices: 302 us -> 12.3 us
  matrix products: 66.5 us -> 0 us
  starting transfers between devices: 0.38 us -> 58.8 us
  Pallas kernels: 0 us -> 30.2 us
  local copies, waits for them, and re-layouts: 32 us -> 7.74 us
  between operations: 13.9 us -> 0.86 us
  loops' own time: 5.65 us -> 0 us
  other arithmetic: 6.29 us -> 1.56 us
    reduce_scatter x2 -> x0, waiting for transfers between devices: 149 us -> none  [the longest x1 88.7 us: shards(): lax.psum_scatter(branch_grads, 'cols', scatter_dimension=1, tiled=True)]
    psum x1 -> x0, waiting for transfers between devices: 76 us -> none  [shards(): row_whole = lax.psum(root_grads, 'rows')]
    all_gather x2 -> x0, waiting for transfers between devices: 75.6 us -> none  [the longest x1 51.6 us: shards(): piece = lax.all_gather(branch_kv, 'cols', axis=1, tiled=True)]
    dot_general x45 -> x0, matrix products: 66.5 us -> none  [the longest x9 22.3 us: block_grads(): jnp.einsum('thk,kd->thd', dscore_b, keys_part, preferred_element_type=jnp...]
    ppermute x0 -> x32, starting transfers between devices: none -> 58.8 us  [shift(): lax.ppermute(value, axis, [(i, (i + by) % size) for i in range(size)])]
    pallas_call x0 -> x4, Pallas kernels: none -> 30.2 us  [the longest x1 13.2 us: shards(): pl.pallas_call(root_kernel, out_shape=(shape((HD, ROWS), F32), shape((HD,...]
    ppermute x0 -> x32, waiting for transfers between devices: none -> 12.3 us  [shift(): lax.ppermute(value, axis, [(i, (i + by) % size) for i in range(size)])]
    dynamic_update_slice x16 -> x0, local copies, waits for them, and re-layouts: 8.34 us -> none  [sweep_keys(): lax.scan(visit_block, start_sum, jnp.arange(count_rows // block_rows, dty...]
  transfers between devices with their start and end apart: 5 -> 32, of which waited for: 5 -> 6; matrix products, arithmetic and copies ran while one was open for 15% -> 2% of each run, Pallas kernels for 0% -> 26%
where the time goes in v1:
time: 112 us; the launch traced here: 111 us
  starting transfers between devices  58.8 us (52%)
  Pallas kernels  30.2 us (27%)
  waiting for transfers between devices  12.3 us (11%)
  local copies, waits for them, and re-layouts  7.74 us (7%)
  other arithmetic  1.56 us (1%)
    ppermute x32, starting transfers between devices, shift(): lax.ppermute(value, axis, [(i, (i + by) % size) for i in range(size)])  58.8 us
    pallas_call x1, Pallas kernels, shards(): pl.pallas_call(root_kernel, out_shape=(shape((HD, ROWS), F32), shape((HD,...  13.2 us
    ppermute x32, waiting for transfers between devices, shift(): lax.ppermute(value, axis, [(i, (i + by) % size) for i in range(size)])  12.3 us
    pallas_call x1, Pallas kernels, shards(): pl.pallas_call(branch_kernel, out_shape=(shape((HD, ROWS), F32), shape((H...  11.7 us
    unnamed x28, local copies, waits for them, and re-layouts  7.59 us
    pallas_call x1, Pallas kernels, shards(): pl.pallas_call(prepare_kernel, out_shape=(shape((ROWS, HD), BF), shape((R...  3.75 us
  transfers between devices with their start and end apart: 32, of which 6 were waited for; matrix products, arithmetic and copies ran while one was open for 2% of the time, Pallas kernels for 26%

profile of v1, /device:TPU:2, one launch (start us, length us, event | category | flops | bytes accessed | tf_op | source)
XLA Modules:
  0.0 111.5 jit_solution(10035550319094123723)
XLA Ops:
  0.7 3.3 %collective-permute-start.2 = (bf16[64,256]{1,0:T(8,128)(2,1)}, bf16[64,256]{1,0:T(8,128)(2,1)S(1)}, u32[]{:S(2)}, u32[]{:S(2)}) collective-permute-start(bf16[64,256]{1,0:T(8,128)(2,1)} %bitcast.6), channel_id=1, source_target_pairs={{0,2},{2,4},{4,6},{6,0},{1,3},{3,5},{5,7},{7,1},{8,10},{10,12},{12... | collective-permute-start | bytes 98312 | tf_op jit(solution)/shard_map/ppermute | solution.py:219
  4.0 5.4 %collective-permute-start.1 = (bf16[64,256]{1,0:T(8,128)(2,1)}, bf16[64,256]{1,0:T(8,128)(2,1)S(1)}, u32[]{:S(2)}, u32[]{:S(2)}) collective-permute-start(bf16[64,256]{1,0:T(8,128)(2,1)} %bitcast.7), channel_id=1, source_target_pairs={{0,4},{2,6},{4,0},{6,2},{1,5},{3,7},{5,1},{7,3},{8,12},{10,14},{12... | collective-permute-start | bytes 98312 | tf_op jit(solution)/shard_map/ppermute | solution.py:219
  9.4 0.5 collective-permute-start.10
  9.9 3.1 %collective-permute-start.9 = (bf16[64,256]{1,0:T(8,128)(2,1)}, bf16[64,256]{1,0:T(8,128)(2,1)S(1)}, u32[]{:S(2)}, u32[]{:S(2)}) collective-permute-start(bf16[64,256]{1,0:T(8,128)(2,1)} %param.15), channel_id=1, source_target_pairs={{0,6},{2,0},{4,2},{6,4},{1,7},{3,1},{5,3},{7,5},{8,14},{10,8},{12,... | collective-permute-start | bytes 98312 | tf_op jit(solution)/shard_map/ppermute | solution.py:219
  13.1 0.8 copy.14.norm_ref
  13.9 0.0 copy-start
  13.9 1.0 copy-done
  15.0 1.0 copy-done.1
  16.0 1.0 copy-done.2
  17.1 3.7 %prepare.1 = (bf16[2048,128]{1,0:T(8,128)(2,1)S(1)}, bf16[2048,128]{1,0:T(8,128)(2,1)S(1)}, f32[4,2048]{1,0:T(4,128)S(1)}, bf16[256,256]{1,0:T(8,128)(2,1)S(1)},...) custom-call(s32[1,8]{1,0:T(1,128)S(1)} %copy-done.5, bf16[256,1024]{1,0:T(8,128)(2,1)S(1)} %copy-done, ...), custom_call_target="tpu_custom_call" | custom-call | flops 4000000000 | bytes 5000000 | tf_op jit(solution)/shard_map/prepare/pallas_call | solution.py:245
  20.8 1.0 copy-done.6
  21.8 0.0 collective-permute-start.6
  21.8 0.0 collective-permute-done.9
  21.8 0.6 collective-permute-start.7
  22.4 0.0 collective-permute-done.10
  22.4 1.4 %collective-permute-start.11 = (bf16[64,256]{1,0:T(8,128)(2,1)S(1)}, bf16[64,256]{1,0:T(8,128)(2,1)S(1)}, u32[]{:S(2)}, u32[]{:S(2)}) collective-permute-start(bf16[64,256]{1,0:T(8,128)(2,1)S(1)} %copy-done.9), channel_id=1, source_target_pairs={{0,2},{2,4},{4,6},{6,0},{1,3},{3,5},{5,7},{7,1},{8,10},{10,12},{12... | collective-permute-start | bytes 98312 | tf_op jit(solution)/shard_map/ppermute | solution.py:219
  23.9 0.0 collective-permute-done.2
  23.9 2.9 %collective-permute-start = (bf16[64,256]{1,0:T(8,128)(2,1)S(1)}, bf16[64,256]{1,0:T(8,128)(2,1)S(1)}, u32[]{:S(2)}, u32[]{:S(2)}) collective-permute-start(bf16[64,256]{1,0:T(8,128)(2,1)S(1)} %bitcast.8), channel_id=1, source_target_pairs={{0,6},{2,0},{4,2},{6,4},{1,7},{3,1},{5,3},{7,5},{8,14},{10,8},{12,... | collective-permute-start | bytes 98312 | tf_op jit(solution)/shard_map/ppermute | solution.py:219
  26.7 1.8 %collective-permute-done.11 = bf16[64,256]{1,0:T(8,128)(2,1)S(1)} collective-permute-done((bf16[64,256]{1,0:T(8,128)(2,1)S(1)}, bf16[64,256]{1,0:T(8,128)(2,1)S(1)}, u32[]{:S(2)}, u32[]{:S(2)}) %collective-permute-start.11) | collective-permute-done | bytes 32800 | tf_op jit(solution)/shard_map/ppermute | solution.py:219
  28.6 1.7 %collective-permute-start.14 = (bf16[256,256]{1,0:T(8,128)(2,1)S(1)}, bf16[256,256]{1,0:T(8,128)(2,1)S(1)}, u32[]{:S(2)}, u32[]{:S(2)}) collective-permute-start(bf16[256,256]{1,0:T(8,128)(2,1)S(1)} %constant_dynamic-update-slice_fusion.kv0), channel_id=1, source_target_pairs={{0,8},{8,16},{16,24},{24,0},{1,9},{9,17},{17,25},{25,1},{2,10},{10... | collective-permute-start | bytes 393224 | tf_op jit(solution)/shard_map/ppermute | solution.py:219
  30.2 2.9 %collective-permute-start.13 = (bf16[256,256]{1,0:T(8,128)(2,1)S(1)}, bf16[256,256]{1,0:T(8,128)(2,1)S(1)}, u32[]{:S(2)}, u32[]{:S(2)}) collective-permute-start(bf16[256,256]{1,0:T(8,128)(2,1)S(1)} %constant_dynamic-update-slice_fusion.kv0), channel_id=1, source_target_pairs={{0,16},{8,24},{16,0},{24,8},{1,17},{9,25},{17,1},{25,9},{2,18},{10... | collective-permute-start | bytes 393224 | tf_op jit(solution)/shard_map/ppermute | solution.py:219
  33.2 1.3 %collective-permute-start.12 = (bf16[256,256]{1,0:T(8,128)(2,1)S(1)}, bf16[256,256]{1,0:T(8,128)(2,1)S(1)}, u32[]{:S(2)}, u32[]{:S(2)}) collective-permute-start(bf16[256,256]{1,0:T(8,128)(2,1)S(1)} %constant_dynamic-update-slice_fusion.kv0), channel_id=1, source_target_pairs={{0,24},{8,0},{16,8},{24,16},{1,25},{9,1},{17,9},{25,17},{2,26},{10... | collective-permute-start | bytes 393224 | tf_op jit(solution)/shard_map/ppermute | solution.py:219
  34.5 0.1 pad_add_fusion.place
  34.6 0.7 copy-done.11
  35.2 0.1 dynamic_slice.3.lengths
  35.3 0.4 collective-permute-done.14.kv3
  35.8 0.4 collective-permute-start.5
  36.2 4.0 %collective-permute-done.13.kv2 = bf16[256,256]{1,0:T(8,128)(2,1)S(1)} collective-permute-done((bf16[256,256]{1,0:T(8,128)(2,1)S(1)}, bf16[256,256]{1,0:T(8,128)(2,1)S(1)}, u32[]{:S(2)}, u32[]{:S(2)}) %collective-permute-start.13) | collective-permute-done | bytes 131104 | tf_op jit(solution)/shard_map/ppermute | solution.py:219
  40.2 0.7 collective-permute-start.4
  41.0 0.0 collective-permute-done.12.kv1
  41.0 1.7 %collective-permute-start.3 = (bf16[256,256]{1,0:T(8,128)(2,1)S(1)}, bf16[256,256]{1,0:T(8,128)(2,1)S(1)}, u32[]{:S(2)}, u32[]{:S(2)}) collective-permute-start(bf16[256,256]{1,0:T(8,128)(2,1)S(1)} %pad_maximum_fusion.kv0), channel_id=1, source_target_pairs={{0,24},{8,0},{16,8},{24,16},{1,25},{9,1},{17,9},{25,17},{2,26},{10... | collective-permute-start | bytes 393224 | tf_op jit(solution)/shard_map/ppermute | solution.py:219
  42.7 0.0 collective-permute-done.6.q1
  42.7 0.0 collective-permute-done.7.g1
  42.7 13.2 %root.1 = (f32[128,2048]{1,0:T(8,128)S(1)}, f32[128,2048]{1,0:T(8,128)S(1)}, bf16[1024,256]{1,0:T(8,128)(2,1)S(1)}) custom-call(bf16[256,256]{1,0:T(8,128)(2,1)S(1)} %constant_dynamic-update-slice_fusion.kv0, bf16[256,256]{1,0:T(8,128)(2,1)S(1)} %collective-permute-done.12.kv1, bf16[256,256]{1,0:T(8,128)(2,1)S(1)} %collective-permute-done.13.kv2, ...), custom_call_target="tpu_custom_call" | custom-call | flops 10000000000 | bytes 8000000 | tf_op jit(solution)/shard_map/root/pallas_call | solution.py:265
  55.9 1.0 copy-done.7
  56.9 1.0 copy-done.8
  57.9 0.4 collective-permute-start.16
  58.3 2.9 %collective-permute-start.18 = (bf16[256,256]{1,0:T(8,128)(2,1)S(1)}, bf16[256,256]{1,0:T(8,128)(2,1)S(1)}, u32[]{:S(2)}, u32[]{:S(2)}) collective-permute-start(bf16[256,256]{1,0:T(8,128)(2,1)S(1)} %get-tuple-element.32), channel_id=1, source_target_pairs={{0,24},{8,0},{16,8},{24,16},{1,25},{9,1},{17,9},{25,17},{2,26},{10... | collective-permute-start | bytes 393224 | tf_op jit(solution)/shard_map/ppermute | solution.py:219
  61.2 0.0 collective-permute-done.5.kv3
  61.2 0.0 collective-permute-done.3.kv1
  61.2 11.7 %branch.1 = (f32[128,2048]{1,0:T(8,128)S(1)}, f32[128,2048]{1,0:T(8,128)S(1)}, bf16[1024,256]{1,0:T(8,128)(2,1)S(1)}) custom-call(s32[3]{0:T(128)S(1)} %pad_add_fusion.place, s32[2]{0:T(128)S(1)} %dynamic_slice.3.lengths, bf16[256,256]{1,0:T(8,128)(2,1)S(1)} %pad_maximum_fusion.kv0, bf16[256,256]{1,0:T(8,128)(2,1)S(1)} %collective-permute-done.3.kv1, ...), custom_call_target="tpu_custom_call" | custom-call | flops 8000000000 | bytes 8000000 | tf_op jit(solution)/shard_map/branch/pallas_call | solution.py:276
  73.0 1.4 %collective-permute-start.26 = (bf16[256,256]{1,0:T(8,128)(2,1)S(1)}, bf16[256,256]{1,0:T(8,128)(2,1)S(1)}, u32[]{:S(2)}, u32[]{:S(2)}) collective-permute-start(bf16[256,256]{1,0:T(8,128)(2,1)S(1)} %get-tuple-element.28), channel_id=1, source_target_pairs={{0,8},{8,16},{16,24},{24,0},{1,9},{9,17},{17,25},{25,1},{2,10},{10... | collective-permute-start | bytes 393224 | tf_op jit(solution)/shard_map/ppermute | solution.py:219
  74.4 2.0 %collective-permute-start.28 = (bf16[256,256]{1,0:T(8,128)(2,1)S(1)}, bf16[256,256]{1,0:T(8,128)(2,1)S(1)}, u32[]{:S(2)}, u32[]{:S(2)}) collective-permute-start(bf16[256,256]{1,0:T(8,128)(2,1)S(1)} %get-tuple-element.29), channel_id=1, source_target_pairs={{0,24},{8,0},{16,8},{24,16},{1,25},{9,1},{17,9},{25,17},{2,26},{10... | collective-permute-start | bytes 393224 | tf_op jit(solution)/shard_map/ppermute | solution.py:219
  76.3 2.3 %collective-permute-start.27 = (bf16[256,256]{1,0:T(8,128)(2,1)S(1)}, bf16[256,256]{1,0:T(8,128)(2,1)S(1)}, u32[]{:S(2)}, u32[]{:S(2)}) collective-permute-start(bf16[256,256]{1,0:T(8,128)(2,1)S(1)} %get-tuple-element.30), channel_id=1, source_target_pairs={{0,16},{8,24},{16,0},{24,8},{1,17},{9,25},{17,1},{25,9},{2,18},{10... | collective-permute-start | bytes 393224 | tf_op jit(solution)/shard_map/ppermute | solution.py:219
  78.6 0.0 collective-permute-done.18
  78.7 0.1 add_convert_fusion.1
  78.7 3.0 %collective-permute-start.19 = (bf16[64,256]{1,0:T(8,128)(2,1)S(1)}, bf16[64,256]{1,0:T(8,128)(2,1)S(1)}, u32[]{:S(2)}, u32[]{:S(2)}) collective-permute-start(bf16[64,256]{1,0:T(8,128)(2,1)S(1)} %get-tuple-element.37), channel_id=1, source_target_pairs={{0,2},{2,4},{4,6},{6,0},{1,3},{3,5},{5,7},{7,1},{8,10},{10,12},{12... | collective-permute-start | bytes 98312 | tf_op jit(solution)/shard_map/ppermute | solution.py:219
  81.7 0.0 collective-permute-done.26
  81.7 1.2 %collective-permute-start.21 = (bf16[64,256]{1,0:T(8,128)(2,1)S(1)}, bf16[64,256]{1,0:T(8,128)(2,1)S(1)}, u32[]{:S(2)}, u32[]{:S(2)}) collective-permute-start(bf16[64,256]{1,0:T(8,128)(2,1)S(1)} %get-tuple-element.38), channel_id=1, source_target_pairs={{0,6},{2,0},{4,2},{6,4},{1,7},{3,1},{5,3},{7,5},{8,14},{10,8},{12,... | collective-permute-start | bytes 98312 | tf_op jit(solution)/shard_map/ppermute | solution.py:219
  83.0 4.9 %collective-permute-start.20 = (bf16[64,256]{1,0:T(8,128)(2,1)S(1)}, bf16[64,256]{1,0:T(8,128)(2,1)S(1)}, u32[]{:S(2)}, u32[]{:S(2)}) collective-permute-start(bf16[64,256]{1,0:T(8,128)(2,1)S(1)} %get-tuple-element.39), channel_id=1, source_target_pairs={{0,4},{2,6},{4,0},{6,2},{1,5},{3,7},{5,1},{7,3},{8,12},{10,14},{12... | collective-permute-start | bytes 98312 | tf_op jit(solution)/shard_map/ppermute | solution.py:219
  87.8 0.1 add_convert_fusion
  87.9 3.2 %collective-permute-done.20 = bf16[64,256]{1,0:T(8,128)(2,1)S(1)} collective-permute-done((bf16[64,256]{1,0:T(8,128)(2,1)S(1)}, bf16[64,256]{1,0:T(8,128)(2,1)S(1)}, u32[]{:S(2)}, u32[]{:S(2)}) %collective-permute-start.20) | collective-permute-done | bytes 32800 | tf_op jit(solution)/shard_map/ppermute | solution.py:219
  91.2 0.1 collective-permute-start.24
  91.3 2.9 %collective-permute-start.23 = (f32[64,256]{1,0:T(8,128)S(1)}, f32[64,256]{1,0:T(8,128)S(1)}, u32[]{:S(2)}, u32[]{:S(2)}) collective-permute-start(f32[64,256]{1,0:T(8,128)S(1)} %convert_add_fusion.1), channel_id=1, source_target_pairs={{0,64},{32,96},{64,0},{96,32},{1,65},{33,97},{65,1},{97,33},{2,66}... | collective-permute-start | bytes 196616 | tf_op jit(solution)/shard_map/ppermute | solution.py:219
  94.2 1.2 %collective-permute-start.22 = (f32[64,256]{1,0:T(8,128)S(1)}, f32[64,256]{1,0:T(8,128)S(1)}, u32[]{:S(2)}, u32[]{:S(2)}) collective-permute-start(f32[64,256]{1,0:T(8,128)S(1)} %convert_add_fusion.1), channel_id=1, source_target_pairs={{0,32},{32,64},{64,96},{96,0},{1,33},{33,65},{65,97},{97,1},{2,34}... | collective-permute-start | bytes 196616 | tf_op jit(solution)/shard_map/ppermute | solution.py:219
  95.4 2.1 %collective-permute-start.29 = (bf16[64,256]{1,0:T(8,128)(2,1)S(1)}, bf16[64,256]{1,0:T(8,128)(2,1)S(1)}, u32[]{:S(2)}, u32[]{:S(2)}) collective-permute-start(bf16[64,256]{1,0:T(8,128)(2,1)S(1)} %get-tuple-element.34), channel_id=1, source_target_pairs={{0,2},{2,4},{4,6},{6,0},{1,3},{3,5},{5,7},{7,1},{8,10},{10,12},{12... | collective-permute-start | bytes 98312 | tf_op jit(solution)/shard_map/ppermute | solution.py:219
  97.4 2.1 %collective-permute-start.31 = (bf16[64,256]{1,0:T(8,128)(2,1)S(1)}, bf16[64,256]{1,0:T(8,128)(2,1)S(1)}, u32[]{:S(2)}, u32[]{:S(2)}) collective-permute-start(bf16[64,256]{1,0:T(8,128)(2,1)S(1)} %get-tuple-element.35), channel_id=1, source_target_pairs={{0,6},{2,0},{4,2},{6,4},{1,7},{3,1},{5,3},{7,5},{8,14},{10,8},{12,... | collective-permute-start | bytes 98312 | tf_op jit(solution)/shard_map/ppermute | solution.py:219
  99.6 5.3 %collective-permute-start.30 = (bf16[64,256]{1,0:T(8,128)(2,1)S(1)}, bf16[64,256]{1,0:T(8,128)(2,1)S(1)}, u32[]{:S(2)}, u32[]{:S(2)}) collective-permute-start(bf16[64,256]{1,0:T(8,128)(2,1)S(1)} %get-tuple-element.36), channel_id=1, source_target_pairs={{0,4},{2,6},{4,0},{6,2},{1,5},{3,7},{5,1},{7,3},{8,12},{10,14},{12... | collective-permute-start | bytes 98312 | tf_op jit(solution)/shard_map/ppermute | solution.py:219
  105.0 1.0 collective-permute-start.25
  105.9 1.5 %collective-permute-done.30 = bf16[64,256]{1,0:T(8,128)(2,1)S(1)} collective-permute-done((bf16[64,256]{1,0:T(8,128)(2,1)S(1)}, bf16[64,256]{1,0:T(8,128)(2,1)S(1)}, u32[]{:S(2)}, u32[]{:S(2)}) %collective-permute-start.30) | collective-permute-done | bytes 32800 | tf_op jit(solution)/shard_map/ppermute | solution.py:219
  107.4 0.6 convert_add_fusion
  108.1 1.2 %collective-permute-done.25 = f32[64,256]{1,0:T(8,128)S(1)} collective-permute-done((f32[64,256]{1,0:T(8,128)S(1)}, f32[64,256]{1,0:T(8,128)S(1)}, u32[]{:S(2)}, u32[]{:S(2)}) %collective-permute-start.25) | collective-permute-done | bytes 65568 | tf_op jit(solution)/shard_map/ppermute | solution.py:219
  109.3 0.6 add.65
  109.9 1.5 %finish.1 = bf16[256,1024]{1,0:T(8,128)(2,1)} custom-call(bf16[256,256]{1,0:T(8,128)(2,1)S(1)} %get-tuple-element.16.onehot_ref, f32[128,2048]{1,0:T(8,128)S(1)} %get-tuple-element.23.mine, f32[128,2048]{1,0:T(8,128)S(1)} %collective-permute-done.15.other), custom_call_target="tpu_custom_call" | custom-call | flops 200000000 | bytes 3000000 | tf_op jit(solution)/shard_map/finish/pallas_call | solution.py:295
  (46 shorter events, 0.2 us)
Async XLA Ops:
  0.6 13.3 %copy-start.3 = (bf16[256,256]{1,0:T(8,128)(2,1)S(1)}, bf16[256,256]{1,0:T(8,128)(2,1)}, u32[]{:S(2)}) copy-start(bf16[256,256]{1,0:T(8,128)(2,1)} %leaf_ref.1) | copy-start | bytes 393220
  0.6 13.3 %copy-start.4 = (s32[1,256]{1,0:T(1,128)S(1)}, s32[1,256]{1,0:T(1,128)}, u32[]{:S(2)}) copy-start(s32[1,256]{1,0:T(1,128)} %seg_ref.1) | copy-start | bytes 3076
  0.7 13.3 %copy-start.5 = (s32[1,8]{1,0:T(1,128)S(1)}, s32[1,8]{1,0:T(1,128)}, u32[]{:S(2)}) copy-start(s32[1,8]{1,0:T(1,128)} %seg_branch.1) | copy-start | bytes 100
  0.7 23.2 %collective-permute-start.2 = (bf16[64,256]{1,0:T(8,128)(2,1)}, bf16[64,256]{1,0:T(8,128)(2,1)S(1)}, u32[]{:S(2)}, u32[]{:S(2)}) collective-permute-start(bf16[64,256]{1,0:T(8,128)(2,1)} %bitcast.6), channel_id=1, source_target_pairs={{0,2},{2,4},{4,6},{6,0},{1,3},{3,5},{5,7},{7,1},{8,10},{10,12},{12... | collective-permute-start | bytes 98312 | tf_op jit(solution)/shard_map/ppermute | solution.py:219
  4.0 24.6 %collective-permute-start.1 = (bf16[64,256]{1,0:T(8,128)(2,1)}, bf16[64,256]{1,0:T(8,128)(2,1)S(1)}, u32[]{:S(2)}, u32[]{:S(2)}) collective-permute-start(bf16[64,256]{1,0:T(8,128)(2,1)} %bitcast.7), channel_id=1, source_target_pairs={{0,4},{2,6},{4,0},{6,2},{1,5},{3,7},{5,1},{7,3},{8,12},{10,14},{12... | collective-permute-start | bytes 98312 | tf_op jit(solution)/shard_map/ppermute | solution.py:219
  9.4 13.0 %collective-permute-start.10 = (bf16[64,256]{1,0:T(8,128)(2,1)}, bf16[64,256]{1,0:T(8,128)(2,1)S(1)}, u32[]{:S(2)}, u32[]{:S(2)}) collective-permute-start(bf16[64,256]{1,0:T(8,128)(2,1)} %param.15), channel_id=1, source_target_pairs={{0,4},{2,6},{4,0},{6,2},{1,5},{3,7},{5,1},{7,3},{8,12},{10,14},{12... | collective-permute-start | bytes 98312 | tf_op jit(solution)/shard_map/ppermute | solution.py:219
  9.9 11.9 %collective-permute-start.9 = (bf16[64,256]{1,0:T(8,128)(2,1)}, bf16[64,256]{1,0:T(8,128)(2,1)S(1)}, u32[]{:S(2)}, u32[]{:S(2)}) collective-permute-start(bf16[64,256]{1,0:T(8,128)(2,1)} %param.15), channel_id=1, source_target_pairs={{0,6},{2,0},{4,2},{6,4},{1,7},{3,1},{5,3},{7,5},{8,14},{10,8},{12,... | collective-permute-start | bytes 98312 | tf_op jit(solution)/shard_map/ppermute | solution.py:219
  13.9 1.0 copy-start
  15.0 1.0 copy-start.1
  16.0 1.0 copy-start.2
  17.1 4.7 %copy-start.9 = (bf16[64,256]{1,0:T(8,128)(2,1)S(1)}, bf16[64,256]{1,0:T(8,128)(2,1)}, u32[]{:S(2)}) copy-start(bf16[64,256]{1,0:T(8,128)(2,1)} %param.15) | copy-start | bytes 98308
  20.8 1.0 copy-start.6
  21.8 20.9 %collective-permute-start.6 = (bf16[2048,128]{1,0:T(8,128)(2,1)S(1)}, bf16[2048,128]{1,0:T(8,128)(2,1)S(1)}, u32[]{:S(2)}, u32[]{:S(2)}) collective-permute-start(bf16[2048,128]{1,0:T(8,128)(2,1)S(1)} %get-tuple-element.17.q0), channel_id=1, source_target_pairs={{0,1},{1,0},{2,3},{3,2},{4,5},{5,4},{6,7},{7,6},{8,9},{9,8},{10,11... | collective-permute-start | bytes 1572872 | tf_op jit(solution)/shard_map/ppermute | solution.py:219
  21.8 20.8 %collective-permute-start.7 = (bf16[2048,128]{1,0:T(8,128)(2,1)S(1)}, bf16[2048,128]{1,0:T(8,128)(2,1)S(1)}, u32[]{:S(2)}, u32[]{:S(2)}) collective-permute-start(bf16[2048,128]{1,0:T(8,128)(2,1)S(1)} %get-tuple-element.18.g0), channel_id=1, source_target_pairs={{0,1},{1,0},{2,3},{3,2},{4,5},{5,4},{6,7},{7,6},{8,9},{9,8},{10,11... | collective-permute-start | bytes 1572872 | tf_op jit(solution)/shard_map/ppermute | solution.py:219
  22.4 1.4 %copy-start.10 = (bf16[2,32,256]{2,1,0:T(8,128)(2,1)S(1)}, bf16[2,32,256]{2,1,0:T(8,128)(2,1)}, u32[]{:S(2)}) copy-start(bf16[2,32,256]{2,1,0:T(8,128)(2,1)} %param.16) | copy-start | bytes 98308
  22.4 6.1 %collective-permute-start.11 = (bf16[64,256]{1,0:T(8,128)(2,1)S(1)}, bf16[64,256]{1,0:T(8,128)(2,1)S(1)}, u32[]{:S(2)}, u32[]{:S(2)}) collective-permute-start(bf16[64,256]{1,0:T(8,128)(2,1)S(1)} %copy-done.9), channel_id=1, source_target_pairs={{0,2},{2,4},{4,6},{6,0},{1,3},{3,5},{5,7},{7,1},{8,10},{10,12},{12... | collective-permute-start | bytes 98312 | tf_op jit(solution)/shard_map/ppermute | solution.py:219
  23.9 6.4 %collective-permute-start = (bf16[64,256]{1,0:T(8,128)(2,1)S(1)}, bf16[64,256]{1,0:T(8,128)(2,1)S(1)}, u32[]{:S(2)}, u32[]{:S(2)}) collective-permute-start(bf16[64,256]{1,0:T(8,128)(2,1)S(1)} %bitcast.8), channel_id=1, source_target_pairs={{0,6},{2,0},{4,2},{6,4},{1,7},{3,1},{5,3},{7,5},{8,14},{10,8},{12,... | collective-permute-start | bytes 98312 | tf_op jit(solution)/shard_map/ppermute | solution.py:219
  28.6 4.6 %collective-permute-start.8 = (f32[4,2048]{1,0:T(4,128)S(1)}, f32[4,2048]{1,0:T(4,128)S(1)}, u32[]{:S(2)}, u32[]{:S(2)}) collective-permute-start(f32[4,2048]{1,0:T(4,128)S(1)} %get-tuple-element.19.s0), channel_id=1, source_target_pairs={{0,1},{1,0},{2,3},{3,2},{4,5},{5,4},{6,7},{7,6},{8,9},{9,8},{10,11... | collective-permute-start | bytes 98312 | tf_op jit(solution)/shard_map/ppermute | solution.py:219
  28.6 7.2 %collective-permute-start.14 = (bf16[256,256]{1,0:T(8,128)(2,1)S(1)}, bf16[256,256]{1,0:T(8,128)(2,1)S(1)}, u32[]{:S(2)}, u32[]{:S(2)}) collective-permute-start(bf16[256,256]{1,0:T(8,128)(2,1)S(1)} %constant_dynamic-update-slice_fusion.kv0), channel_id=1, source_target_pairs={{0,8},{8,16},{16,24},{24,0},{1,9},{9,17},{17,25},{25,1},{2,10},{10... | collective-permute-start | bytes 393224 | tf_op jit(solution)/shard_map/ppermute | solution.py:219
  30.2 10.0 %collective-permute-start.13 = (bf16[256,256]{1,0:T(8,128)(2,1)S(1)}, bf16[256,256]{1,0:T(8,128)(2,1)S(1)}, u32[]{:S(2)}, u32[]{:S(2)}) collective-permute-start(bf16[256,256]{1,0:T(8,128)(2,1)S(1)} %constant_dynamic-update-slice_fusion.kv0), channel_id=1, source_target_pairs={{0,16},{8,24},{16,0},{24,8},{1,17},{9,25},{17,1},{25,9},{2,18},{10... | collective-permute-start | bytes 393224 | tf_op jit(solution)/shard_map/ppermute | solution.py:219
  33.2 7.8 %collective-permute-start.12 = (bf16[256,256]{1,0:T(8,128)(2,1)S(1)}, bf16[256,256]{1,0:T(8,128)(2,1)S(1)}, u32[]{:S(2)}, u32[]{:S(2)}) collective-permute-start(bf16[256,256]{1,0:T(8,128)(2,1)S(1)} %constant_dynamic-update-slice_fusion.kv0), channel_id=1, source_target_pairs={{0,24},{8,0},{16,8},{24,16},{1,25},{9,1},{17,9},{25,17},{2,26},{10... | collective-permute-start | bytes 393224 | tf_op jit(solution)/shard_map/ppermute | solution.py:219
  34.6 0.7 copy-start.11
  35.8 25.4 %collective-permute-start.5 = (bf16[256,256]{1,0:T(8,128)(2,1)S(1)}, bf16[256,256]{1,0:T(8,128)(2,1)S(1)}, u32[]{:S(2)}, u32[]{:S(2)}) collective-permute-start(bf16[256,256]{1,0:T(8,128)(2,1)S(1)} %pad_maximum_fusion.kv0), channel_id=1, source_target_pairs={{0,8},{8,16},{16,24},{24,0},{1,9},{9,17},{17,25},{25,1},{2,10},{10... | collective-permute-start | bytes 393224 | tf_op jit(solution)/shard_map/ppermute | solution.py:219
  40.2 21.0 %collective-permute-start.4 = (bf16[256,256]{1,0:T(8,128)(2,1)S(1)}, bf16[256,256]{1,0:T(8,128)(2,1)S(1)}, u32[]{:S(2)}, u32[]{:S(2)}) collective-permute-start(bf16[256,256]{1,0:T(8,128)(2,1)S(1)} %pad_maximum_fusion.kv0), channel_id=1, source_target_pairs={{0,16},{8,24},{16,0},{24,8},{1,17},{9,25},{17,1},{25,9},{2,18},{10... | collective-permute-start | bytes 393224 | tf_op jit(solution)/shard_map/ppermute | solution.py:219
  41.0 20.3 %collective-permute-start.3 = (bf16[256,256]{1,0:T(8,128)(2,1)S(1)}, bf16[256,256]{1,0:T(8,128)(2,1)S(1)}, u32[]{:S(2)}, u32[]{:S(2)}) collective-permute-start(bf16[256,256]{1,0:T(8,128)(2,1)S(1)} %pad_maximum_fusion.kv0), channel_id=1, source_target_pairs={{0,24},{8,0},{16,8},{24,16},{1,25},{9,1},{17,9},{25,17},{2,26},{10... | collective-permute-start | bytes 393224 | tf_op jit(solution)/shard_map/ppermute | solution.py:219
  55.9 1.0 copy-start.7
  56.9 1.0 copy-start.8
  57.9 18.4 %collective-permute-start.16 = (bf16[256,256]{1,0:T(8,128)(2,1)S(1)}, bf16[256,256]{1,0:T(8,128)(2,1)S(1)}, u32[]{:S(2)}, u32[]{:S(2)}) collective-permute-start(bf16[256,256]{1,0:T(8,128)(2,1)S(1)} %get-tuple-element.31), channel_id=1, source_target_pairs={{0,8},{8,16},{16,24},{24,0},{1,9},{9,17},{17,25},{25,1},{2,10},{10... | collective-permute-start | bytes 393224 | tf_op jit(solution)/shard_map/ppermute | solution.py:219
  58.3 20.3 %collective-permute-start.18 = (bf16[256,256]{1,0:T(8,128)(2,1)S(1)}, bf16[256,256]{1,0:T(8,128)(2,1)S(1)}, u32[]{:S(2)}, u32[]{:S(2)}) collective-permute-start(bf16[256,256]{1,0:T(8,128)(2,1)S(1)} %get-tuple-element.32), channel_id=1, source_target_pairs={{0,24},{8,0},{16,8},{24,16},{1,25},{9,1},{17,9},{25,17},{2,26},{10... | collective-permute-start | bytes 393224 | tf_op jit(solution)/shard_map/ppermute | solution.py:219
  61.2 17.4 %collective-permute-start.17 = (bf16[256,256]{1,0:T(8,128)(2,1)S(1)}, bf16[256,256]{1,0:T(8,128)(2,1)S(1)}, u32[]{:S(2)}, u32[]{:S(2)}) collective-permute-start(bf16[256,256]{1,0:T(8,128)(2,1)S(1)} %get-tuple-element.33), channel_id=1, source_target_pairs={{0,16},{8,24},{16,0},{24,8},{1,17},{9,25},{17,1},{25,9},{2,18},{10... | collective-permute-start | bytes 393224 | tf_op jit(solution)/shard_map/ppermute | solution.py:219
  73.0 8.7 %collective-permute-start.26 = (bf16[256,256]{1,0:T(8,128)(2,1)S(1)}, bf16[256,256]{1,0:T(8,128)(2,1)S(1)}, u32[]{:S(2)}, u32[]{:S(2)}) collective-permute-start(bf16[256,256]{1,0:T(8,128)(2,1)S(1)} %get-tuple-element.28), channel_id=1, source_target_pairs={{0,8},{8,16},{16,24},{24,0},{1,9},{9,17},{17,25},{25,1},{2,10},{10... | collective-permute-start | bytes 393224 | tf_op jit(solution)/shard_map/ppermute | solution.py:219
  74.4 8.6 %collective-permute-start.28 = (bf16[256,256]{1,0:T(8,128)(2,1)S(1)}, bf16[256,256]{1,0:T(8,128)(2,1)S(1)}, u32[]{:S(2)}, u32[]{:S(2)}) collective-permute-start(bf16[256,256]{1,0:T(8,128)(2,1)S(1)} %get-tuple-element.29), channel_id=1, source_target_pairs={{0,24},{8,0},{16,8},{24,16},{1,25},{9,1},{17,9},{25,17},{2,26},{10... | collective-permute-start | bytes 393224 | tf_op jit(solution)/shard_map/ppermute | solution.py:219
  76.3 11.5 %collective-permute-start.27 = (bf16[256,256]{1,0:T(8,128)(2,1)S(1)}, bf16[256,256]{1,0:T(8,128)(2,1)S(1)}, u32[]{:S(2)}, u32[]{:S(2)}) collective-permute-start(bf16[256,256]{1,0:T(8,128)(2,1)S(1)} %get-tuple-element.30), channel_id=1, source_target_pairs={{0,16},{8,24},{16,0},{24,8},{1,17},{9,25},{17,1},{25,9},{2,18},{10... | collective-permute-start | bytes 393224 | tf_op jit(solution)/shard_map/ppermute | solution.py:219
  78.6 31.3 %collective-permute-start.15 = (f32[128,2048]{1,0:T(8,128)S(1)}, f32[128,2048]{1,0:T(8,128)S(1)}, u32[]{:S(2)}, u32[]{:S(2)}) collective-permute-start(f32[128,2048]{1,0:T(8,128)S(1)} %get-tuple-element.24), channel_id=1, source_target_pairs={{0,1},{1,0},{2,3},{3,2},{4,5},{5,4},{6,7},{7,6},{8,9},{9,8},{10,11... | collective-permute-start | bytes 3145736 | tf_op jit(solution)/shard_map/ppermute | solution.py:219
  78.7 9.2 %collective-permute-start.19 = (bf16[64,256]{1,0:T(8,128)(2,1)S(1)}, bf16[64,256]{1,0:T(8,128)(2,1)S(1)}, u32[]{:S(2)}, u32[]{:S(2)}) collective-permute-start(bf16[64,256]{1,0:T(8,128)(2,1)S(1)} %get-tuple-element.37), channel_id=1, source_target_pairs={{0,2},{2,4},{4,6},{6,0},{1,3},{3,5},{5,7},{7,1},{8,10},{10,12},{12... | collective-permute-start | bytes 98312 | tf_op jit(solution)/shard_map/ppermute | solution.py:219
  81.7 6.2 %collective-permute-start.21 = (bf16[64,256]{1,0:T(8,128)(2,1)S(1)}, bf16[64,256]{1,0:T(8,128)(2,1)S(1)}, u32[]{:S(2)}, u32[]{:S(2)}) collective-permute-start(bf16[64,256]{1,0:T(8,128)(2,1)S(1)} %get-tuple-element.38), channel_id=1, source_target_pairs={{0,6},{2,0},{4,2},{6,4},{1,7},{3,1},{5,3},{7,5},{8,14},{10,8},{12,... | collective-permute-start | bytes 98312 | tf_op jit(solution)/shard_map/ppermute | solution.py:219
  83.0 8.2 %collective-permute-start.20 = (bf16[64,256]{1,0:T(8,128)(2,1)S(1)}, bf16[64,256]{1,0:T(8,128)(2,1)S(1)}, u32[]{:S(2)}, u32[]{:S(2)}) collective-permute-start(bf16[64,256]{1,0:T(8,128)(2,1)S(1)} %get-tuple-element.39), channel_id=1, source_target_pairs={{0,4},{2,6},{4,0},{6,2},{1,5},{3,7},{5,1},{7,3},{8,12},{10,14},{12... | collective-permute-start | bytes 98312 | tf_op jit(solution)/shard_map/ppermute | solution.py:219
  91.2 6.3 %collective-permute-start.24 = (f32[64,256]{1,0:T(8,128)S(1)}, f32[64,256]{1,0:T(8,128)S(1)}, u32[]{:S(2)}, u32[]{:S(2)}) collective-permute-start(f32[64,256]{1,0:T(8,128)S(1)} %convert_add_fusion.1), channel_id=1, source_target_pairs={{0,96},{32,0},{64,32},{96,64},{1,97},{33,1},{65,33},{97,65},{2,98}... | collective-permute-start | bytes 196616 | tf_op jit(solution)/shard_map/ppermute | solution.py:219
  91.3 8.3 %collective-permute-start.23 = (f32[64,256]{1,0:T(8,128)S(1)}, f32[64,256]{1,0:T(8,128)S(1)}, u32[]{:S(2)}, u32[]{:S(2)}) collective-permute-start(f32[64,256]{1,0:T(8,128)S(1)} %convert_add_fusion.1), channel_id=1, source_target_pairs={{0,64},{32,96},{64,0},{96,32},{1,65},{33,97},{65,1},{97,33},{2,66}... | collective-permute-start | bytes 196616 | tf_op jit(solution)/shard_map/ppermute | solution.py:219
  94.2 10.7 %collective-permute-start.22 = (f32[64,256]{1,0:T(8,128)S(1)}, f32[64,256]{1,0:T(8,128)S(1)}, u32[]{:S(2)}, u32[]{:S(2)}) collective-permute-start(f32[64,256]{1,0:T(8,128)S(1)} %convert_add_fusion.1), channel_id=1, source_target_pairs={{0,32},{32,64},{64,96},{96,0},{1,33},{33,65},{65,97},{97,1},{2,34}... | collective-permute-start | bytes 196616 | tf_op jit(solution)/shard_map/ppermute | solution.py:219
  95.4 10.6 %collective-permute-start.29 = (bf16[64,256]{1,0:T(8,128)(2,1)S(1)}, bf16[64,256]{1,0:T(8,128)(2,1)S(1)}, u32[]{:S(2)}, u32[]{:S(2)}) collective-permute-start(bf16[64,256]{1,0:T(8,128)(2,1)S(1)} %get-tuple-element.34), channel_id=1, source_target_pairs={{0,2},{2,4},{4,6},{6,0},{1,3},{3,5},{5,7},{7,1},{8,10},{10,12},{12... | collective-permute-start | bytes 98312 | tf_op jit(solution)/shard_map/ppermute | solution.py:219
  97.4 8.5 %collective-permute-start.31 = (bf16[64,256]{1,0:T(8,128)(2,1)S(1)}, bf16[64,256]{1,0:T(8,128)(2,1)S(1)}, u32[]{:S(2)}, u32[]{:S(2)}) collective-permute-start(bf16[64,256]{1,0:T(8,128)(2,1)S(1)} %get-tuple-element.35), channel_id=1, source_target_pairs={{0,6},{2,0},{4,2},{6,4},{1,7},{3,1},{5,3},{7,5},{8,14},{10,8},{12,... | collective-permute-start | bytes 98312 | tf_op jit(solution)/shard_map/ppermute | solution.py:219
  99.6 7.8 %collective-permute-start.30 = (bf16[64,256]{1,0:T(8,128)(2,1)S(1)}, bf16[64,256]{1,0:T(8,128)(2,1)S(1)}, u32[]{:S(2)}, u32[]{:S(2)}) collective-permute-start(bf16[64,256]{1,0:T(8,128)(2,1)S(1)} %get-tuple-element.36), channel_id=1, source_target_pairs={{0,4},{2,6},{4,0},{6,2},{1,5},{3,7},{5,1},{7,3},{8,12},{10,14},{12... | collective-permute-start | bytes 98312 | tf_op jit(solution)/shard_map/ppermute | solution.py:219
  105.0 4.4 %collective-permute-start.25 = (f32[64,256]{1,0:T(8,128)S(1)}, f32[64,256]{1,0:T(8,128)S(1)}, u32[]{:S(2)}, u32[]{:S(2)}) collective-permute-start(f32[64,256]{1,0:T(8,128)S(1)} %add_add_fusion), channel_id=1, source_target_pairs={{0,128},{128,0},{1,129},{129,1},{2,130},{130,2},{3,131},{131,3},{4... | collective-permute-start | bytes 196616 | tf_op jit(solution)/shard_map/ppermute | solution.py:219

commit v2 on v1

v2 whole, which is shorter than its diff:
```python
import math

import jax
import jax.numpy as jnp
from jax import lax
from jax.experimental import pallas as pl
from jax.experimental.pallas import tpu as pltpu
from jax.sharding import Mesh
from jax.sharding import PartitionSpec as P

HEADS = 8
HD = 128
TOK = 256
SEGS = 8
TILE = 128
TILES = TOK // TILE
TROWS = TILE * HEADS
ROWS = TOK * HEADS
ROOT_SH = 64
BR_SH = 32
NY = 4
NZ = 4
KB = NY * NZ * BR_SH
SCALE = HD ** (-0.5)
LOG2E = math.log2(math.e)
BIG = 1e30
BF = jnp.bfloat16
F32 = jnp.float32
VMEM = pl.BlockSpec(memory_space=pltpu.VMEM)
HBM = pl.BlockSpec(memory_space=pltpu.HBM)
SMEM = pl.BlockSpec(memory_space=pltpu.SMEM)
PARAMS = pltpu.CompilerParams(vmem_limit_bytes=20 << 20)


def dot(a, b, ca, cb):
    return lax.dot_general(a, b, (((ca,), (cb,)), ((), ())), preferred_element_type=F32)


def move(rows, onehot):
    total = None
    for _ in range(3):
        part = rows.astype(BF)
        rows = rows - part.astype(F32)
        term = dot(part, onehot, 1, 1)
        total = term if total is None else total + term
    return total


def pair_terms(keys, values, q, g, norm, delta, mask=None):
    weight = jnp.exp2(dot(keys, q, 1, 1) * (SCALE * LOG2E) - norm)
    if mask is not None:
        weight = jnp.where(mask, weight, 0.0)
    dscore = weight * (dot(values, g, 1, 1) - delta)
    return weight.astype(BF), dscore.astype(BF)


def prepare_kernel(
    seg_branch, q_hbm, o_hbm, g_hbm, norm_ref, leaf_ref, seg_ref, z0, z1, z2, z3,
    qg_ref, stat_ref, onehot_ref, grad_ref, dq_ref, root_ref, branch_ref, q_ref, o_ref, g_ref, sems,
):
    copies = [
        pltpu.make_async_copy(source, target, sems.at[i])
        for i, (source, target) in enumerate(((q_hbm, q_ref), (g_hbm, g_ref), (o_hbm, o_ref)))
    ]
    for copy in copies:
        copy.start()
    for i, piece in enumerate((z0, z1, z2, z3)):
        at = pl.ds(i * ROOT_SH, ROOT_SH)
        root_ref[at, :] = piece[:ROOT_SH, :]
        branch_ref[at, :] = piece[ROOT_SH:, :]
    segment = seg_ref[...]
    lane = lax.broadcasted_iota(jnp.int32, (1, TOK), 1)
    branch = jnp.zeros((1, TOK), jnp.int32)
    first = jnp.zeros((1, TOK), jnp.int32)
    for s in range(SEGS):
        here = segment == s
        branch = jnp.where(here, seg_branch[0, s], branch)
        ahead = jnp.sum((segment < s).astype(F32), axis=1, keepdims=True).astype(jnp.int32)
        first = jnp.where(here, ahead, first)
    zero_branch = (branch == 0).astype(F32)
    row = lax.broadcasted_iota(jnp.int32, (TOK, TOK), 0)
    col = lax.broadcasted_iota(jnp.int32, (TOK, TOK), 1)
    before = (row < col).astype(F32).astype(BF)
    count = dot(jnp.broadcast_to(zero_branch, (8, TOK)).astype(BF), before, 1, 0)[:1].astype(jnp.int32)
    zeros = jnp.sum(zero_branch, axis=1, keepdims=True).astype(jnp.int32)
    rank = jnp.where(branch == 0, count, zeros + lane - count)
    onehot = (row == rank).astype(F32).astype(BF)
    onehot_ref[...] = onehot

    for i, source in enumerate((q_ref, g_ref)):
        copies[i].wait()
        for h in range(HEADS):
            moved = dot(onehot, source[:, h * HD : (h + 1) * HD], 1, 0).astype(BF)
            for t in range(TILES):
                qg_ref[pl.ds(i * ROWS + (t * HEADS + h) * TILE, TILE), :] = moved[t * TILE : (t + 1) * TILE]
    copies[2].wait()

    columns = []
    for h in range(HEADS):
        at = slice(h * HD, (h + 1) * HD)
        columns.append(
            jnp.sum(g_ref[:, at].astype(F32) * o_ref[:, at].astype(F32), axis=1, keepdims=True)
        )
    delta = move(jnp.concatenate(columns, axis=1).T, onehot)
    norm = move(norm_ref[...], onehot) * LOG2E
    place = jnp.concatenate([lane, first, branch, lane, lane, lane, lane, lane], axis=0)
    place = dot(place.astype(F32).astype(BF), onehot, 1, 1).astype(jnp.int32)
    norm0 = jnp.where(place[2:3] == 0, norm, BIG)
    norm1 = jnp.where(place[2:3] == 0, BIG, norm)
    for t in range(TILES):
        for h in range(HEADS):
            at = pl.ds((t * HEADS + h) * TILE, TILE)
            tok = slice(t * TILE, (t + 1) * TILE)
            for r, value in enumerate((norm, norm0, norm1, delta)):
                stat_ref[r : r + 1, at] = value[h : h + 1, tok]

    keys = leaf_ref[:, :HD]
    values = leaf_ref[:, HD:]
    keys_t = keys.T
    slot = lax.broadcasted_iota(jnp.int32, (TOK, TILE), 0)
    dkey = jnp.zeros((TOK, HD), F32)
    dvalue = jnp.zeros((TOK, HD), F32)
    for t in range(TILES):
        tok = slice(t * TILE, (t + 1) * TILE)
        mask = ((slot >= place[1:2, tok]) & (slot <= place[0:1, tok])).astype(F32)
        mask = jnp.concatenate([mask] * HEADS, axis=1) > 0.0
        at = pl.ds(t * TROWS, TROWS)
        q = qg_ref[at, :]
        g = qg_ref[pl.ds(ROWS + t * TROWS, TROWS), :]
        weight, dscore = pair_terms(keys, values, q, g, stat_ref[0:1, at], stat_ref[3:4, at], mask)
        dkey += dot(dscore, q, 1, 0)
        dvalue += dot(weight, g, 1, 0)
        dq_ref[:, at] = dot(keys_t, dscore, 1, 0)
    grad_ref[:, :HD] = dkey * SCALE
    grad_ref[:, HD:] = dvalue


def sweep(kv_ref, sources, norm_row, grads):
    keys = kv_ref[:, :HD]
    values = kv_ref[:, HD:]
    keys_t = keys.T
    grads[...] = jnp.zeros_like(grads)
    for qg_ref, stat_ref, dq_ref in sources:

        def visit(t, carry):
            at = pl.ds(pl.multiple_of(t * TROWS, TROWS), TROWS)
            g_at = pl.ds(pl.multiple_of(ROWS + t * TROWS, TROWS), TROWS)
            norm = stat_ref[norm_row : norm_row + 1, at]

            def work():
                q = qg_ref[at, :]
                g = qg_ref[g_at, :]
                weight, dscore = pair_terms(keys, values, q, g, norm, stat_ref[3:4, at])
                grads[:, :HD] += dot(dscore, q, 1, 0)
                grads[:, HD:] += dot(weight, g, 1, 0)
                dq_ref[:, at] += dot(keys_t, dscore, 1, 0)

            if norm_row == 0:
                work()
            else:
                pl.when(jnp.min(norm) < 0.5 * BIG)(work)
            return carry

        lax.fori_loop(0, TILES, visit, 0)


def root_kernel(kv0, kv1, kv2, kv3, qg0, s0, qg1, s1, dq0, dq1, to0, to1, to2, to3, kv_ref, total):
    dq0[...] = jnp.zeros_like(dq0)
    dq1[...] = jnp.zeros_like(dq1)
    sources = ((qg0, s0, dq0), (qg1, s1, dq1))
    pieces, targets = (kv0, kv1, kv2, kv3), (to0, to1, to2, to3)
    each = NZ * ROOT_SH
    for first in range(0, NY, KB // each):
        for i in range(KB // each):
            kv_ref[pl.ds(i * each, each), :] = pieces[first + i][...]
        sweep(kv_ref, sources, 0, total)
        for i in range(KB // each):
            at = pl.ds(i * each, each)
            targets[first + i][:, :HD] = (total[at, :HD] * SCALE).astype(BF)
            targets[first + i][:, HD:] = total[at, HD:].astype(BF)


def branch_kernel(
    place, lengths, kv0, kv1, kv2, kv3, qg0, s0, qg1, s1, dq0_in, dq1_in, dq0, dq1, to0, to1, to2, to3, kv_ref, total
):
    dq0[...] = dq0_in[...]
    dq1[...] = dq1_in[...]
    sources = ((qg0, s0, dq0), (qg1, s1, dq1))
    pieces, targets = (kv0, kv1, kv2, kv3), (to0, to1, to2, to3)
    inner = lax.broadcasted_iota(jnp.int32, (BR_SH, 1), 0)

    def live(b, dy, dz):
        y = lax.rem(place[0] + dy, NY)
        z = lax.rem(place[1] + dz, NZ)
        return inner + ((y * NZ + z) * 2 + place[2]) * BR_SH < lengths[b]

    for b in range(2):
        for dy in range(NY):
            for z in range(NZ):
                rows = pieces[dy][pl.ds((z * 2 + b) * BR_SH, BR_SH), :].astype(F32)
                at = pl.ds((dy * NZ + z) * BR_SH, BR_SH)
                kv_ref[at, :] = jnp.where(live(b, dy, z), rows, 0.0).astype(BF)
        sweep(kv_ref, sources, 1 + b, total)
        for dy in range(NY):
            for z in range(NZ):
                ok = live(b, dy, z)
                at = pl.ds((dy * NZ + z) * BR_SH, BR_SH)
                to = pl.ds((z * 2 + b) * BR_SH, BR_SH)
                targets[dy][to, :HD] = jnp.where(ok, total[at, :HD] * SCALE, 0.0).astype(BF)
                targets[dy][to, HD:] = jnp.where(ok, total[at, HD:], 0.0).astype(BF)


def finish_kernel(onehot_ref, leaf, mine, other, out_ref):
    for h in range(HEADS):
        parts = []
        for t in range(TILES):
            at = pl.ds((t * HEADS + h) * TILE, TILE)
            parts.append((((leaf[:, at] + mine[:, at] + other[:, at]) * SCALE).T).astype(BF))
        column = jnp.concatenate(parts, axis=0)
        out_ref[:, h * HD : (h + 1) * HD] = dot(onehot_ref[...], column, 0, 0).astype(BF)


def shape(dims, dtype):
    return jax.ShapeDtypeStruct(dims, dtype)


def shift(value, axis, size, by):
    return lax.ppermute(value, axis, [(i, (i + by) % size) for i in range(size)])


def gather(value, axis, size):
    return [value] + [shift(value, axis, size, -k) for k in range(1, size)]


def exchange(blocks, axis, size):
    return [blocks[0]] + [shift(blocks[k], axis, size, k) for k in range(1, size)]


def added(terms):
    return sum(term.astype(F32) for term in terms[1:]) + terms[0].astype(F32)


def shards(
    queries, attn_out, out_grad, log_norm, leaf_kv, root_kv, branch_kv, branch_len, segment_ids, segment_branch
):
    row_index = lax.axis_index("zl") * 4 + lax.axis_index("x")
    lengths = lax.dynamic_slice_in_dim(branch_len, row_index * 2, 2, 0)
    place = jnp.stack([lax.axis_index("y"), lax.axis_index("zh"), lax.axis_index("c")]).astype(jnp.int32)

    shard = jnp.concatenate([root_kv, branch_kv.reshape(2 * BR_SH, 2 * HD)], axis=0)
    block = shape((NZ * ROOT_SH, 2 * HD), BF)
    qg0, s0, onehot, leaf_grad, dq_leaf, root_z, branch_z = pl.pallas_call(
        prepare_kernel,
        out_shape=(
            shape((2 * ROWS, HD), BF),
            shape((4, ROWS), F32),
            shape((TOK, TOK), BF),
            shape((TOK, 2 * HD), F32),
            shape((HD, ROWS), F32),
            block,
            block,
        ),
        in_specs=[SMEM] + [HBM] * 3 + [VMEM] * 7,
        out_specs=(VMEM,) * 7,
        scratch_shapes=[pltpu.VMEM((TOK, HEADS * HD), BF)] * 3 + [pltpu.SemaphoreType.DMA((3,))],
        compiler_params=PARAMS,
        cost_estimate=pl.CostEstimate(flops=4_000_000_000, bytes_accessed=5_000_000, transcendentals=0),
        name="prepare",
    )(segment_branch, *(pltpu.with_memory_space_constraint(x, pltpu.HBM) for x in (queries, attn_out, out_grad)), log_norm.T, leaf_kv, segment_ids, *gather(shard, "zh", NZ))
    roots = gather(root_z, "y", NY)
    branches = gather(branch_z, "y", NY)
    qg1 = shift(qg0, "c", 2, 1)
    s1 = shift(s0, "c", 2, 1)
    tokens = (qg0, s0, qg1, s1)
    dq_shape = shape((HD, ROWS), F32)


    scratch = [pltpu.VMEM((KB, 2 * HD), BF), pltpu.VMEM((KB, 2 * HD), F32)]

    dq0, dq1, *root_terms = pl.pallas_call(
        root_kernel,
        out_shape=(dq_shape, dq_shape, block, block, block, block),
        in_specs=[VMEM] * 8,
        out_specs=(VMEM,) * 6,
        scratch_shapes=scratch,
        compiler_params=PARAMS,
        cost_estimate=pl.CostEstimate(flops=10_000_000_000, bytes_accessed=8_000_000, transcendentals=0),
        name="root",
    )(*roots, *tokens)
    root_y = exchange(root_terms, "y", NY)

    dq0, dq1, *branch_terms = pl.pallas_call(
        branch_kernel,
        out_shape=(dq_shape, dq_shape, block, block, block, block),
        in_specs=[SMEM] * 2 + [VMEM] * 10,
        out_specs=(VMEM,) * 6,
        scratch_shapes=scratch,
        input_output_aliases={10: 0, 11: 1},
        compiler_params=PARAMS,
        cost_estimate=pl.CostEstimate(flops=9_000_000_000, bytes_accessed=8_000_000, transcendentals=0),
        name="branch",
    )(place, lengths, *branches, *tokens, dq0, dq1)
    root_y, branch_terms, dq0, dq1 = lax.optimization_barrier((root_y, branch_terms, dq0, dq1))
    branch_y = exchange(branch_terms, "y", NY)
    root_y = added(root_y).astype(BF).reshape(NZ, ROOT_SH, 2 * HD)
    other, root_y = lax.optimization_barrier((shift(dq1, "c", 2, 1), root_y))
    root_z = [root_y[0]] + [shift(root_y[k], "zh", NZ, k) for k in (1, 2)]
    last, branch_y[1] = lax.optimization_barrier((root_y[3], branch_y[1]))
    root_z.append(shift(last, "zh", NZ, 3))
    query_grad = pl.pallas_call(
        finish_kernel,
        out_shape=shape((TOK, HEADS * HD), BF),
        in_specs=[VMEM] * 4,
        out_specs=VMEM,
        compiler_params=PARAMS,
        cost_estimate=pl.CostEstimate(flops=200_000_000, bytes_accessed=3_000_000, transcendentals=0),
        name="finish",
    )(onehot, dq_leaf, dq0, other)
    branch_y, root_z, query_grad = lax.optimization_barrier((branch_y, root_z, query_grad))

    root_part = added(root_z)
    near = [shift(root_part, "x", 4, k) for k in (1, 2, 3)]
    branch_y = added(branch_y).astype(BF).reshape(NZ, 2, BR_SH, 2 * HD)
    branch_z = exchange([branch_y[k] for k in range(NZ)], "zh", NZ)
    root_x = (root_part + near[1]) + (near[0] + near[2])
    root_one = root_x + shift(root_x, "zl", 2, 1)
    branch_one = added(branch_z)
    return query_grad, leaf_grad, root_one, branch_one


def solution(mesh):
    fine = Mesh(mesh.devices.reshape(2, 4, NY, NZ, 2), ("zl", "x", "y", "zh", "c"))
    rows, cols = ("zl", "x"), ("y", "zh", "c")
    both = rows + cols
    in_specs = (
        P(both, None),
        P(both, None),
        P(both, None),
        P(both, None),
        P(both, None),
        P(cols, None),
        P(rows, cols, None),
        P(),
        P(both, None),
        P(both, None),
    )
    out_specs = (P(both, None), P(both, None), P(cols, None), P(rows, cols, None))
    return jax.shard_map(shards, mesh=fine, in_specs=in_specs, out_specs=out_specs, check_vma=False)
```

time: 112 us -> 106 us (0.946)
  starting transfers between devices: 58.8 us -> 51.4 us
  waiting for transfers between devices: 12.3 us -> 18.2 us
  local copies, waits for them, and re-layouts: 7.74 us -> 2.82 us
    ppermute x32 -> x28, starting transfers between devices: 58.8 us -> 51.4 us  [shift(): lax.ppermute(value, axis, [(i, (i + by) % size) for i in range(size)])]
    ppermute x32 -> x28, waiting for transfers between devices: 12.3 us -> 18.2 us  [shift(): lax.ppermute(value, axis, [(i, (i + by) % size) for i in range(size)])]
    unnamed x28 -> x14, local copies, waits for them, and re-layouts: 7.59 us -> 2.72 us
  transfers between devices with their start and end apart: 32 -> 28, of which waited for: 6 -> 7; matrix products, arithmetic and copies ran while one was open for 2% -> 1% of each run, Pallas kernels for 26% -> 24%
where the time goes in v2:
time: 106 us
  starting transfers between devices  51.4 us (48%)
  Pallas kernels  30.5 us (29%)
  waiting for transfers between devices  18.2 us (17%)
  local copies, waits for them, and re-layouts  2.82 us (3%)
  other arithmetic  2.36 us (2%)
    ppermute x28, starting transfers between devices, shift(): lax.ppermute(value, axis, [(i, (i + by) % size) for i in range(size)])  51.4 us
    ppermute x28, waiting for transfers between devices, shift(): lax.ppermute(value, axis, [(i, (i + by) % size) for i in range(size)])  18.2 us
    pallas_call x1, Pallas kernels, shards(): pl.pallas_call(root_kernel, out_shape=(dq_shape, dq_shape, block, block,...  12.8 us
    pallas_call x1, Pallas kernels, shards(): pl.pallas_call(branch_kernel, out_shape=(dq_shape, dq_shape, block, block...  10.9 us
    pallas_call x1, Pallas kernels, shards(): pl.pallas_call(prepare_kernel, out_shape=(shape((2 * ROWS, HD), BF), shap...  5.28 us
    unnamed x14, local copies, waits for them, and re-layouts  2.72 us
  transfers between devices with their start and end apart: 28, of which 7 were waited for; matrix products, arithmetic and copies ran while one was open for 1% of the time, Pallas kernels for 24%

profile of v2, /device:TPU:2, one launch (start us, length us, event | category | flops | bytes accessed | tf_op | source)
XLA Modules:
  0.0 106.1 jit_solution(10999928337361168275)
XLA Ops:
  0.6 0.8 pad_maximum_fusion.z0
  1.5 3.3 %collective-permute-start.2 = (bf16[128,256]{1,0:T(8,128)(2,1)S(1)}, bf16[128,256]{1,0:T(8,128)(2,1)S(1)}, u32[]{:S(2)}, u32[]{:S(2)}) collective-permute-start(bf16[128,256]{1,0:T(8,128)(2,1)S(1)} %pad_maximum_fusion.z0), channel_id=1, source_target_pairs={{0,2},{2,4},{4,6},{6,0},{1,3},{3,5},{5,7},{7,1},{8,10},{10,12},{12... | collective-permute-start | bytes 196616 | tf_op jit(solution)/shard_map/ppermute | solution.py:228
  4.8 5.4 %collective-permute-start.1 = (bf16[128,256]{1,0:T(8,128)(2,1)S(1)}, bf16[128,256]{1,0:T(8,128)(2,1)S(1)}, u32[]{:S(2)}, u32[]{:S(2)}) collective-permute-start(bf16[128,256]{1,0:T(8,128)(2,1)S(1)} %pad_maximum_fusion.z0), channel_id=1, source_target_pairs={{0,4},{2,6},{4,0},{6,2},{1,5},{3,7},{5,1},{7,3},{8,12},{10,14},{12... | collective-permute-start | bytes 196616 | tf_op jit(solution)/shard_map/ppermute | solution.py:228
  10.2 2.7 %collective-permute-start = (bf16[128,256]{1,0:T(8,128)(2,1)S(1)}, bf16[128,256]{1,0:T(8,128)(2,1)S(1)}, u32[]{:S(2)}, u32[]{:S(2)}) collective-permute-start(bf16[128,256]{1,0:T(8,128)(2,1)S(1)} %pad_maximum_fusion.z0), channel_id=1, source_target_pairs={{0,6},{2,0},{4,2},{6,4},{1,7},{3,1},{5,3},{7,5},{8,14},{10,8},{12,... | collective-permute-start | bytes 196616 | tf_op jit(solution)/shard_map/ppermute | solution.py:228
  12.9 1.5 %collective-permute-done.1.z2 = bf16[128,256]{1,0:T(8,128)(2,1)S(1)} collective-permute-done((bf16[128,256]{1,0:T(8,128)(2,1)S(1)}, bf16[128,256]{1,0:T(8,128)(2,1)S(1)}, u32[]{:S(2)}, u32[]{:S(2)}) %collective-permute-start.1) | collective-permute-done | bytes 65568 | tf_op jit(solution)/shard_map/ppermute | solution.py:228
  14.3 2.8 %collective-permute-done.z1 = bf16[128,256]{1,0:T(8,128)(2,1)S(1)} collective-permute-done((bf16[128,256]{1,0:T(8,128)(2,1)S(1)}, bf16[128,256]{1,0:T(8,128)(2,1)S(1)}, u32[]{:S(2)}, u32[]{:S(2)}) %collective-permute-start) | collective-permute-done | bytes 65568 | tf_op jit(solution)/shard_map/ppermute | solution.py:228
  17.1 0.0 copy-start.3
  17.2 0.7 copy-done.3
  17.8 5.3 %prepare.1 = (bf16[4096,128]{1,0:T(8,128)(2,1)S(1)}, f32[4,2048]{1,0:T(4,128)S(1)}, bf16[256,256]{1,0:T(8,128)(2,1)S(1)}, f32[256,256]{1,0:T(8,128)}, f32[128,20...) custom-call(s32[1,8]{1,0:T(1,128)S(1)} %copy-done.5, bf16[256,1024]{1,0:T(8,128)(2,1)} %q_hbm.1, ...), custom_call_target="tpu_custom_call" | custom-call | flops 4000000000 | bytes 5000000 | tf_op jit(solution)/shard_map/prepare/pallas_call | solution.py:252
  23.1 0.0 copy-start.1
  23.1 0.6 copy-done.1
  23.8 0.0 collective-permute-start.6
  23.8 1.6 %collective-permute-start.5 = (bf16[256,256]{1,0:T(8,128)(2,1)S(1)}, bf16[256,256]{1,0:T(8,128)(2,1)}, u32[]{:S(2)}, u32[]{:S(2)}) collective-permute-start(bf16[256,256]{1,0:T(8,128)(2,1)S(1)} %get-tuple-element.46.kv0), channel_id=1, source_target_pairs={{0,8},{8,16},{16,24},{24,0},{1,9},{9,17},{17,25},{25,1},{2,10},{10... | collective-permute-start | bytes 393224 | tf_op jit(solution)/shard_map/ppermute | solution.py:228
  25.3 2.9 %collective-permute-start.4 = (bf16[256,256]{1,0:T(8,128)(2,1)S(1)}, bf16[256,256]{1,0:T(8,128)(2,1)}, u32[]{:S(2)}, u32[]{:S(2)}) collective-permute-start(bf16[256,256]{1,0:T(8,128)(2,1)S(1)} %get-tuple-element.46.kv0), channel_id=1, source_target_pairs={{0,16},{8,24},{16,0},{24,8},{1,17},{9,25},{17,1},{25,9},{2,18},{10... | collective-permute-start | bytes 393224 | tf_op jit(solution)/shard_map/ppermute | solution.py:228
  28.2 1.3 %collective-permute-start.3 = (bf16[256,256]{1,0:T(8,128)(2,1)S(1)}, bf16[256,256]{1,0:T(8,128)(2,1)}, u32[]{:S(2)}, u32[]{:S(2)}) collective-permute-start(bf16[256,256]{1,0:T(8,128)(2,1)S(1)} %get-tuple-element.46.kv0), channel_id=1, source_target_pairs={{0,24},{8,0},{16,8},{24,16},{1,25},{9,1},{17,9},{25,17},{2,26},{10... | collective-permute-start | bytes 393224 | tf_op jit(solution)/shard_map/ppermute | solution.py:228
  29.6 0.0 collective-permute-start.7
  29.6 0.1 pad_add_fusion.place
  29.7 0.7 copy-done.6
  30.3 0.1 dynamic_slice.3.lengths
  30.4 0.7 collective-permute-done.7.s1
  31.1 0.7 collective-permute-start.13
  31.8 0.0 collective-permute-done.5.kv3
  31.8 4.0 %collective-permute-start.12 = (bf16[256,256]{1,0:T(8,128)(2,1)S(1)}, bf16[256,256]{1,0:T(8,128)(2,1)S(1)}, u32[]{:S(2)}, u32[]{:S(2)}) collective-permute-start(bf16[256,256]{1,0:T(8,128)(2,1)S(1)} %get-tuple-element.53.kv0), channel_id=1, source_target_pairs={{0,16},{8,24},{16,0},{24,8},{1,17},{9,25},{17,1},{25,9},{2,18},{10... | collective-permute-start | bytes 393224 | tf_op jit(solution)/shard_map/ppermute | solution.py:228
  35.8 0.0 collective-permute-done.4.kv2
  35.8 0.0 collective-permute-start.11
  35.8 0.0 collective-permute-done.3.kv1
  35.8 0.0 copy-start.2
  35.8 0.7 copy-done.2
  36.6 12.8 %root.1 = (f32[128,2048]{1,0:T(8,128)S(1)}, f32[128,2048]{1,0:T(8,128)S(1)}, bf16[256,256]{1,0:T(8,128)(2,1)S(1)}, bf16[256,256]{1,0:T(8,128)(2,1)S(1)}, bf16[25...) custom-call(bf16[256,256]{1,0:T(8,128)(2,1)S(1)} %get-tuple-element.46.kv0, ...), custom_call_target="tpu_custom_call" | custom-call | flops 10000000000 | bytes 8000000 | tf_op jit(solution)/shard_map/root/pallas_call | solution.py:280
  49.3 2.1 %collective-permute-start.8 = (bf16[256,256]{1,0:T(8,128)(2,1)S(1)}, bf16[256,256]{1,0:T(8,128)(2,1)S(1)}, u32[]{:S(2)}, u32[]{:S(2)}) collective-permute-start(bf16[256,256]{1,0:T(8,128)(2,1)S(1)} %get-tuple-element.50), channel_id=1, source_target_pairs={{0,8},{8,16},{16,24},{24,0},{1,9},{9,17},{17,25},{25,1},{2,10},{10... | collective-permute-start | bytes 393224 | tf_op jit(solution)/shard_map/ppermute | solution.py:228
  51.4 0.8 collective-permute-start.9
  52.2 0.0 collective-permute-done.13.kv3
  52.2 2.4 %collective-permute-start.10 = (bf16[256,256]{1,0:T(8,128)(2,1)S(1)}, bf16[256,256]{1,0:T(8,128)(2,1)S(1)}, u32[]{:S(2)}, u32[]{:S(2)}) collective-permute-start(bf16[256,256]{1,0:T(8,128)(2,1)S(1)} %get-tuple-element.52), channel_id=1, source_target_pairs={{0,24},{8,0},{16,8},{24,16},{1,25},{9,1},{17,9},{25,17},{2,26},{10... | collective-permute-start | bytes 393224 | tf_op jit(solution)/shard_map/ppermute | solution.py:228
  54.6 0.0 collective-permute-done.12.kv2
  54.6 0.0 collective-permute-done.11.kv1
  54.6 10.9 %branch.1 = (f32[128,2048]{1,0:T(8,128)S(1)}, f32[128,2048]{1,0:T(8,128)S(1)}, bf16[256,256]{1,0:T(8,128)(2,1)S(1)}, bf16[256,256]{1,0:T(8,128)(2,1)S(1)}, bf16[...) custom-call(s32[3]{0:T(128)S(1)} %pad_add_fusion.place, ...), custom_call_target="tpu_custom_call", output_to_operand_aliasing={{0}: (10, {}), {1}: (11, {})} | custom-call | flops 8999999488 | bytes 8000000 | tf_op jit(solution)/shard_map/branch/pallas_call | solution.py:292
  65.5 0.0 collective-permute-done.8
  65.5 0.0 collective-permute-done.10
  65.5 0.1 collective-permute-start.14
  65.6 0.1 collective-permute-start.15
  65.7 2.4 %collective-permute-start.16 = (bf16[256,256]{1,0:T(8,128)(2,1)S(1)}, bf16[256,256]{1,0:T(8,128)(2,1)S(1)}, u32[]{:S(2)}, u32[]{:S(2)}) collective-permute-start(bf16[256,256]{1,0:T(8,128)(2,1)S(1)} %get-tuple-element.71), channel_id=1, source_target_pairs={{0,16},{8,24},{16,0},{24,8},{1,17},{9,25},{17,1},{25,9},{2,18},{10... | collective-permute-start | bytes 393224 | tf_op jit(solution)/shard_map/ppermute | solution.py:228
  68.1 1.2 %collective-permute-start.17 = (bf16[256,256]{1,0:T(8,128)(2,1)S(1)}, bf16[256,256]{1,0:T(8,128)(2,1)S(1)}, u32[]{:S(2)}, u32[]{:S(2)}) collective-permute-start(bf16[256,256]{1,0:T(8,128)(2,1)S(1)} %get-tuple-element.72), channel_id=1, source_target_pairs={{0,24},{8,0},{16,8},{24,16},{1,25},{9,1},{17,9},{25,17},{2,26},{10... | collective-permute-start | bytes 393224 | tf_op jit(solution)/shard_map/ppermute | solution.py:228
  69.3 0.1 add_convert_fusion.1
  69.4 6.1 %collective-permute-done.15 = bf16[256,256]{1,0:T(8,128)(2,1)S(1)} collective-permute-done((bf16[256,256]{1,0:T(8,128)(2,1)S(1)}, bf16[256,256]{1,0:T(8,128)(2,1)S(1)}, u32[]{:S(2)}, u32[]{:S(2)}) %collective-permute-start.15) | collective-permute-done | bytes 131104 | tf_op jit(solution)/shard_map/ppermute | solution.py:228
  75.5 3.4 %collective-permute-start.20 = (bf16[64,256]{1,0:T(8,128)(2,1)S(1)}, bf16[64,256]{1,0:T(8,128)(2,1)S(1)}, u32[]{:S(2)}, u32[]{:S(2)}) collective-permute-start(bf16[64,256]{1,0:T(8,128)(2,1)S(1)} %get-tuple-element.73), channel_id=1, source_target_pairs={{0,6},{2,0},{4,2},{6,4},{1,7},{3,1},{5,3},{7,5},{8,14},{10,8},{12,... | collective-permute-start | bytes 98312 | tf_op jit(solution)/shard_map/ppermute | solution.py:228
  78.9 2.2 %collective-permute-start.19 = (bf16[64,256]{1,0:T(8,128)(2,1)S(1)}, bf16[64,256]{1,0:T(8,128)(2,1)S(1)}, u32[]{:S(2)}, u32[]{:S(2)}) collective-permute-start(bf16[64,256]{1,0:T(8,128)(2,1)S(1)} %get-tuple-element.92), channel_id=1, source_target_pairs={{0,4},{2,6},{4,0},{6,2},{1,5},{3,7},{5,1},{7,3},{8,12},{10,14},{12... | collective-permute-start | bytes 98312 | tf_op jit(solution)/shard_map/ppermute | solution.py:228
  81.1 1.2 %collective-permute-start.18 = (bf16[64,256]{1,0:T(8,128)(2,1)S(1)}, bf16[64,256]{1,0:T(8,128)(2,1)S(1)}, u32[]{:S(2)}, u32[]{:S(2)}) collective-permute-start(bf16[64,256]{1,0:T(8,128)(2,1)S(1)} %get-tuple-element.93), channel_id=1, source_target_pairs={{0,2},{2,4},{4,6},{6,0},{1,3},{3,5},{5,7},{7,1},{8,10},{10,12},{12... | collective-permute-start | bytes 98312 | tf_op jit(solution)/shard_map/ppermute | solution.py:228
  82.4 1.6 %finish.1 = bf16[256,1024]{1,0:T(8,128)(2,1)} custom-call(bf16[256,256]{1,0:T(8,128)(2,1)S(1)} %get-tuple-element.74.onehot_ref, f32[128,2048]{1,0:T(8,128)S(1)} %get-tuple-element.75.leaf, f32[128,2048]{1,0:T(8,128)S(1)} %get-tuple-element.76.mine, f32[128,2048]{1,0:T(8,128)S(1)} %collective-permute-done.14.other), custom_call_target="tpu_custom_call" | custom-call | flops 200000000 | bytes 3000000 | tf_op jit(solution)/shard_map/finish/pallas_call | solution.py:310
  83.9 0.0 collective-permute-done.16
  83.9 0.0 collective-permute-done.17
  83.9 0.0 collective-permute-done.20
  83.9 2.9 %collective-permute-done.19 = bf16[64,256]{1,0:T(8,128)(2,1)S(1)} collective-permute-done((bf16[64,256]{1,0:T(8,128)(2,1)S(1)}, bf16[64,256]{1,0:T(8,128)(2,1)S(1)}, u32[]{:S(2)}, u32[]{:S(2)}) %collective-permute-start.19) | collective-permute-done | bytes 32800 | tf_op jit(solution)/shard_map/ppermute | solution.py:228
  86.8 0.3 collective-permute-done.18
  87.2 0.6 collective-permute-start.23
  87.8 1.5 %collective-permute-start.22 = (f32[64,256]{1,0:T(8,128)S(1)}, f32[64,256]{1,0:T(8,128)S(1)}, u32[]{:S(2)}, u32[]{:S(2)}) collective-permute-start(f32[64,256]{1,0:T(8,128)S(1)} %convert_add_fusion.1), channel_id=1, source_target_pairs={{0,32},{32,64},{64,96},{96,0},{1,33},{33,65},{65,97},{97,1},{2,34}... | collective-permute-start | bytes 196616 | tf_op jit(solution)/shard_map/ppermute | solution.py:228
  89.3 3.3 %collective-permute-start.21 = (f32[64,256]{1,0:T(8,128)S(1)}, f32[64,256]{1,0:T(8,128)S(1)}, u32[]{:S(2)}, u32[]{:S(2)}) collective-permute-start(f32[64,256]{1,0:T(8,128)S(1)} %convert_add_fusion.1), channel_id=1, source_target_pairs={{0,64},{32,96},{64,0},{96,32},{1,65},{33,97},{65,1},{97,33},{2,66}... | collective-permute-start | bytes 196616 | tf_op jit(solution)/shard_map/ppermute | solution.py:228
  92.6 0.1 add_convert_fusion
  92.7 0.1 collective-permute-start.25
  92.8 4.1 %collective-permute-start.27 = (bf16[2,32,256]{2,1,0:T(8,128)(2,1)S(1)}, bf16[2,32,256]{2,1,0:T(8,128)(2,1)S(1)}, u32[]{:S(2)}, u32[]{:S(2)}) collective-permute-start(bf16[2,32,256]{2,1,0:T(8,128)(2,1)S(1)} %bitcast.24), channel_id=1, source_target_pairs={{0,6},{2,0},{4,2},{6,4},{1,7},{3,1},{5,3},{7,5},{8,14},{10,8},{12,... | collective-permute-start | bytes 98312 | tf_op jit(solution)/shard_map/ppermute | solution.py:228
  96.9 3.8 %collective-permute-start.26 = (bf16[2,32,256]{2,1,0:T(8,128)(2,1)S(1)}, bf16[2,32,256]{2,1,0:T(8,128)(2,1)S(1)}, u32[]{:S(2)}, u32[]{:S(2)}) collective-permute-start(bf16[2,32,256]{2,1,0:T(8,128)(2,1)S(1)} %bitcast.23), channel_id=1, source_target_pairs={{0,4},{2,6},{4,0},{6,2},{1,5},{3,7},{5,1},{7,3},{8,12},{10,14},{12... | collective-permute-start | bytes 98312 | tf_op jit(solution)/shard_map/ppermute | solution.py:228
  100.7 0.3 collective-permute-start.24
  101.0 3.8 %collective-permute-done.26 = bf16[2,32,256]{2,1,0:T(8,128)(2,1)S(1)} collective-permute-done((bf16[2,32,256]{2,1,0:T(8,128)(2,1)S(1)}, bf16[2,32,256]{2,1,0:T(8,128)(2,1)S(1)}, u32[]{:S(2)}, u32[]{:S(2)}) %collective-permute-start.26) | collective-permute-done | bytes 32800 | tf_op jit(solution)/shard_map/ppermute | solution.py:228
  104.8 0.6 convert_add_fusion
  105.5 0.6 add.65
  (21 shorter events, 0.1 us)
Async XLA Ops:
  0.6 16.5 %copy-start = (bf16[256,256]{1,0:T(8,128)(2,1)S(1)}, bf16[256,256]{1,0:T(8,128)(2,1)}, u32[]{:S(2)}) copy-start(bf16[256,256]{1,0:T(8,128)(2,1)} %leaf_ref.1) | copy-start | bytes 393220
  1.5 15.7 %copy-start.4 = (s32[1,256]{1,0:T(1,128)S(1)}, s32[1,256]{1,0:T(1,128)}, u32[]{:S(2)}) copy-start(s32[1,256]{1,0:T(1,128)} %seg_ref.1) | copy-start | bytes 3076
  1.5 15.7 %copy-start.5 = (s32[1,8]{1,0:T(1,128)S(1)}, s32[1,8]{1,0:T(1,128)}, u32[]{:S(2)}) copy-start(s32[1,8]{1,0:T(1,128)} %seg_branch.1) | copy-start | bytes 100
  1.5 11.4 %collective-permute-start.2 = (bf16[128,256]{1,0:T(8,128)(2,1)S(1)}, bf16[128,256]{1,0:T(8,128)(2,1)S(1)}, u32[]{:S(2)}, u32[]{:S(2)}) collective-permute-start(bf16[128,256]{1,0:T(8,128)(2,1)S(1)} %pad_maximum_fusion.z0), channel_id=1, source_target_pairs={{0,2},{2,4},{4,6},{6,0},{1,3},{3,5},{5,7},{7,1},{8,10},{10,12},{12... | collective-permute-start | bytes 196616 | tf_op jit(solution)/shard_map/ppermute | solution.py:228
  4.8 9.5 %collective-permute-start.1 = (bf16[128,256]{1,0:T(8,128)(2,1)S(1)}, bf16[128,256]{1,0:T(8,128)(2,1)S(1)}, u32[]{:S(2)}, u32[]{:S(2)}) collective-permute-start(bf16[128,256]{1,0:T(8,128)(2,1)S(1)} %pad_maximum_fusion.z0), channel_id=1, source_target_pairs={{0,4},{2,6},{4,0},{6,2},{1,5},{3,7},{5,1},{7,3},{8,12},{10,14},{12... | collective-permute-start | bytes 196616 | tf_op jit(solution)/shard_map/ppermute | solution.py:228
  10.2 6.9 %collective-permute-start = (bf16[128,256]{1,0:T(8,128)(2,1)S(1)}, bf16[128,256]{1,0:T(8,128)(2,1)S(1)}, u32[]{:S(2)}, u32[]{:S(2)}) collective-permute-start(bf16[128,256]{1,0:T(8,128)(2,1)S(1)} %pad_maximum_fusion.z0), channel_id=1, source_target_pairs={{0,6},{2,0},{4,2},{6,4},{1,7},{3,1},{5,3},{7,5},{8,14},{10,8},{12,... | collective-permute-start | bytes 196616 | tf_op jit(solution)/shard_map/ppermute | solution.py:228
  17.1 0.7 copy-start.3
  23.1 0.6 copy-start.1
  23.8 12.0 %collective-permute-start.6 = (bf16[4096,128]{1,0:T(8,128)(2,1)S(1)}, bf16[4096,128]{1,0:T(8,128)(2,1)S(1)}, u32[]{:S(2)}, u32[]{:S(2)}) collective-permute-start(bf16[4096,128]{1,0:T(8,128)(2,1)S(1)} %get-tuple-element.47.qg0), channel_id=1, source_target_pairs={{0,1},{1,0},{2,3},{3,2},{4,5},{5,4},{6,7},{7,6},{8,9},{9,8},{10,11... | collective-permute-start | bytes 3145736 | tf_op jit(solution)/shard_map/ppermute | solution.py:228
  23.8 8.1 %collective-permute-start.5 = (bf16[256,256]{1,0:T(8,128)(2,1)S(1)}, bf16[256,256]{1,0:T(8,128)(2,1)}, u32[]{:S(2)}, u32[]{:S(2)}) collective-permute-start(bf16[256,256]{1,0:T(8,128)(2,1)S(1)} %get-tuple-element.46.kv0), channel_id=1, source_target_pairs={{0,8},{8,16},{16,24},{24,0},{1,9},{9,17},{17,25},{25,1},{2,10},{10... | collective-permute-start | bytes 393224 | tf_op jit(solution)/shard_map/ppermute | solution.py:228
  25.3 10.4 %collective-permute-start.4 = (bf16[256,256]{1,0:T(8,128)(2,1)S(1)}, bf16[256,256]{1,0:T(8,128)(2,1)}, u32[]{:S(2)}, u32[]{:S(2)}) collective-permute-start(bf16[256,256]{1,0:T(8,128)(2,1)S(1)} %get-tuple-element.46.kv0), channel_id=1, source_target_pairs={{0,16},{8,24},{16,0},{24,8},{1,17},{9,25},{17,1},{25,9},{2,18},{10... | collective-permute-start | bytes 393224 | tf_op jit(solution)/shard_map/ppermute | solution.py:228
  28.2 7.6 %collective-permute-start.3 = (bf16[256,256]{1,0:T(8,128)(2,1)S(1)}, bf16[256,256]{1,0:T(8,128)(2,1)}, u32[]{:S(2)}, u32[]{:S(2)}) collective-permute-start(bf16[256,256]{1,0:T(8,128)(2,1)S(1)} %get-tuple-element.46.kv0), channel_id=1, source_target_pairs={{0,24},{8,0},{16,8},{24,16},{1,25},{9,1},{17,9},{25,17},{2,26},{10... | collective-permute-start | bytes 393224 | tf_op jit(solution)/shard_map/ppermute | solution.py:228
  29.6 1.6 %collective-permute-start.7 = (f32[4,2048]{1,0:T(4,128)}, f32[4,2048]{1,0:T(4,128)}, u32[]{:S(2)}, u32[]{:S(2)}) collective-permute-start(f32[4,2048]{1,0:T(4,128)} %copy-done.1), channel_id=1, source_target_pairs={{0,1},{1,0},{2,3},{3,2},{4,5},{5,4},{6,7},{7,6},{8,9},{9,8},{10,11... | collective-permute-start | bytes 98312 | tf_op jit(solution)/shard_map/ppermute | solution.py:228
  29.7 0.7 copy-start.6
  31.1 21.1 %collective-permute-start.13 = (bf16[256,256]{1,0:T(8,128)(2,1)S(1)}, bf16[256,256]{1,0:T(8,128)(2,1)S(1)}, u32[]{:S(2)}, u32[]{:S(2)}) collective-permute-start(bf16[256,256]{1,0:T(8,128)(2,1)S(1)} %get-tuple-element.53.kv0), channel_id=1, source_target_pairs={{0,8},{8,16},{16,24},{24,0},{1,9},{9,17},{17,25},{25,1},{2,10},{10... | collective-permute-start | bytes 393224 | tf_op jit(solution)/shard_map/ppermute | solution.py:228
  31.8 22.8 %collective-permute-start.12 = (bf16[256,256]{1,0:T(8,128)(2,1)S(1)}, bf16[256,256]{1,0:T(8,128)(2,1)S(1)}, u32[]{:S(2)}, u32[]{:S(2)}) collective-permute-start(bf16[256,256]{1,0:T(8,128)(2,1)S(1)} %get-tuple-element.53.kv0), channel_id=1, source_target_pairs={{0,16},{8,24},{16,0},{24,8},{1,17},{9,25},{17,1},{25,9},{2,18},{10... | collective-permute-start | bytes 393224 | tf_op jit(solution)/shard_map/ppermute | solution.py:228
  35.8 18.8 %collective-permute-start.11 = (bf16[256,256]{1,0:T(8,128)(2,1)S(1)}, bf16[256,256]{1,0:T(8,128)(2,1)S(1)}, u32[]{:S(2)}, u32[]{:S(2)}) collective-permute-start(bf16[256,256]{1,0:T(8,128)(2,1)S(1)} %get-tuple-element.53.kv0), channel_id=1, source_target_pairs={{0,24},{8,0},{16,8},{24,16},{1,25},{9,1},{17,9},{25,17},{2,26},{10... | collective-permute-start | bytes 393224 | tf_op jit(solution)/shard_map/ppermute | solution.py:228
  35.8 0.8 copy-start.2
  49.3 16.1 %collective-permute-start.8 = (bf16[256,256]{1,0:T(8,128)(2,1)S(1)}, bf16[256,256]{1,0:T(8,128)(2,1)S(1)}, u32[]{:S(2)}, u32[]{:S(2)}) collective-permute-start(bf16[256,256]{1,0:T(8,128)(2,1)S(1)} %get-tuple-element.50), channel_id=1, source_target_pairs={{0,8},{8,16},{16,24},{24,0},{1,9},{9,17},{17,25},{25,1},{2,10},{10... | collective-permute-start | bytes 393224 | tf_op jit(solution)/shard_map/ppermute | solution.py:228
  51.4 14.1 %collective-permute-start.9 = (bf16[256,256]{1,0:T(8,128)(2,1)S(1)}, bf16[256,256]{1,0:T(8,128)(2,1)S(1)}, u32[]{:S(2)}, u32[]{:S(2)}) collective-permute-start(bf16[256,256]{1,0:T(8,128)(2,1)S(1)} %get-tuple-element.51), channel_id=1, source_target_pairs={{0,16},{8,24},{16,0},{24,8},{1,17},{9,25},{17,1},{25,9},{2,18},{10... | collective-permute-start | bytes 393224 | tf_op jit(solution)/shard_map/ppermute | solution.py:228
  52.2 13.3 %collective-permute-start.10 = (bf16[256,256]{1,0:T(8,128)(2,1)S(1)}, bf16[256,256]{1,0:T(8,128)(2,1)S(1)}, u32[]{:S(2)}, u32[]{:S(2)}) collective-permute-start(bf16[256,256]{1,0:T(8,128)(2,1)S(1)} %get-tuple-element.52), channel_id=1, source_target_pairs={{0,24},{8,0},{16,8},{24,16},{1,25},{9,1},{17,9},{25,17},{2,26},{10... | collective-permute-start | bytes 393224 | tf_op jit(solution)/shard_map/ppermute | solution.py:228
  65.5 3.9 %collective-permute-start.14 = (f32[128,2048]{1,0:T(8,128)S(1)}, f32[128,2048]{1,0:T(8,128)S(1)}, u32[]{:S(2)}, u32[]{:S(2)}) collective-permute-start(f32[128,2048]{1,0:T(8,128)S(1)} %get-tuple-element.63), channel_id=1, source_target_pairs={{0,1},{1,0},{2,3},{3,2},{4,5},{5,4},{6,7},{7,6},{8,9},{9,8},{10,11... | collective-permute-start | bytes 3145736 | tf_op jit(solution)/shard_map/ppermute | solution.py:228
  65.6 9.9 %collective-permute-start.15 = (bf16[256,256]{1,0:T(8,128)(2,1)S(1)}, bf16[256,256]{1,0:T(8,128)(2,1)S(1)}, u32[]{:S(2)}, u32[]{:S(2)}) collective-permute-start(bf16[256,256]{1,0:T(8,128)(2,1)S(1)} %get-tuple-element.69), channel_id=1, source_target_pairs={{0,8},{8,16},{16,24},{24,0},{1,9},{9,17},{17,25},{25,1},{2,10},{10... | collective-permute-start | bytes 393224 | tf_op jit(solution)/shard_map/ppermute | solution.py:228
  65.7 18.2 %collective-permute-start.16 = (bf16[256,256]{1,0:T(8,128)(2,1)S(1)}, bf16[256,256]{1,0:T(8,128)(2,1)S(1)}, u32[]{:S(2)}, u32[]{:S(2)}) collective-permute-start(bf16[256,256]{1,0:T(8,128)(2,1)S(1)} %get-tuple-element.71), channel_id=1, source_target_pairs={{0,16},{8,24},{16,0},{24,8},{1,17},{9,25},{17,1},{25,9},{2,18},{10... | collective-permute-start | bytes 393224 | tf_op jit(solution)/shard_map/ppermute | solution.py:228
  68.1 15.8 %collective-permute-start.17 = (bf16[256,256]{1,0:T(8,128)(2,1)S(1)}, bf16[256,256]{1,0:T(8,128)(2,1)S(1)}, u32[]{:S(2)}, u32[]{:S(2)}) collective-permute-start(bf16[256,256]{1,0:T(8,128)(2,1)S(1)} %get-tuple-element.72), channel_id=1, source_target_pairs={{0,24},{8,0},{16,8},{24,16},{1,25},{9,1},{17,9},{25,17},{2,26},{10... | collective-permute-start | bytes 393224 | tf_op jit(solution)/shard_map/ppermute | solution.py:228
  75.5 8.4 %collective-permute-start.20 = (bf16[64,256]{1,0:T(8,128)(2,1)S(1)}, bf16[64,256]{1,0:T(8,128)(2,1)S(1)}, u32[]{:S(2)}, u32[]{:S(2)}) collective-permute-start(bf16[64,256]{1,0:T(8,128)(2,1)S(1)} %get-tuple-element.73), channel_id=1, source_target_pairs={{0,6},{2,0},{4,2},{6,4},{1,7},{3,1},{5,3},{7,5},{8,14},{10,8},{12,... | collective-permute-start | bytes 98312 | tf_op jit(solution)/shard_map/ppermute | solution.py:228
  78.9 7.9 %collective-permute-start.19 = (bf16[64,256]{1,0:T(8,128)(2,1)S(1)}, bf16[64,256]{1,0:T(8,128)(2,1)S(1)}, u32[]{:S(2)}, u32[]{:S(2)}) collective-permute-start(bf16[64,256]{1,0:T(8,128)(2,1)S(1)} %get-tuple-element.92), channel_id=1, source_target_pairs={{0,4},{2,6},{4,0},{6,2},{1,5},{3,7},{5,1},{7,3},{8,12},{10,14},{12... | collective-permute-start | bytes 98312 | tf_op jit(solution)/shard_map/ppermute | solution.py:228
  81.1 6.0 %collective-permute-start.18 = (bf16[64,256]{1,0:T(8,128)(2,1)S(1)}, bf16[64,256]{1,0:T(8,128)(2,1)S(1)}, u32[]{:S(2)}, u32[]{:S(2)}) collective-permute-start(bf16[64,256]{1,0:T(8,128)(2,1)S(1)} %get-tuple-element.93), channel_id=1, source_target_pairs={{0,2},{2,4},{4,6},{6,0},{1,3},{3,5},{5,7},{7,1},{8,10},{10,12},{12... | collective-permute-start | bytes 98312 | tf_op jit(solution)/shard_map/ppermute | solution.py:228
  87.2 9.8 %collective-permute-start.23 = (f32[64,256]{1,0:T(8,128)S(1)}, f32[64,256]{1,0:T(8,128)S(1)}, u32[]{:S(2)}, u32[]{:S(2)}) collective-permute-start(f32[64,256]{1,0:T(8,128)S(1)} %convert_add_fusion.1), channel_id=1, source_target_pairs={{0,96},{32,0},{64,32},{96,64},{1,97},{33,1},{65,33},{97,65},{2,98}... | collective-permute-start | bytes 196616 | tf_op jit(solution)/shard_map/ppermute | solution.py:228
  87.8 12.9 %collective-permute-start.22 = (f32[64,256]{1,0:T(8,128)S(1)}, f32[64,256]{1,0:T(8,128)S(1)}, u32[]{:S(2)}, u32[]{:S(2)}) collective-permute-start(f32[64,256]{1,0:T(8,128)S(1)} %convert_add_fusion.1), channel_id=1, source_target_pairs={{0,32},{32,64},{64,96},{96,0},{1,33},{33,65},{65,97},{97,1},{2,34}... | collective-permute-start | bytes 196616 | tf_op jit(solution)/shard_map/ppermute | solution.py:228
  89.3 11.4 %collective-permute-start.21 = (f32[64,256]{1,0:T(8,128)S(1)}, f32[64,256]{1,0:T(8,128)S(1)}, u32[]{:S(2)}, u32[]{:S(2)}) collective-permute-start(f32[64,256]{1,0:T(8,128)S(1)} %convert_add_fusion.1), channel_id=1, source_target_pairs={{0,64},{32,96},{64,0},{96,32},{1,65},{33,97},{65,1},{97,33},{2,66}... | collective-permute-start | bytes 196616 | tf_op jit(solution)/shard_map/ppermute | solution.py:228
  92.7 8.3 %collective-permute-start.25 = (bf16[2,32,256]{2,1,0:T(8,128)(2,1)S(1)}, bf16[2,32,256]{2,1,0:T(8,128)(2,1)S(1)}, u32[]{:S(2)}, u32[]{:S(2)}) collective-permute-start(bf16[2,32,256]{2,1,0:T(8,128)(2,1)S(1)} %bitcast.25), channel_id=1, source_target_pairs={{0,2},{2,4},{4,6},{6,0},{1,3},{3,5},{5,7},{7,1},{8,10},{10,12},{12... | collective-permute-start | bytes 98312 | tf_op jit(solution)/shard_map/ppermute | solution.py:228
  92.8 8.2 %collective-permute-start.27 = (bf16[2,32,256]{2,1,0:T(8,128)(2,1)S(1)}, bf16[2,32,256]{2,1,0:T(8,128)(2,1)S(1)}, u32[]{:S(2)}, u32[]{:S(2)}) collective-permute-start(bf16[2,32,256]{2,1,0:T(8,128)(2,1)S(1)} %bitcast.24), channel_id=1, source_target_pairs={{0,6},{2,0},{4,2},{6,4},{1,7},{3,1},{5,3},{7,5},{8,14},{10,8},{12,... | collective-permute-start | bytes 98312 | tf_op jit(solution)/shard_map/ppermute | solution.py:228
  96.9 7.9 %collective-permute-start.26 = (bf16[2,32,256]{2,1,0:T(8,128)(2,1)S(1)}, bf16[2,32,256]{2,1,0:T(8,128)(2,1)S(1)}, u32[]{:S(2)}, u32[]{:S(2)}) collective-permute-start(bf16[2,32,256]{2,1,0:T(8,128)(2,1)S(1)} %bitcast.23), channel_id=1, source_target_pairs={{0,4},{2,6},{4,0},{6,2},{1,5},{3,7},{5,1},{7,3},{8,12},{10,14},{12... | collective-permute-start | bytes 98312 | tf_op jit(solution)/shard_map/ppermute | solution.py:228
  100.7 4.8 %collective-permute-start.24 = (f32[64,256]{1,0:T(8,128)S(1)}, f32[64,256]{1,0:T(8,128)S(1)}, u32[]{:S(2)}, u32[]{:S(2)}) collective-permute-start(f32[64,256]{1,0:T(8,128)S(1)} %add_add_fusion), channel_id=1, source_target_pairs={{0,128},{128,0},{1,129},{129,1},{2,130},{130,2},{3,131},{131,3},{4... | collective-permute-start | bytes 196616 | tf_op jit(solution)/shard_map/ppermute | solution.py:228

commit v3 on v2

--- a/solution.py
+++ b/solution.py
@@ -55,8 +55,8 @@
 
 
 def prepare_kernel(
-    seg_branch, q_hbm, o_hbm, g_hbm, norm_ref, leaf_ref, seg_ref, z0, z1, z2, z3,
-    qg_ref, stat_ref, onehot_ref, grad_ref, dq_ref, root_ref, branch_ref, q_ref, o_ref, g_ref, sems,
+    seg_branch, q_hbm, o_hbm, g_hbm, norm_ref, leaf_ref, seg_ref,
+    qg_ref, stat_ref, onehot_ref, grad_ref, dq_ref, q_ref, o_ref, g_ref, sems,
 ):
     copies = [
         pltpu.make_async_copy(source, target, sems.at[i])
@@ -64,10 +64,6 @@
     ]
     for copy in copies:
         copy.start()
-    for i, piece in enumerate((z0, z1, z2, z3)):
-        at = pl.ds(i * ROOT_SH, ROOT_SH)
-        root_ref[at, :] = piece[:ROOT_SH, :]
-        branch_ref[at, :] = piece[ROOT_SH:, :]
     segment = seg_ref[...]
     lane = lax.broadcasted_iota(jnp.int32, (1, TOK), 1)
     branch = jnp.zeros((1, TOK), jnp.int32)
@@ -135,11 +131,17 @@
     grad_ref[:, HD:] = dvalue
 
 
+def pack_kernel(z0, z1, z2, z3, root_ref, branch_ref):
+    for i, piece in enumerate((z0, z1, z2, z3)):
+        at = pl.ds(i * ROOT_SH, ROOT_SH)
+        root_ref[at, :] = piece[:ROOT_SH, :]
+        branch_ref[at, :] = piece[ROOT_SH:, :]
+
+
 def sweep(kv_ref, sources, norm_row, grads):
     keys = kv_ref[:, :HD]
     values = kv_ref[:, HD:]
     keys_t = keys.T
-    grads[...] = jnp.zeros_like(grads)
     for qg_ref, stat_ref, dq_ref in sources:
 
         def visit(t, carry):
@@ -173,6 +175,7 @@
     for first in range(0, NY, KB // each):
         for i in range(KB // each):
             kv_ref[pl.ds(i * each, each), :] = pieces[first + i][...]
+        total[...] = jnp.zeros_like(total)
         sweep(kv_ref, sources, 0, total)
         for i in range(KB // each):
             at = pl.ds(i * each, each)
@@ -180,34 +183,41 @@
             targets[first + i][:, HD:] = total[at, HD:].astype(BF)
 
 
-def branch_kernel(
-    place, lengths, kv0, kv1, kv2, kv3, qg0, s0, qg1, s1, dq0_in, dq1_in, dq0, dq1, to0, to1, to2, to3, kv_ref, total
+def live_slots(place, lengths, b, dy, dz):
+    y = lax.rem(place[0] + dy, NY)
+    z = lax.rem(place[1] + dz, NZ)
+    start = ((y * NZ + z) * 2 + place[2]) * BR_SH
+    return lax.broadcasted_iota(jnp.int32, (BR_SH, 1), 0) + start < lengths[b]
+
+
+def branch_other_kernel(place, lengths, kv0, kv1, kv2, kv3, qg_ref, stat_ref, dq_in, dq_ref, kv_ref, total):
+    dq_ref[...] = dq_in[...]
+    total[...] = jnp.zeros_like(total)
+    for b in range(2):
+        for dy, piece in enumerate((kv0, kv1, kv2, kv3)):
+            for dz in range(NZ):
+                rows = piece[pl.ds((dz * 2 + b) * BR_SH, BR_SH), :].astype(F32)
+                at = pl.ds(b * KB + (dy * NZ + dz) * BR_SH, BR_SH)
+                kv_ref[at, :] = jnp.where(live_slots(place, lengths, b, dy, dz), rows, 0.0).astype(BF)
+        at = pl.ds(b * KB, KB)
+        sweep(kv_ref.at[at, :], ((qg_ref, stat_ref, dq_ref),), 1 + b, total.at[at, :])
+
+
+def branch_own_kernel(
+    place, lengths, kv_ref, total_in, qg_ref, stat_ref, dq_in, dq_ref, to0, to1, to2, to3, total
 ):
-    dq0[...] = dq0_in[...]
-    dq1[...] = dq1_in[...]
-    sources = ((qg0, s0, dq0), (qg1, s1, dq1))
-    pieces, targets = (kv0, kv1, kv2, kv3), (to0, to1, to2, to3)
-    inner = lax.broadcasted_iota(jnp.int32, (BR_SH, 1), 0)
-
-    def live(b, dy, dz):
-        y = lax.rem(place[0] + dy, NY)
-        z = lax.rem(place[1] + dz, NZ)
-        return inner + ((y * NZ + z) * 2 + place[2]) * BR_SH < lengths[b]
-
+    dq_ref[...] = dq_in[...]
     for b in range(2):
-        for dy in range(NY):
-            for z in range(NZ):
-                rows = pieces[dy][pl.ds((z * 2 + b) * BR_SH, BR_SH), :].astype(F32)
-                at = pl.ds((dy * NZ + z) * BR_SH, BR_SH)
-                kv_ref[at, :] = jnp.where(live(b, dy, z), rows, 0.0).astype(BF)
-        sweep(kv_ref, sources, 1 + b, total)
-        for dy in range(NY):
-            for z in range(NZ):
-                ok = live(b, dy, z)
-                at = pl.ds((dy * NZ + z) * BR_SH, BR_SH)
-                to = pl.ds((z * 2 + b) * BR_SH, BR_SH)
-                targets[dy][to, :HD] = jnp.where(ok, total[at, :HD] * SCALE, 0.0).astype(BF)
-                targets[dy][to, HD:] = jnp.where(ok, total[at, HD:], 0.0).astype(BF)
+        whole = pl.ds(b * KB, KB)
+        total[...] = total_in[whole, :]
+        sweep(kv_ref.at[whole, :], ((qg_ref, stat_ref, dq_ref),), 1 + b, total)
+        for dy, target in enumerate((to0, to1, to2, to3)):
+            for dz in range(NZ):
+                ok = live_slots(place, lengths, b, dy, dz)
+                at = pl.ds((dy * NZ + dz) * BR_SH, BR_SH)
+                to = pl.ds((dz * 2 + b) * BR_SH, BR_SH)
+                target[to, :HD] = jnp.where(ok, total[at, :HD] * SCALE, 0.0).astype(BF)
+                target[to, HD:] = jnp.where(ok, total[at, HD:], 0.0).astype(BF)
 
 
 def finish_kernel(onehot_ref, leaf, mine, other, out_ref):
@@ -249,7 +259,7 @@
 
     shard = jnp.concatenate([root_kv, branch_kv.reshape(2 * BR_SH, 2 * HD)], axis=0)
     block = shape((NZ * ROOT_SH, 2 * HD), BF)
-    qg0, s0, onehot, leaf_grad, dq_leaf, root_z, branch_z = pl.pallas_call(
+    qg0, s0, onehot, leaf_grad, dq_leaf = pl.pallas_call(
         prepare_kernel,
         out_shape=(
             shape((2 * ROWS, HD), BF),
@@ -257,16 +267,24 @@
             shape((TOK, TOK), BF),
             shape((TOK, 2 * HD), F32),
             shape((HD, ROWS), F32),
-            block,
-            block,
         ),
-        in_specs=[SMEM] + [HBM] * 3 + [VMEM] * 7,
-        out_specs=(VMEM,) * 7,
+        in_specs=[SMEM] + [HBM] * 3 + [VMEM] * 3,
+        out_specs=(VMEM,) * 5,
         scratch_shapes=[pltpu.VMEM((TOK, HEADS * HD), BF)] * 3 + [pltpu.SemaphoreType.DMA((3,))],
         compiler_params=PARAMS,
         cost_estimate=pl.CostEstimate(flops=4_000_000_000, bytes_accessed=5_000_000, transcendentals=0),
         name="prepare",
-    )(segment_branch, *(pltpu.with_memory_space_constraint(x, pltpu.HBM) for x in (queries, attn_out, out_grad)), log_norm.T, leaf_kv, segment_ids, *gather(shard, "zh", NZ))
+    )(segment_branch, *(pltpu.with_memory_space_constraint(x, pltpu.HBM) for x in (queries, attn_out, out_grad)), log_norm.T, leaf_kv, segment_ids)
+    pieces, qg0, s0 = lax.optimization_barrier((gather(shard, "zh", NZ), qg0, s0))
+    root_z, branch_z = pl.pallas_call(
+        pack_kernel,
+        out_shape=(block, block),
+        in_specs=[VMEM] * 4,
+        out_specs=(VMEM,) * 2,
+        compiler_params=PARAMS,
+        cost_estimate=pl.CostEstimate(flops=0, bytes_accessed=600_000, transcendentals=0),
+        name="pack",
+    )(*pieces)
     roots = gather(root_z, "y", NY)
     branches = gather(branch_z, "y", NY)
     qg1 = shift(qg0, "c", 2, 1)
@@ -289,24 +307,38 @@
     )(*roots, *tokens)
     root_y = exchange(root_terms, "y", NY)
 
-    dq0, dq1, *branch_terms = pl.pallas_call(
-        branch_kernel,
-        out_shape=(dq_shape, dq_shape, block, block, block, block),
-        in_specs=[SMEM] * 2 + [VMEM] * 10,
-        out_specs=(VMEM,) * 6,
-        scratch_shapes=scratch,
-        input_output_aliases={10: 0, 11: 1},
-        compiler_params=PARAMS,
-        cost_estimate=pl.CostEstimate(flops=9_000_000_000, bytes_accessed=8_000_000, transcendentals=0),
-        name="branch",
-    )(place, lengths, *branches, *tokens, dq0, dq1)
-    root_y, branch_terms, dq0, dq1 = lax.optimization_barrier((root_y, branch_terms, dq0, dq1))
+    branch_cost = pl.CostEstimate(flops=4_500_000_000, bytes_accessed=5_000_000, transcendentals=0)
+    dq1, branch_kv_all, branch_total = pl.pallas_call(
+        branch_other_kernel,
+        out_shape=(dq_shape, shape((2 * KB, 2 * HD), BF), shape((2 * KB, 2 * HD), F32)),
+        in_specs=[SMEM] * 2 + [VMEM] * 7,
+        out_specs=(VMEM,) * 3,
+        input_output_aliases={8: 0},
+        compiler_params=PARAMS,
+        cost_estimate=branch_cost,
+        name="branch_other",
+    )(place, lengths, *branches, qg1, s1, dq1)
+    root_y, dq1, branch_total = lax.optimization_barrier((root_y, dq1, branch_total))
+    other = shift(dq1, "c", 2, 1)
+    root_y = added(root_y).astype(BF).reshape(NZ, ROOT_SH, 2 * HD)
+    root_z = exchange([root_y[k] for k in range(NZ)], "zh", NZ)
+
+    dq0, *branch_terms = pl.pallas_call(
+        branch_own_kernel,
+        out_shape=(dq_shape, block, block, block, block),
+        in_specs=[SMEM] * 2 + [VMEM] * 5,
+        out_specs=(VMEM,) * 5,
+        scratch_shapes=[pltpu.VMEM((KB, 2 * HD), F32)],
+        input_output_aliases={6: 0},
+        compiler_params=PARAMS,
+        cost_estimate=branch_cost,
+        name="branch_own",
+    )(place, lengths, branch_kv_all, branch_total, qg0, s0, dq0)
+    root_z, other, branch_terms, dq0 = lax.optimization_barrier((root_z, other, branch_terms, dq0))
+
     branch_y = exchange(branch_terms, "y", NY)
-    root_y = added(root_y).astype(BF).reshape(NZ, ROOT_SH, 2 * HD)
-    other, root_y = lax.optimization_barrier((shift(dq1, "c", 2, 1), root_y))
-    root_z = [root_y[0]] + [shift(root_y[k], "zh", NZ, k) for k in (1, 2)]
-    last, branch_y[1] = lax.optimization_barrier((root_y[3], branch_y[1]))
-    root_z.append(shift(last, "zh", NZ, 3))
+    root_part = added(root_z)
+    near = [shift(root_part, "x", 4, k) for k in (1, 2, 3)]
     query_grad = pl.pallas_call(
         finish_kernel,
         out_shape=shape((TOK, HEADS * HD), BF),
@@ -316,10 +348,8 @@
         cost_estimate=pl.CostEstimate(flops=200_000_000, bytes_accessed=3_000_000, transcendentals=0),
         name="finish",
     )(onehot, dq_leaf, dq0, other)
-    branch_y, root_z, query_grad = lax.optimization_barrier((branch_y, root_z, query_grad))
-
-    root_part = added(root_z)
-    near = [shift(root_part, "x", 4, k) for k in (1, 2, 3)]
+    branch_y, near, query_grad = lax.optimization_barrier((branch_y, near, query_grad))
+
     branch_y = added(branch_y).astype(BF).reshape(NZ, 2, BR_SH, 2 * HD)
     branch_z = exchange([branch_y[k] for k in range(NZ)], "zh", NZ)
     root_x = (root_part + near[1]) + (near[0] + near[2])

time: 106 us -> 93.6 us (0.88); the launches traced: 106 us -> 91.7 us
  waiting for transfers between devices: 18.2 us -> 4.62 us
  starting transfers between devices: 51.4 us -> 49.9 us
    ppermute x28, waiting for transfers between devices: 18.2 us -> 4.62 us  [shift(): lax.ppermute(value, axis, [(i, (i + by) % size) for i in range(size)])]
    ppermute x28, starting transfers between devices: 51.4 us -> 49.9 us  [shift(): lax.ppermute(value, axis, [(i, (i + by) % size) for i in range(size)])]
    pallas_call x1 -> x3, Pallas kernels: 10.9 us -> 11.8 us  [the longest x1 6.04 us: shards(): pl.pallas_call(branch_other_kernel, out_shape=(dq_shape, shape((2 * KB, 2...]
    unnamed x14 -> x16, local copies, waits for them, and re-layouts: 2.72 us -> 2.57 us
  transfers between devices with their start and end apart: 28 -> 28, of which waited for: 7 -> 4; matrix products, arithmetic and copies ran while one was open for 1% -> 1% of each run, Pallas kernels for 24% -> 34%
where the time goes in v3:
time: 93.6 us; the launch traced here: 91.7 us
  starting transfers between devices  49.9 us (53%)
  Pallas kernels  31.3 us (33%)
  waiting for transfers between devices  4.62 us (5%)
  local copies, waits for them, and re-layouts  2.67 us (3%)
  other arithmetic  2.36 us (3%)
    ppermute x28, starting transfers between devices, shift(): lax.ppermute(value, axis, [(i, (i + by) % size) for i in range(size)])  49.9 us
    pallas_call x1, Pallas kernels, shards(): pl.pallas_call(root_kernel, out_shape=(dq_shape, dq_shape, block, block,...  12.8 us
    pallas_call x1, Pallas kernels, shards(): pl.pallas_call(branch_other_kernel, out_shape=(dq_shape, shape((2 * KB, 2...  6.04 us
    pallas_call x1, Pallas kernels, shards(): pl.pallas_call(branch_own_kernel, out_shape=(dq_shape, block, block, bloc...  5.71 us
    pallas_call x1, Pallas kernels, shards(): pl.pallas_call(prepare_kernel, out_shape=(shape((2 * ROWS, HD), BF), shap...  5.26 us
    ppermute x28, waiting for transfers between devices, shift(): lax.ppermute(value, axis, [(i, (i + by) % size) for i in range(size)])  4.62 us
    unnamed x16, local copies, waits for them, and re-layouts  2.57 us
  transfers between devices with their start and end apart: 28, of which 4 were waited for; matrix products, arithmetic and copies ran while one was open for 1% of the time, Pallas kernels for 34%

profile of v3, /device:TPU:2, one launch (start us, length us, event | category | flops | bytes accessed | tf_op | source)
XLA Modules:
  0.0 91.7 jit_solution(5456015386142141251)
XLA Ops:
  0.6 0.8 pad_maximum_fusion.z0
  1.5 3.3 %collective-permute-start.2 = (bf16[128,256]{1,0:T(8,128)(2,1)S(1)}, bf16[128,256]{1,0:T(8,128)(2,1)S(1)}, u32[]{:S(2)}, u32[]{:S(2)}) collective-permute-start(bf16[128,256]{1,0:T(8,128)(2,1)S(1)} %pad_maximum_fusion.z0), channel_id=1, source_target_pairs={{0,2},{2,4},{4,6},{6,0},{1,3},{3,5},{5,7},{7,1},{8,10},{10,12},{12... | collective-permute-start | bytes 196616 | tf_op jit(solution)/shard_map/ppermute | solution.py:238
  4.8 5.4 %collective-permute-start.1 = (bf16[128,256]{1,0:T(8,128)(2,1)S(1)}, bf16[128,256]{1,0:T(8,128)(2,1)S(1)}, u32[]{:S(2)}, u32[]{:S(2)}) collective-permute-start(bf16[128,256]{1,0:T(8,128)(2,1)S(1)} %pad_maximum_fusion.z0), channel_id=1, source_target_pairs={{0,4},{2,6},{4,0},{6,2},{1,5},{3,7},{5,1},{7,3},{8,12},{10,14},{12... | collective-permute-start | bytes 196616 | tf_op jit(solution)/shard_map/ppermute | solution.py:238
  10.2 2.7 %collective-permute-start = (bf16[128,256]{1,0:T(8,128)(2,1)S(1)}, bf16[128,256]{1,0:T(8,128)(2,1)S(1)}, u32[]{:S(2)}, u32[]{:S(2)}) collective-permute-start(bf16[128,256]{1,0:T(8,128)(2,1)S(1)} %pad_maximum_fusion.z0), channel_id=1, source_target_pairs={{0,6},{2,0},{4,2},{6,4},{1,7},{3,1},{5,3},{7,5},{8,14},{10,8},{12,... | collective-permute-start | bytes 196616 | tf_op jit(solution)/shard_map/ppermute | solution.py:238
  12.9 0.7 copy-done.4
  13.6 5.3 %prepare.1 = (bf16[4096,128]{1,0:T(8,128)(2,1)S(1)}, f32[4,2048]{1,0:T(4,128)S(1)}, bf16[256,256]{1,0:T(8,128)(2,1)S(1)}, f32[256,256]{1,0:T(8,128)}, f32[128,2048]{1,0:T(8,128)S(1)}) custom-call(s32[1,8]{1,0:T(1,128)S(1)} %copy-done.6, bf16[256,1024]{1,0:T(8,128)(2,1)} %q_hbm.1, bf16[256,1024]{1,0:T(8,128)(2,1)} %o_hbm.1, bf16[256,1024]{1,0:T(8,128)(2,1)} %g_hbm.1, ...), custom_call_target="tpu_custom_call" | custom-call | flops 4000000000 | bytes 5000000 | tf_op jit(solution)/shard_map/prepare/pallas_call | solution.py:262
  18.8 0.0 copy-start.1
  18.9 0.0 collective-permute-done.2.z3
  18.9 0.0 collective-permute-done.1.z2
  18.9 0.0 collective-permute-done.z1
  18.9 0.1 collective-permute-start.6
  19.0 0.4 copy-done.1
  19.5 1.6 %collective-permute-start.5 = (bf16[256,256]{1,0:T(8,128)(2,1)S(1)}, bf16[256,256]{1,0:T(8,128)(2,1)}, u32[]{:S(2)}, u32[]{:S(2)}) collective-permute-start(bf16[256,256]{1,0:T(8,128)(2,1)S(1)} %get-tuple-element.61.kv0), channel_id=1, source_target_pairs={{0,8},{8,16},{16,24},{24,0},{1,9},{9,17},{17,25},{25,1},{2,10},{10... | collective-permute-start | bytes 393224 | tf_op jit(solution)/shard_map/ppermute | solution.py:238
  21.0 2.9 %collective-permute-start.4 = (bf16[256,256]{1,0:T(8,128)(2,1)S(1)}, bf16[256,256]{1,0:T(8,128)(2,1)}, u32[]{:S(2)}, u32[]{:S(2)}) collective-permute-start(bf16[256,256]{1,0:T(8,128)(2,1)S(1)} %get-tuple-element.61.kv0), channel_id=1, source_target_pairs={{0,16},{8,24},{16,0},{24,8},{1,17},{9,25},{17,1},{25,9},{2,18},{10... | collective-permute-start | bytes 393224 | tf_op jit(solution)/shard_map/ppermute | solution.py:238
  23.9 1.3 %collective-permute-start.3 = (bf16[256,256]{1,0:T(8,128)(2,1)S(1)}, bf16[256,256]{1,0:T(8,128)(2,1)}, u32[]{:S(2)}, u32[]{:S(2)}) collective-permute-start(bf16[256,256]{1,0:T(8,128)(2,1)S(1)} %get-tuple-element.61.kv0), channel_id=1, source_target_pairs={{0,24},{8,0},{16,8},{24,16},{1,25},{9,1},{17,9},{25,17},{2,26},{10... | collective-permute-start | bytes 393224 | tf_op jit(solution)/shard_map/ppermute | solution.py:238
  25.3 0.0 collective-permute-start.7
  25.3 0.1 pad_add_fusion.place
  25.4 0.7 copy-done.7
  26.0 0.1 dynamic_slice.3.lengths
  26.1 0.7 collective-permute-done.7.s1.stat_ref
  26.8 0.7 collective-permute-start.13
  27.5 3.6 %collective-permute-start.12 = (bf16[256,256]{1,0:T(8,128)(2,1)S(1)}, bf16[256,256]{1,0:T(8,128)(2,1)S(1)}, u32[]{:S(2)}, u32[]{:S(2)}) collective-permute-start(bf16[256,256]{1,0:T(8,128)(2,1)S(1)} %get-tuple-element.68.kv0), channel_id=1, source_target_pairs={{0,16},{8,24},{16,0},{24,8},{1,17},{9,25},{17,1},{25,9},{2,18},{10... | collective-permute-start | bytes 393224 | tf_op jit(solution)/shard_map/ppermute | solution.py:238
  31.1 0.1 collective-permute-done.4.kv2
  31.2 0.0 collective-permute-start.11
  31.2 0.0 collective-permute-done.3.kv1
  31.2 0.0 collective-permute-done.6.qg1.qg_ref
  31.2 0.0 copy-start.2
  31.2 0.7 copy-done.2
  31.9 12.8 %root.1 = (f32[128,2048]{1,0:T(8,128)S(1)}, f32[128,2048]{1,0:T(8,128)S(1)}, bf16[256,256]{1,0:T(8,128)(2,1)S(1)}, bf16[256,256]{1,0:T(8,128)(2,1)S(1)}, bf16[25...) custom-call(bf16[256,256]{1,0:T(8,128)(2,1)S(1)} %get-tuple-element.61.kv0, ...), custom_call_target="tpu_custom_call" | custom-call | flops 10000000000 | bytes 8000000 | tf_op jit(solution)/shard_map/root/pallas_call | solution.py:298
  44.7 2.1 %collective-permute-start.8 = (bf16[256,256]{1,0:T(8,128)(2,1)S(1)}, bf16[256,256]{1,0:T(8,128)(2,1)S(1)}, u32[]{:S(2)}, u32[]{:S(2)}) collective-permute-start(bf16[256,256]{1,0:T(8,128)(2,1)S(1)} %get-tuple-element.65), channel_id=1, source_target_pairs={{0,8},{8,16},{16,24},{24,0},{1,9},{9,17},{17,25},{25,1},{2,10},{10... | collective-permute-start | bytes 393224 | tf_op jit(solution)/shard_map/ppermute | solution.py:238
  46.8 0.8 collective-permute-start.9
  47.6 0.0 collective-permute-done.13.kv3
  47.6 2.0 %collective-permute-start.10 = (bf16[256,256]{1,0:T(8,128)(2,1)S(1)}, bf16[256,256]{1,0:T(8,128)(2,1)S(1)}, u32[]{:S(2)}, u32[]{:S(2)}) collective-permute-start(bf16[256,256]{1,0:T(8,128)(2,1)S(1)} %get-tuple-element.67), channel_id=1, source_target_pairs={{0,24},{8,0},{16,8},{24,16},{1,25},{9,1},{17,9},{25,17},{2,26},{10... | collective-permute-start | bytes 393224 | tf_op jit(solution)/shard_map/ppermute | solution.py:238
  49.6 6.0 %branch_other.1 = (f32[128,2048]{1,0:T(8,128)S(1)}, bf16[1024,256]{1,0:T(8,128)(2,1)S(1)}, f32[1024,256]{1,0:T(8,128)S(1)}) custom-call(s32[3]{0:T(128)S(1)} %pad_add_fusion.place, s32[2]{0:T(128)S(1)} %dynamic_slice.3.lengths, bf16[256,256]{1,0:T(8,128)(2,1)S(1)} %get-tuple-element.68.kv0, ...), custom_call_target="tpu_custom_call", output_to_operand_aliasing={{0}: (8, {})} | custom-call | flops 4499999744 | bytes 5000000 | tf_op jit(solution)/shard_map/branch_other/pallas_call | solution.py:311
  55.6 0.0 collective-permute-done.8
  55.7 0.0 collective-permute-done.10
  55.7 0.1 collective-permute-start.17
  55.8 0.1 add_convert_fusion.1
  55.9 0.0 copy-start.3
  55.9 2.1 %collective-permute-start.16 = (bf16[64,256]{1,0:T(8,128)(2,1)S(1)}, bf16[64,256]{1,0:T(8,128)(2,1)S(1)}, u32[]{:S(2)}, u32[]{:S(2)}) collective-permute-start(bf16[64,256]{1,0:T(8,128)(2,1)S(1)} %get-tuple-element.110), channel_id=1, source_target_pairs={{0,6},{2,0},{4,2},{6,4},{1,7},{3,1},{5,3},{7,5},{8,14},{10,8},{12,... | collective-permute-start | bytes 98312 | tf_op jit(solution)/shard_map/ppermute | solution.py:238
  58.0 2.0 %collective-permute-start.15 = (bf16[64,256]{1,0:T(8,128)(2,1)S(1)}, bf16[64,256]{1,0:T(8,128)(2,1)S(1)}, u32[]{:S(2)}, u32[]{:S(2)}) collective-permute-start(bf16[64,256]{1,0:T(8,128)(2,1)S(1)} %get-tuple-element.111), channel_id=1, source_target_pairs={{0,4},{2,6},{4,0},{6,2},{1,5},{3,7},{5,1},{7,3},{8,12},{10,14},{12... | collective-permute-start | bytes 98312 | tf_op jit(solution)/shard_map/ppermute | solution.py:238
  60.0 1.4 %collective-permute-start.14 = (bf16[64,256]{1,0:T(8,128)(2,1)S(1)}, bf16[64,256]{1,0:T(8,128)(2,1)S(1)}, u32[]{:S(2)}, u32[]{:S(2)}) collective-permute-start(bf16[64,256]{1,0:T(8,128)(2,1)S(1)} %get-tuple-element.112), channel_id=1, source_target_pairs={{0,2},{2,4},{4,6},{6,0},{1,3},{3,5},{5,7},{7,1},{8,10},{10,12},{12... | collective-permute-start | bytes 98312 | tf_op jit(solution)/shard_map/ppermute | solution.py:238
  61.5 5.7 %branch_own.1 = (f32[128,2048]{1,0:T(8,128)S(1)}, bf16[256,256]{1,0:T(8,128)(2,1)S(1)}, bf16[256,256]{1,0:T(8,128)(2,1)S(1)}, bf16[256,256]{1,0:T(8,128)(2,1)S(1)}, bf16[256,256]{1,0:T(8,128)(2,1)S(1)}) custom-call(s32[3]{0:T(128)S(1)} %pad_add_fusion.place, s32[2]{0:T(128)S(1)} %dynamic_slice.3.lengths, ...), custom_call_target="tpu_custom_call", output_to_operand_aliasing={{0}: (6, {})} | custom-call | flops 4499999744 | bytes 5000000 | tf_op jit(solution)/shard_map/branch_own/pallas_call | solution.py:326
  67.2 0.0 collective-permute-done.16
  67.2 0.0 collective-permute-done.14
  67.2 0.0 collective-permute-done.17.other
  67.2 0.6 collective-permute-start.23
  67.9 0.0 collective-permute-start.18
  67.9 2.4 %collective-permute-start.19 = (bf16[256,256]{1,0:T(8,128)(2,1)S(1)}, bf16[256,256]{1,0:T(8,128)(2,1)S(1)}, u32[]{:S(2)}, u32[]{:S(2)}) collective-permute-start(bf16[256,256]{1,0:T(8,128)(2,1)S(1)} %get-tuple-element.87), channel_id=1, source_target_pairs={{0,16},{8,24},{16,0},{24,8},{1,17},{9,25},{17,1},{25,9},{2,18},{10... | collective-permute-start | bytes 393224 | tf_op jit(solution)/shard_map/ppermute | solution.py:238
  70.3 1.2 %collective-permute-start.20 = (bf16[256,256]{1,0:T(8,128)(2,1)S(1)}, bf16[256,256]{1,0:T(8,128)(2,1)S(1)}, u32[]{:S(2)}, u32[]{:S(2)}) collective-permute-start(bf16[256,256]{1,0:T(8,128)(2,1)S(1)} %get-tuple-element.88), channel_id=1, source_target_pairs={{0,24},{8,0},{16,8},{24,16},{1,25},{9,1},{17,9},{25,17},{2,26},{10... | collective-permute-start | bytes 393224 | tf_op jit(solution)/shard_map/ppermute | solution.py:238
  71.5 2.4 %collective-permute-start.22 = (f32[64,256]{1,0:T(8,128)S(1)}, f32[64,256]{1,0:T(8,128)S(1)}, u32[]{:S(2)}, u32[]{:S(2)}) collective-permute-start(f32[64,256]{1,0:T(8,128)S(1)} %convert_add_fusion.1), channel_id=1, source_target_pairs={{0,64},{32,96},{64,0},{96,32},{1,65},{33,97},{65,1},{97,33},{2,66}... | collective-permute-start | bytes 196616 | tf_op jit(solution)/shard_map/ppermute | solution.py:238
  73.9 1.8 %collective-permute-start.21 = (f32[64,256]{1,0:T(8,128)S(1)}, f32[64,256]{1,0:T(8,128)S(1)}, u32[]{:S(2)}, u32[]{:S(2)}) collective-permute-start(f32[64,256]{1,0:T(8,128)S(1)} %convert_add_fusion.1), channel_id=1, source_target_pairs={{0,32},{32,64},{64,96},{96,0},{1,33},{33,65},{65,97},{97,1},{2,34}... | collective-permute-start | bytes 196616 | tf_op jit(solution)/shard_map/ppermute | solution.py:238
  75.7 1.5 %finish.1 = bf16[256,1024]{1,0:T(8,128)(2,1)} custom-call(bf16[256,256]{1,0:T(8,128)(2,1)S(1)} %get-tuple-element.93.onehot_ref, f32[128,2048]{1,0:T(8,128)S(1)} %get-tuple-element.94.leaf, f32[128,2048]{1,0:T(8,128)S(1)} %get-tuple-element.95.mine, f32[128,2048]{1,0:T(8,128)S(1)} %collective-permute-done.17.other), custom_call_target="tpu_custom_call" | custom-call | flops 200000000 | bytes 3000000 | tf_op jit(solution)/shard_map/finish/pallas_call | solution.py:342
  77.3 0.9 collective-permute-done.21
  78.2 0.1 add_convert_fusion
  78.3 3.2 %collective-permute-start.25 = (bf16[2,32,256]{2,1,0:T(8,128)(2,1)S(1)}, bf16[2,32,256]{2,1,0:T(8,128)(2,1)S(1)}, u32[]{:S(2)}, u32[]{:S(2)}) collective-permute-start(bf16[2,32,256]{2,1,0:T(8,128)(2,1)S(1)} %bitcast.15), channel_id=1, source_target_pairs={{0,2},{2,4},{4,6},{6,0},{1,3},{3,5},{5,7},{7,1},{8,10},{10,12},{12... | collective-permute-start | bytes 98312 | tf_op jit(solution)/shard_map/ppermute | solution.py:238
  81.5 1.0 %collective-permute-start.27 = (bf16[2,32,256]{2,1,0:T(8,128)(2,1)S(1)}, bf16[2,32,256]{2,1,0:T(8,128)(2,1)S(1)}, u32[]{:S(2)}, u32[]{:S(2)}) collective-permute-start(bf16[2,32,256]{2,1,0:T(8,128)(2,1)S(1)} %bitcast.14), channel_id=1, source_target_pairs={{0,6},{2,0},{4,2},{6,4},{1,7},{3,1},{5,3},{7,5},{8,14},{10,8},{12,... | collective-permute-start | bytes 98312 | tf_op jit(solution)/shard_map/ppermute | solution.py:238
  82.5 4.0 %collective-permute-start.26 = (bf16[2,32,256]{2,1,0:T(8,128)(2,1)S(1)}, bf16[2,32,256]{2,1,0:T(8,128)(2,1)S(1)}, u32[]{:S(2)}, u32[]{:S(2)}) collective-permute-start(bf16[2,32,256]{2,1,0:T(8,128)(2,1)S(1)} %bitcast.13), channel_id=1, source_target_pairs={{0,4},{2,6},{4,0},{6,2},{1,5},{3,7},{5,1},{7,3},{8,12},{10,14},{12... | collective-permute-start | bytes 98312 | tf_op jit(solution)/shard_map/ppermute | solution.py:238
  86.5 1.1 %collective-permute-start.24 = (f32[64,256]{1,0:T(8,128)S(1)}, f32[64,256]{1,0:T(8,128)S(1)}, u32[]{:S(2)}, u32[]{:S(2)}) collective-permute-start(f32[64,256]{1,0:T(8,128)S(1)} %add_add_fusion), channel_id=1, source_target_pairs={{0,128},{128,0},{1,129},{129,1},{2,130},{130,2},{3,131},{131,3},{4... | collective-permute-start | bytes 196616 | tf_op jit(solution)/shard_map/ppermute | solution.py:238
  87.6 0.0 collective-permute-done.25
  87.6 0.0 collective-permute-done.27
  87.6 2.9 %collective-permute-done.26 = bf16[2,32,256]{2,1,0:T(8,128)(2,1)S(1)} collective-permute-done((bf16[2,32,256]{2,1,0:T(8,128)(2,1)S(1)}, bf16[2,32,256]{2,1,0:T(8,128)(2,1)S(1)}, u32[]{:S(2)}, u32[]{:S(2)}) %collective-permute-start.26) | collective-permute-done | bytes 32800 | tf_op jit(solution)/shard_map/ppermute | solution.py:238
  90.4 0.6 convert_add_fusion
  91.1 0.6 add.65
  (25 shorter events, 0.1 us)
Async XLA Ops:
  0.6 12.2 %copy-start = (bf16[256,256]{1,0:T(8,128)(2,1)S(1)}, bf16[256,256]{1,0:T(8,128)(2,1)}, u32[]{:S(2)}) copy-start(bf16[256,256]{1,0:T(8,128)(2,1)} %leaf_ref.1) | copy-start | bytes 393220
  1.5 11.4 %copy-start.5 = (s32[1,256]{1,0:T(1,128)S(1)}, s32[1,256]{1,0:T(1,128)}, u32[]{:S(2)}) copy-start(s32[1,256]{1,0:T(1,128)} %seg_ref.1) | copy-start | bytes 3076
  1.5 11.4 %copy-start.6 = (s32[1,8]{1,0:T(1,128)S(1)}, s32[1,8]{1,0:T(1,128)}, u32[]{:S(2)}) copy-start(s32[1,8]{1,0:T(1,128)} %seg_branch.1) | copy-start | bytes 100
  1.5 17.4 %collective-permute-start.2 = (bf16[128,256]{1,0:T(8,128)(2,1)S(1)}, bf16[128,256]{1,0:T(8,128)(2,1)S(1)}, u32[]{:S(2)}, u32[]{:S(2)}) collective-permute-start(bf16[128,256]{1,0:T(8,128)(2,1)S(1)} %pad_maximum_fusion.z0), channel_id=1, source_target_pairs={{0,2},{2,4},{4,6},{6,0},{1,3},{3,5},{5,7},{7,1},{8,10},{10,12},{12... | collective-permute-start | bytes 196616 | tf_op jit(solution)/shard_map/ppermute | solution.py:238
  4.8 14.1 %collective-permute-start.1 = (bf16[128,256]{1,0:T(8,128)(2,1)S(1)}, bf16[128,256]{1,0:T(8,128)(2,1)S(1)}, u32[]{:S(2)}, u32[]{:S(2)}) collective-permute-start(bf16[128,256]{1,0:T(8,128)(2,1)S(1)} %pad_maximum_fusion.z0), channel_id=1, source_target_pairs={{0,4},{2,6},{4,0},{6,2},{1,5},{3,7},{5,1},{7,3},{8,12},{10,14},{12... | collective-permute-start | bytes 196616 | tf_op jit(solution)/shard_map/ppermute | solution.py:238
  10.2 8.7 %collective-permute-start = (bf16[128,256]{1,0:T(8,128)(2,1)S(1)}, bf16[128,256]{1,0:T(8,128)(2,1)S(1)}, u32[]{:S(2)}, u32[]{:S(2)}) collective-permute-start(bf16[128,256]{1,0:T(8,128)(2,1)S(1)} %pad_maximum_fusion.z0), channel_id=1, source_target_pairs={{0,6},{2,0},{4,2},{6,4},{1,7},{3,1},{5,3},{7,5},{8,14},{10,8},{12,... | collective-permute-start | bytes 196616 | tf_op jit(solution)/shard_map/ppermute | solution.py:238
  12.9 0.7 copy-start.4
  18.8 0.6 copy-start.1
  18.9 12.3 %collective-permute-start.6 = (bf16[4096,128]{1,0:T(8,128)(2,1)S(1)}, bf16[4096,128]{1,0:T(8,128)(2,1)S(1)}, u32[]{:S(2)}, u32[]{:S(2)}) collective-permute-start(bf16[4096,128]{1,0:T(8,128)(2,1)S(1)} %get-tuple-element.62.qg0.qg_ref), channel_id=1, source_target_pairs={{0,1},{1,0},{2,3},{3,2},{4,5},{5,4},{6,7},{7,6},{8,9},{9,8},{10,11... | collective-permute-start | bytes 3145736 | tf_op jit(solution)/shard_map/ppermute | solution.py:238
  19.5 8.1 %collective-permute-start.5 = (bf16[256,256]{1,0:T(8,128)(2,1)S(1)}, bf16[256,256]{1,0:T(8,128)(2,1)}, u32[]{:S(2)}, u32[]{:S(2)}) collective-permute-start(bf16[256,256]{1,0:T(8,128)(2,1)S(1)} %get-tuple-element.61.kv0), channel_id=1, source_target_pairs={{0,8},{8,16},{16,24},{24,0},{1,9},{9,17},{17,25},{25,1},{2,10},{10... | collective-permute-start | bytes 393224 | tf_op jit(solution)/shard_map/ppermute | solution.py:238
  21.0 10.1 %collective-permute-start.4 = (bf16[256,256]{1,0:T(8,128)(2,1)S(1)}, bf16[256,256]{1,0:T(8,128)(2,1)}, u32[]{:S(2)}, u32[]{:S(2)}) collective-permute-start(bf16[256,256]{1,0:T(8,128)(2,1)S(1)} %get-tuple-element.61.kv0), channel_id=1, source_target_pairs={{0,16},{8,24},{16,0},{24,8},{1,17},{9,25},{17,1},{25,9},{2,18},{10... | collective-permute-start | bytes 393224 | tf_op jit(solution)/shard_map/ppermute | solution.py:238
  23.9 7.2 %collective-permute-start.3 = (bf16[256,256]{1,0:T(8,128)(2,1)S(1)}, bf16[256,256]{1,0:T(8,128)(2,1)}, u32[]{:S(2)}, u32[]{:S(2)}) collective-permute-start(bf16[256,256]{1,0:T(8,128)(2,1)S(1)} %get-tuple-element.61.kv0), channel_id=1, source_target_pairs={{0,24},{8,0},{16,8},{24,16},{1,25},{9,1},{17,9},{25,17},{2,26},{10... | collective-permute-start | bytes 393224 | tf_op jit(solution)/shard_map/ppermute | solution.py:238
  25.3 1.6 %collective-permute-start.7 = (f32[4,2048]{1,0:T(4,128)}, f32[4,2048]{1,0:T(4,128)}, u32[]{:S(2)}, u32[]{:S(2)}) collective-permute-start(f32[4,2048]{1,0:T(4,128)} %copy-done.1), channel_id=1, source_target_pairs={{0,1},{1,0},{2,3},{3,2},{4,5},{5,4},{6,7},{7,6},{8,9},{9,8},{10,11... | collective-permute-start | bytes 98312 | tf_op jit(solution)/shard_map/ppermute | solution.py:238
  25.4 0.7 copy-start.7
  26.8 20.8 %collective-permute-start.13 = (bf16[256,256]{1,0:T(8,128)(2,1)S(1)}, bf16[256,256]{1,0:T(8,128)(2,1)S(1)}, u32[]{:S(2)}, u32[]{:S(2)}) collective-permute-start(bf16[256,256]{1,0:T(8,128)(2,1)S(1)} %get-tuple-element.68.kv0), channel_id=1, source_target_pairs={{0,8},{8,16},{16,24},{24,0},{1,9},{9,17},{17,25},{25,1},{2,10},{10... | collective-permute-start | bytes 393224 | tf_op jit(solution)/shard_map/ppermute | solution.py:238
  27.5 22.1 %collective-permute-start.12 = (bf16[256,256]{1,0:T(8,128)(2,1)S(1)}, bf16[256,256]{1,0:T(8,128)(2,1)S(1)}, u32[]{:S(2)}, u32[]{:S(2)}) collective-permute-start(bf16[256,256]{1,0:T(8,128)(2,1)S(1)} %get-tuple-element.68.kv0), channel_id=1, source_target_pairs={{0,16},{8,24},{16,0},{24,8},{1,17},{9,25},{17,1},{25,9},{2,18},{10... | collective-permute-start | bytes 393224 | tf_op jit(solution)/shard_map/ppermute | solution.py:238
  31.2 18.4 %collective-permute-start.11 = (bf16[256,256]{1,0:T(8,128)(2,1)S(1)}, bf16[256,256]{1,0:T(8,128)(2,1)S(1)}, u32[]{:S(2)}, u32[]{:S(2)}) collective-permute-start(bf16[256,256]{1,0:T(8,128)(2,1)S(1)} %get-tuple-element.68.kv0), channel_id=1, source_target_pairs={{0,24},{8,0},{16,8},{24,16},{1,25},{9,1},{17,9},{25,17},{2,26},{10... | collective-permute-start | bytes 393224 | tf_op jit(solution)/shard_map/ppermute | solution.py:238
  31.2 0.8 copy-start.2
  44.7 10.9 %collective-permute-start.8 = (bf16[256,256]{1,0:T(8,128)(2,1)S(1)}, bf16[256,256]{1,0:T(8,128)(2,1)S(1)}, u32[]{:S(2)}, u32[]{:S(2)}) collective-permute-start(bf16[256,256]{1,0:T(8,128)(2,1)S(1)} %get-tuple-element.65), channel_id=1, source_target_pairs={{0,8},{8,16},{16,24},{24,0},{1,9},{9,17},{17,25},{25,1},{2,10},{10... | collective-permute-start | bytes 393224 | tf_op jit(solution)/shard_map/ppermute | solution.py:238
  46.8 8.8 %collective-permute-start.9 = (bf16[256,256]{1,0:T(8,128)(2,1)S(1)}, bf16[256,256]{1,0:T(8,128)(2,1)S(1)}, u32[]{:S(2)}, u32[]{:S(2)}) collective-permute-start(bf16[256,256]{1,0:T(8,128)(2,1)S(1)} %get-tuple-element.66), channel_id=1, source_target_pairs={{0,16},{8,24},{16,0},{24,8},{1,17},{9,25},{17,1},{25,9},{2,18},{10... | collective-permute-start | bytes 393224 | tf_op jit(solution)/shard_map/ppermute | solution.py:238
  47.6 8.1 %collective-permute-start.10 = (bf16[256,256]{1,0:T(8,128)(2,1)S(1)}, bf16[256,256]{1,0:T(8,128)(2,1)S(1)}, u32[]{:S(2)}, u32[]{:S(2)}) collective-permute-start(bf16[256,256]{1,0:T(8,128)(2,1)S(1)} %get-tuple-element.67), channel_id=1, source_target_pairs={{0,24},{8,0},{16,8},{24,16},{1,25},{9,1},{17,9},{25,17},{2,26},{10... | collective-permute-start | bytes 393224 | tf_op jit(solution)/shard_map/ppermute | solution.py:238
  55.7 11.5 %collective-permute-start.17 = (f32[128,2048]{1,0:T(8,128)S(1)}, f32[128,2048]{1,0:T(8,128)S(1)}, u32[]{:S(2)}, u32[]{:S(2)}) collective-permute-start(f32[128,2048]{1,0:T(8,128)S(1)} %get-tuple-element.76), channel_id=1, source_target_pairs={{0,1},{1,0},{2,3},{3,2},{4,5},{5,4},{6,7},{7,6},{8,9},{9,8},{10,11... | collective-permute-start | bytes 3145736 | tf_op jit(solution)/shard_map/ppermute | solution.py:238
  55.9 5.6 %copy-start.3 = (f32[4,2048]{1,0:T(4,128)S(1)}, f32[4,2048]{1,0:T(4,128)}, u32[]{:S(2)}) copy-start(f32[4,2048]{1,0:T(4,128)} %copy-done.1) | copy-start | bytes 98308
  55.9 11.3 %collective-permute-start.16 = (bf16[64,256]{1,0:T(8,128)(2,1)S(1)}, bf16[64,256]{1,0:T(8,128)(2,1)S(1)}, u32[]{:S(2)}, u32[]{:S(2)}) collective-permute-start(bf16[64,256]{1,0:T(8,128)(2,1)S(1)} %get-tuple-element.110), channel_id=1, source_target_pairs={{0,6},{2,0},{4,2},{6,4},{1,7},{3,1},{5,3},{7,5},{8,14},{10,8},{12,... | collective-permute-start | bytes 98312 | tf_op jit(solution)/shard_map/ppermute | solution.py:238
  58.0 9.2 %collective-permute-start.15 = (bf16[64,256]{1,0:T(8,128)(2,1)S(1)}, bf16[64,256]{1,0:T(8,128)(2,1)S(1)}, u32[]{:S(2)}, u32[]{:S(2)}) collective-permute-start(bf16[64,256]{1,0:T(8,128)(2,1)S(1)} %get-tuple-element.111), channel_id=1, source_target_pairs={{0,4},{2,6},{4,0},{6,2},{1,5},{3,7},{5,1},{7,3},{8,12},{10,14},{12... | collective-permute-start | bytes 98312 | tf_op jit(solution)/shard_map/ppermute | solution.py:238
  60.0 7.2 %collective-permute-start.14 = (bf16[64,256]{1,0:T(8,128)(2,1)S(1)}, bf16[64,256]{1,0:T(8,128)(2,1)S(1)}, u32[]{:S(2)}, u32[]{:S(2)}) collective-permute-start(bf16[64,256]{1,0:T(8,128)(2,1)S(1)} %get-tuple-element.112), channel_id=1, source_target_pairs={{0,2},{2,4},{4,6},{6,0},{1,3},{3,5},{5,7},{7,1},{8,10},{10,12},{12... | collective-permute-start | bytes 98312 | tf_op jit(solution)/shard_map/ppermute | solution.py:238
  67.2 6.7 %collective-permute-start.23 = (f32[64,256]{1,0:T(8,128)S(1)}, f32[64,256]{1,0:T(8,128)S(1)}, u32[]{:S(2)}, u32[]{:S(2)}) collective-permute-start(f32[64,256]{1,0:T(8,128)S(1)} %convert_add_fusion.1), channel_id=1, source_target_pairs={{0,96},{32,0},{64,32},{96,64},{1,97},{33,1},{65,33},{97,65},{2,98}... | collective-permute-start | bytes 196616 | tf_op jit(solution)/shard_map/ppermute | solution.py:238
  67.9 10.3 %collective-permute-start.18 = (bf16[256,256]{1,0:T(8,128)(2,1)S(1)}, bf16[256,256]{1,0:T(8,128)(2,1)S(1)}, u32[]{:S(2)}, u32[]{:S(2)}) collective-permute-start(bf16[256,256]{1,0:T(8,128)(2,1)S(1)} %get-tuple-element.86), channel_id=1, source_target_pairs={{0,8},{8,16},{16,24},{24,0},{1,9},{9,17},{17,25},{25,1},{2,10},{10... | collective-permute-start | bytes 393224 | tf_op jit(solution)/shard_map/ppermute | solution.py:238
  67.9 10.3 %collective-permute-start.19 = (bf16[256,256]{1,0:T(8,128)(2,1)S(1)}, bf16[256,256]{1,0:T(8,128)(2,1)S(1)}, u32[]{:S(2)}, u32[]{:S(2)}) collective-permute-start(bf16[256,256]{1,0:T(8,128)(2,1)S(1)} %get-tuple-element.87), channel_id=1, source_target_pairs={{0,16},{8,24},{16,0},{24,8},{1,17},{9,25},{17,1},{25,9},{2,18},{10... | collective-permute-start | bytes 393224 | tf_op jit(solution)/shard_map/ppermute | solution.py:238
  70.3 7.9 %collective-permute-start.20 = (bf16[256,256]{1,0:T(8,128)(2,1)S(1)}, bf16[256,256]{1,0:T(8,128)(2,1)S(1)}, u32[]{:S(2)}, u32[]{:S(2)}) collective-permute-start(bf16[256,256]{1,0:T(8,128)(2,1)S(1)} %get-tuple-element.88), channel_id=1, source_target_pairs={{0,24},{8,0},{16,8},{24,16},{1,25},{9,1},{17,9},{25,17},{2,26},{10... | collective-permute-start | bytes 393224 | tf_op jit(solution)/shard_map/ppermute | solution.py:238
  71.5 5.8 %collective-permute-start.22 = (f32[64,256]{1,0:T(8,128)S(1)}, f32[64,256]{1,0:T(8,128)S(1)}, u32[]{:S(2)}, u32[]{:S(2)}) collective-permute-start(f32[64,256]{1,0:T(8,128)S(1)} %convert_add_fusion.1), channel_id=1, source_target_pairs={{0,64},{32,96},{64,0},{96,32},{1,65},{33,97},{65,1},{97,33},{2,66}... | collective-permute-start | bytes 196616 | tf_op jit(solution)/shard_map/ppermute | solution.py:238
  73.9 4.3 %collective-permute-start.21 = (f32[64,256]{1,0:T(8,128)S(1)}, f32[64,256]{1,0:T(8,128)S(1)}, u32[]{:S(2)}, u32[]{:S(2)}) collective-permute-start(f32[64,256]{1,0:T(8,128)S(1)} %convert_add_fusion.1), channel_id=1, source_target_pairs={{0,32},{32,64},{64,96},{96,0},{1,33},{33,65},{65,97},{97,1},{2,34}... | collective-permute-start | bytes 196616 | tf_op jit(solution)/shard_map/ppermute | solution.py:238
  78.3 9.3 %collective-permute-start.25 = (bf16[2,32,256]{2,1,0:T(8,128)(2,1)S(1)}, bf16[2,32,256]{2,1,0:T(8,128)(2,1)S(1)}, u32[]{:S(2)}, u32[]{:S(2)}) collective-permute-start(bf16[2,32,256]{2,1,0:T(8,128)(2,1)S(1)} %bitcast.15), channel_id=1, source_target_pairs={{0,2},{2,4},{4,6},{6,0},{1,3},{3,5},{5,7},{7,1},{8,10},{10,12},{12... | collective-permute-start | bytes 98312 | tf_op jit(solution)/shard_map/ppermute | solution.py:238
  81.5 6.1 %collective-permute-start.27 = (bf16[2,32,256]{2,1,0:T(8,128)(2,1)S(1)}, bf16[2,32,256]{2,1,0:T(8,128)(2,1)S(1)}, u32[]{:S(2)}, u32[]{:S(2)}) collective-permute-start(bf16[2,32,256]{2,1,0:T(8,128)(2,1)S(1)} %bitcast.14), channel_id=1, source_target_pairs={{0,6},{2,0},{4,2},{6,4},{1,7},{3,1},{5,3},{7,5},{8,14},{10,8},{12,... | collective-permute-start | bytes 98312 | tf_op jit(solution)/shard_map/ppermute | solution.py:238
  82.5 7.9 %collective-permute-start.26 = (bf16[2,32,256]{2,1,0:T(8,128)(2,1)S(1)}, bf16[2,32,256]{2,1,0:T(8,128)(2,1)S(1)}, u32[]{:S(2)}, u32[]{:S(2)}) collective-permute-start(bf16[2,32,256]{2,1,0:T(8,128)(2,1)S(1)} %bitcast.13), channel_id=1, source_target_pairs={{0,4},{2,6},{4,0},{6,2},{1,5},{3,7},{5,1},{7,3},{8,12},{10,14},{12... | collective-permute-start | bytes 98312 | tf_op jit(solution)/shard_map/ppermute | solution.py:238
  86.5 4.6 %collective-permute-start.24 = (f32[64,256]{1,0:T(8,128)S(1)}, f32[64,256]{1,0:T(8,128)S(1)}, u32[]{:S(2)}, u32[]{:S(2)}) collective-permute-start(f32[64,256]{1,0:T(8,128)S(1)} %add_add_fusion), channel_id=1, source_target_pairs={{0,128},{128,0},{1,129},{129,1},{2,130},{130,2},{3,131},{131,3},{4... | collective-permute-start | bytes 196616 | tf_op jit(solution)/shard_map/ppermute | solution.py:238

commit v4 on v3

--- a/solution.py
+++ b/solution.py
@@ -172,15 +172,14 @@
     sources = ((qg0, s0, dq0), (qg1, s1, dq1))
     pieces, targets = (kv0, kv1, kv2, kv3), (to0, to1, to2, to3)
     each = NZ * ROOT_SH
-    for first in range(0, NY, KB // each):
-        for i in range(KB // each):
-            kv_ref[pl.ds(i * each, each), :] = pieces[first + i][...]
-        total[...] = jnp.zeros_like(total)
-        sweep(kv_ref, sources, 0, total)
-        for i in range(KB // each):
-            at = pl.ds(i * each, each)
-            targets[first + i][:, :HD] = (total[at, :HD] * SCALE).astype(BF)
-            targets[first + i][:, HD:] = total[at, HD:].astype(BF)
+    for dy in range(NY):
+        kv_ref[pl.ds(dy * each, each), :] = pieces[dy][...]
+    total[...] = jnp.zeros_like(total)
+    sweep(kv_ref, sources, 0, total)
+    for dy in range(NY):
+        at = pl.ds(dy * each, each)
+        targets[dy][:, :HD] = (total[at, :HD] * SCALE).astype(BF)
+        targets[dy][:, HD:] = total[at, HD:].astype(BF)
 
 
 def live_slots(place, lengths, b, dy, dz):
@@ -293,7 +292,7 @@
     dq_shape = shape((HD, ROWS), F32)
 
 
-    scratch = [pltpu.VMEM((KB, 2 * HD), BF), pltpu.VMEM((KB, 2 * HD), F32)]
+    scratch = [pltpu.VMEM((2 * KB, 2 * HD), BF), pltpu.VMEM((2 * KB, 2 * HD), F32)]
 
     dq0, dq1, *root_terms = pl.pallas_call(
         root_kernel,
@@ -337,8 +336,6 @@
     root_z, other, branch_terms, dq0 = lax.optimization_barrier((root_z, other, branch_terms, dq0))
 
     branch_y = exchange(branch_terms, "y", NY)
-    root_part = added(root_z)
-    near = [shift(root_part, "x", 4, k) for k in (1, 2, 3)]
     query_grad = pl.pallas_call(
         finish_kernel,
         out_shape=shape((TOK, HEADS * HD), BF),
@@ -348,12 +345,15 @@
         cost_estimate=pl.CostEstimate(flops=200_000_000, bytes_accessed=3_000_000, transcendentals=0),
         name="finish",
     )(onehot, dq_leaf, dq0, other)
-    branch_y, near, query_grad = lax.optimization_barrier((branch_y, near, query_grad))
-
+    root_part = added(root_z)
+    pair = lax.ppermute(root_part, "x", [(0, 1), (1, 0), (2, 3), (3, 2)])
+    pair, query_grad = lax.optimization_barrier((pair, query_grad))
+    root_part = root_part + pair
+    pair = lax.ppermute(root_part, "x", [(0, 3), (3, 0), (1, 2), (2, 1)])
     branch_y = added(branch_y).astype(BF).reshape(NZ, 2, BR_SH, 2 * HD)
     branch_z = exchange([branch_y[k] for k in range(NZ)], "zh", NZ)
-    root_x = (root_part + near[1]) + (near[0] + near[2])
-    root_one = root_x + shift(root_x, "zl", 2, 1)
+    root_part = root_part + pair
+    root_one = root_part + shift(root_part, "zl", 2, 1)
     branch_one = added(branch_z)
     return query_grad, leaf_grad, root_one, branch_one
 

time: 93.6 us -> 90.8 us (0.970)
  starting transfers between devices: 49.9 us -> 47.3 us
  waiting for transfers between devices: 4.62 us -> 6.01 us
    ppermute x28 -> x25, starting transfers between devices: 49.9 us -> 45 us  [shift(): lax.ppermute(value, axis, [(i, (i + by) % size) for i in range(size)])]
    ppermute x0 -> x2, starting transfers between devices: none -> 2.21 us  [the longest x1 1.57 us: shards(): pair = lax.ppermute(root_part, 'x', [(0, 3), (3, 0), (1, 2), (2, 1)])]
    ppermute x0 -> x2, waiting for transfers between devices: none -> 2.17 us  [the longest x1 2.17 us: shards(): pair = lax.ppermute(root_part, 'x', [(0, 1), (1, 0), (2, 3), (3, 2)])]
    ppermute x28 -> x25, waiting for transfers between devices: 4.62 us -> 3.84 us  [shift(): lax.ppermute(value, axis, [(i, (i + by) % size) for i in range(size)])]
  transfers between devices with their start and end apart: 28 -> 27, of which waited for: 4 -> 5; matrix products, arithmetic and copies ran while one was open for 1% -> 1% of each run, Pallas kernels for 34% -> 34%
where the time goes in v4:
time: 90.8 us; the launch traced here: 89.8 us
  starting transfers between devices  47.3 us (52%)
  Pallas kernels  30.7 us (34%)
  waiting for transfers between devices  6.01 us (7%)
  local copies, waits for them, and re-layouts  2.67 us (3%)
  other arithmetic  2.35 us (3%)
    ppermute x25, starting transfers between devices, shift(): lax.ppermute(value, axis, [(i, (i + by) % size) for i in range(size)])  45 us
    pallas_call x1, Pallas kernels, shards(): pl.pallas_call(root_kernel, out_shape=(dq_shape, dq_shape, block, block,...  12.1 us
    pallas_call x1, Pallas kernels, shards(): pl.pallas_call(branch_other_kernel, out_shape=(dq_shape, shape((2 * KB, 2...  6.04 us
    pallas_call x1, Pallas kernels, shards(): pl.pallas_call(branch_own_kernel, out_shape=(dq_shape, block, block, bloc...  5.71 us
    pallas_call x1, Pallas kernels, shards(): pl.pallas_call(prepare_kernel, out_shape=(shape((2 * ROWS, HD), BF), shap...  5.26 us
    ppermute x25, waiting for transfers between devices, shift(): lax.ppermute(value, axis, [(i, (i + by) % size) for i in range(size)])  3.84 us
    unnamed x16, local copies, waits for them, and re-layouts  2.57 us
    ppermute x1, waiting for transfers between devices, shards(): pair = lax.ppermute(root_part, 'x', [(0, 1), (1, 0), (2, 3), (3, 2)])  2.17 us
  transfers between devices with their start and end apart: 27, of which 5 were waited for; matrix products, arithmetic and copies ran while one was open for 1% of the time, Pallas kernels for 34%

profile of v4, /device:TPU:2, one launch (start us, length us, event | category | flops | bytes accessed | tf_op | source)
XLA Modules:
  0.0 89.8 jit_solution(12328488664743461234)
XLA Ops:
  0.6 0.8 pad_maximum_fusion.z0
  1.5 3.3 %collective-permute-start.2 = (bf16[128,256]{1,0:T(8,128)(2,1)S(1)}, bf16[128,256]{1,0:T(8,128)(2,1)S(1)}, u32[]{:S(2)}, u32[]{:S(2)}) collective-permute-start(bf16[128,256]{1,0:T(8,128)(2,1)S(1)} %pad_maximum_fusion.z0), channel_id=1, source_target_pairs={{0,2},{2,4},{4,6},{6,0},{1,3},{3,5},{5,7},{7,1},{8,10},{10,12},{12... | collective-permute-start | bytes 196616 | tf_op jit(solution)/shard_map/ppermute | solution.py:237
  4.8 5.4 %collective-permute-start.1 = (bf16[128,256]{1,0:T(8,128)(2,1)S(1)}, bf16[128,256]{1,0:T(8,128)(2,1)S(1)}, u32[]{:S(2)}, u32[]{:S(2)}) collective-permute-start(bf16[128,256]{1,0:T(8,128)(2,1)S(1)} %pad_maximum_fusion.z0), channel_id=1, source_target_pairs={{0,4},{2,6},{4,0},{6,2},{1,5},{3,7},{5,1},{7,3},{8,12},{10,14},{12... | collective-permute-start | bytes 196616 | tf_op jit(solution)/shard_map/ppermute | solution.py:237
  10.2 2.7 %collective-permute-start = (bf16[128,256]{1,0:T(8,128)(2,1)S(1)}, bf16[128,256]{1,0:T(8,128)(2,1)S(1)}, u32[]{:S(2)}, u32[]{:S(2)}) collective-permute-start(bf16[128,256]{1,0:T(8,128)(2,1)S(1)} %pad_maximum_fusion.z0), channel_id=1, source_target_pairs={{0,6},{2,0},{4,2},{6,4},{1,7},{3,1},{5,3},{7,5},{8,14},{10,8},{12,... | collective-permute-start | bytes 196616 | tf_op jit(solution)/shard_map/ppermute | solution.py:237
  12.9 0.7 copy-done.4
  13.6 5.3 %prepare.1 = (bf16[4096,128]{1,0:T(8,128)(2,1)S(1)}, f32[4,2048]{1,0:T(4,128)S(1)}, bf16[256,256]{1,0:T(8,128)(2,1)S(1)}, f32[256,256]{1,0:T(8,128)}, f32[128,2048]{1,0:T(8,128)S(1)}) custom-call(s32[1,8]{1,0:T(1,128)S(1)} %copy-done.6, bf16[256,1024]{1,0:T(8,128)(2,1)} %q_hbm.1, bf16[256,1024]{1,0:T(8,128)(2,1)} %o_hbm.1, bf16[256,1024]{1,0:T(8,128)(2,1)} %g_hbm.1, ...), custom_call_target="tpu_custom_call" | custom-call | flops 4000000000 | bytes 5000000 | tf_op jit(solution)/shard_map/prepare/pallas_call | solution.py:261
  18.8 0.0 copy-start.1
  18.9 0.0 collective-permute-done.2.z3
  18.9 0.0 collective-permute-done.z1
  18.9 0.1 collective-permute-start.6
  19.0 0.4 copy-done.1
  19.5 1.6 %collective-permute-start.5 = (bf16[256,256]{1,0:T(8,128)(2,1)S(1)}, bf16[256,256]{1,0:T(8,128)(2,1)}, u32[]{:S(2)}, u32[]{:S(2)}) collective-permute-start(bf16[256,256]{1,0:T(8,128)(2,1)S(1)} %get-tuple-element.55.kv0), channel_id=1, source_target_pairs={{0,8},{8,16},{16,24},{24,0},{1,9},{9,17},{17,25},{25,1},{2,10},{10... | collective-permute-start | bytes 393224 | tf_op jit(solution)/shard_map/ppermute | solution.py:237
  21.0 2.9 %collective-permute-start.4 = (bf16[256,256]{1,0:T(8,128)(2,1)S(1)}, bf16[256,256]{1,0:T(8,128)(2,1)}, u32[]{:S(2)}, u32[]{:S(2)}) collective-permute-start(bf16[256,256]{1,0:T(8,128)(2,1)S(1)} %get-tuple-element.55.kv0), channel_id=1, source_target_pairs={{0,16},{8,24},{16,0},{24,8},{1,17},{9,25},{17,1},{25,9},{2,18},{10... | collective-permute-start | bytes 393224 | tf_op jit(solution)/shard_map/ppermute | solution.py:237
  23.9 1.3 %collective-permute-start.3 = (bf16[256,256]{1,0:T(8,128)(2,1)S(1)}, bf16[256,256]{1,0:T(8,128)(2,1)}, u32[]{:S(2)}, u32[]{:S(2)}) collective-permute-start(bf16[256,256]{1,0:T(8,128)(2,1)S(1)} %get-tuple-element.55.kv0), channel_id=1, source_target_pairs={{0,24},{8,0},{16,8},{24,16},{1,25},{9,1},{17,9},{25,17},{2,26},{10... | collective-permute-start | bytes 393224 | tf_op jit(solution)/shard_map/ppermute | solution.py:237
  25.3 0.0 collective-permute-start.7
  25.3 0.1 pad_add_fusion.place
  25.4 0.7 copy-done.7
  26.0 0.1 dynamic_slice.3.lengths
  26.1 0.7 collective-permute-done.7.s1.stat_ref
  26.8 0.7 collective-permute-start.13
  27.5 0.0 collective-permute-done.5.kv3
  27.5 3.6 %collective-permute-start.12 = (bf16[256,256]{1,0:T(8,128)(2,1)S(1)}, bf16[256,256]{1,0:T(8,128)(2,1)S(1)}, u32[]{:S(2)}, u32[]{:S(2)}) collective-permute-start(bf16[256,256]{1,0:T(8,128)(2,1)S(1)} %get-tuple-element.62.kv0), channel_id=1, source_target_pairs={{0,16},{8,24},{16,0},{24,8},{1,17},{9,25},{17,1},{25,9},{2,18},{10... | collective-permute-start | bytes 393224 | tf_op jit(solution)/shard_map/ppermute | solution.py:237
  31.1 0.1 collective-permute-done.4.kv2
  31.2 0.0 collective-permute-start.11
  31.2 0.0 collective-permute-done.3.kv1
  31.2 0.0 copy-start.2
  31.2 0.7 copy-done.2
  31.9 12.1 %root.1 = (f32[128,2048]{1,0:T(8,128)S(1)}, f32[128,2048]{1,0:T(8,128)S(1)}, bf16[256,256]{1,0:T(8,128)(2,1)S(1)}, bf16[256,256]{1,0:T(8,128)(2,1)S(1)}, bf16[25...) custom-call(bf16[256,256]{1,0:T(8,128)(2,1)S(1)} %get-tuple-element.55.kv0, ...), custom_call_target="tpu_custom_call" | custom-call | flops 10000000000 | bytes 8000000 | tf_op jit(solution)/shard_map/root/pallas_call | solution.py:297
  44.0 2.1 %collective-permute-start.8 = (bf16[256,256]{1,0:T(8,128)(2,1)S(1)}, bf16[256,256]{1,0:T(8,128)(2,1)S(1)}, u32[]{:S(2)}, u32[]{:S(2)}) collective-permute-start(bf16[256,256]{1,0:T(8,128)(2,1)S(1)} %get-tuple-element.59), channel_id=1, source_target_pairs={{0,8},{8,16},{16,24},{24,0},{1,9},{9,17},{17,25},{25,1},{2,10},{10... | collective-permute-start | bytes 393224 | tf_op jit(solution)/shard_map/ppermute | solution.py:237
  46.1 0.8 collective-permute-start.9
  46.9 2.0 %collective-permute-start.10 = (bf16[256,256]{1,0:T(8,128)(2,1)S(1)}, bf16[256,256]{1,0:T(8,128)(2,1)S(1)}, u32[]{:S(2)}, u32[]{:S(2)}) collective-permute-start(bf16[256,256]{1,0:T(8,128)(2,1)S(1)} %get-tuple-element.61), channel_id=1, source_target_pairs={{0,24},{8,0},{16,8},{24,16},{1,25},{9,1},{17,9},{25,17},{2,26},{10... | collective-permute-start | bytes 393224 | tf_op jit(solution)/shard_map/ppermute | solution.py:237
  48.9 0.0 collective-permute-done.12.kv2
  48.9 0.0 collective-permute-done.11.kv1
  48.9 6.0 %branch_other.1 = (f32[128,2048]{1,0:T(8,128)S(1)}, bf16[1024,256]{1,0:T(8,128)(2,1)S(1)}, f32[1024,256]{1,0:T(8,128)S(1)}) custom-call(s32[3]{0:T(128)S(1)} %pad_add_fusion.place, s32[2]{0:T(128)S(1)} %dynamic_slice.3.lengths, bf16[256,256]{1,0:T(8,128)(2,1)S(1)} %get-tuple-element.62.kv0, ...), custom_call_target="tpu_custom_call", output_to_operand_aliasing={{0}: (8, {})} | custom-call | flops 4499999744 | bytes 5000000 | tf_op jit(solution)/shard_map/branch_other/pallas_call | solution.py:310
  55.0 0.0 collective-permute-done.8
  55.0 0.0 collective-permute-done.9
  55.0 0.1 collective-permute-start.17
  55.1 0.1 add_convert_fusion.1
  55.2 0.0 copy-start.3
  55.2 2.1 %collective-permute-start.16 = (bf16[64,256]{1,0:T(8,128)(2,1)S(1)}, bf16[64,256]{1,0:T(8,128)(2,1)S(1)}, u32[]{:S(2)}, u32[]{:S(2)}) collective-permute-start(bf16[64,256]{1,0:T(8,128)(2,1)S(1)} %get-tuple-element.98), channel_id=1, source_target_pairs={{0,6},{2,0},{4,2},{6,4},{1,7},{3,1},{5,3},{7,5},{8,14},{10,8},{12,... | collective-permute-start | bytes 98312 | tf_op jit(solution)/shard_map/ppermute | solution.py:237
  57.3 2.0 %collective-permute-start.15 = (bf16[64,256]{1,0:T(8,128)(2,1)S(1)}, bf16[64,256]{1,0:T(8,128)(2,1)S(1)}, u32[]{:S(2)}, u32[]{:S(2)}) collective-permute-start(bf16[64,256]{1,0:T(8,128)(2,1)S(1)} %get-tuple-element.99), channel_id=1, source_target_pairs={{0,4},{2,6},{4,0},{6,2},{1,5},{3,7},{5,1},{7,3},{8,12},{10,14},{12... | collective-permute-start | bytes 98312 | tf_op jit(solution)/shard_map/ppermute | solution.py:237
  59.3 1.4 %collective-permute-start.14 = (bf16[64,256]{1,0:T(8,128)(2,1)S(1)}, bf16[64,256]{1,0:T(8,128)(2,1)S(1)}, u32[]{:S(2)}, u32[]{:S(2)}) collective-permute-start(bf16[64,256]{1,0:T(8,128)(2,1)S(1)} %get-tuple-element.100), channel_id=1, source_target_pairs={{0,2},{2,4},{4,6},{6,0},{1,3},{3,5},{5,7},{7,1},{8,10},{10,12},{12... | collective-permute-start | bytes 98312 | tf_op jit(solution)/shard_map/ppermute | solution.py:237
  60.8 5.7 %branch_own.1 = (f32[128,2048]{1,0:T(8,128)S(1)}, bf16[256,256]{1,0:T(8,128)(2,1)S(1)}, bf16[256,256]{1,0:T(8,128)(2,1)S(1)}, bf16[256,256]{1,0:T(8,128)(2,1)S(1)}, bf16[256,256]{1,0:T(8,128)(2,1)S(1)}) custom-call(s32[3]{0:T(128)S(1)} %pad_add_fusion.place, s32[2]{0:T(128)S(1)} %dynamic_slice.3.lengths, ...), custom_call_target="tpu_custom_call", output_to_operand_aliasing={{0}: (6, {})} | custom-call | flops 4499999744 | bytes 5000000 | tf_op jit(solution)/shard_map/branch_own/pallas_call | solution.py:325
  66.5 0.0 collective-permute-done.16
  66.5 0.0 collective-permute-done.17.other
  66.5 0.1 collective-permute-start.21
  66.6 2.4 %collective-permute-start.22 = (bf16[256,256]{1,0:T(8,128)(2,1)S(1)}, bf16[256,256]{1,0:T(8,128)(2,1)S(1)}, u32[]{:S(2)}, u32[]{:S(2)}) collective-permute-start(bf16[256,256]{1,0:T(8,128)(2,1)S(1)} %get-tuple-element.91), channel_id=1, source_target_pairs={{0,16},{8,24},{16,0},{24,8},{1,17},{9,25},{17,1},{25,9},{2,18},{10... | collective-permute-start | bytes 393224 | tf_op jit(solution)/shard_map/ppermute | solution.py:237
  69.0 1.2 %collective-permute-start.23 = (bf16[256,256]{1,0:T(8,128)(2,1)S(1)}, bf16[256,256]{1,0:T(8,128)(2,1)S(1)}, u32[]{:S(2)}, u32[]{:S(2)}) collective-permute-start(bf16[256,256]{1,0:T(8,128)(2,1)S(1)} %get-tuple-element.92), channel_id=1, source_target_pairs={{0,24},{8,0},{16,8},{24,16},{1,25},{9,1},{17,9},{25,17},{2,26},{10... | collective-permute-start | bytes 393224 | tf_op jit(solution)/shard_map/ppermute | solution.py:237
  70.3 0.6 collective-permute-start.18
  70.9 1.6 %finish.1 = bf16[256,1024]{1,0:T(8,128)(2,1)} custom-call(bf16[256,256]{1,0:T(8,128)(2,1)S(1)} %get-tuple-element.83.onehot_ref, f32[128,2048]{1,0:T(8,128)S(1)} %get-tuple-element.84.leaf, f32[128,2048]{1,0:T(8,128)S(1)} %get-tuple-element.85.mine, f32[128,2048]{1,0:T(8,128)S(1)} %collective-permute-done.17.other), custom_call_target="tpu_custom_call" | custom-call | flops 200000000 | bytes 3000000 | tf_op jit(solution)/shard_map/finish/pallas_call | solution.py:339
  72.5 2.2 %collective-permute-done.18 = f32[64,256]{1,0:T(8,128)S(1)} collective-permute-done((f32[64,256]{1,0:T(8,128)S(1)}, f32[64,256]{1,0:T(8,128)S(1)}, u32[]{:S(2)}, u32[]{:S(2)}) %collective-permute-start.18) | collective-permute-done | bytes 65568 | tf_op jit(solution)/shard_map/ppermute | solution.py:349
  74.6 1.6 %collective-permute-start.19 = (f32[64,256]{1,0:T(8,128)S(1)}, f32[64,256]{1,0:T(8,128)S(1)}, u32[]{:S(2)}, u32[]{:S(2)}) collective-permute-start(f32[64,256]{1,0:T(8,128)S(1)} %add.59), channel_id=1, source_target_pairs={{0,96},{96,0},{32,64},{64,32},{1,97},{97,1},{33,65},{65,33},{2,98}... | collective-permute-start | bytes 196616 | tf_op jit(solution)/shard_map/ppermute | solution.py:352
  76.2 0.0 collective-permute-done.21
  76.2 0.0 collective-permute-done.22
  76.2 0.1 collective-permute-done.23
  76.3 0.1 add_convert_fusion
  76.4 3.2 %collective-permute-start.24 = (bf16[2,32,256]{2,1,0:T(8,128)(2,1)S(1)}, bf16[2,32,256]{2,1,0:T(8,128)(2,1)S(1)}, u32[]{:S(2)}, u32[]{:S(2)}) collective-permute-start(bf16[2,32,256]{2,1,0:T(8,128)(2,1)S(1)} %bitcast.15), channel_id=1, source_target_pairs={{0,2},{2,4},{4,6},{6,0},{1,3},{3,5},{5,7},{7,1},{8,10},{10,12},{12... | collective-permute-start | bytes 98312 | tf_op jit(solution)/shard_map/ppermute | solution.py:237
  79.5 1.0 %collective-permute-start.26 = (bf16[2,32,256]{2,1,0:T(8,128)(2,1)S(1)}, bf16[2,32,256]{2,1,0:T(8,128)(2,1)S(1)}, u32[]{:S(2)}, u32[]{:S(2)}) collective-permute-start(bf16[2,32,256]{2,1,0:T(8,128)(2,1)S(1)} %bitcast.14), channel_id=1, source_target_pairs={{0,6},{2,0},{4,2},{6,4},{1,7},{3,1},{5,3},{7,5},{8,14},{10,8},{12,... | collective-permute-start | bytes 98312 | tf_op jit(solution)/shard_map/ppermute | solution.py:237
  80.6 3.9 %collective-permute-start.25 = (bf16[2,32,256]{2,1,0:T(8,128)(2,1)S(1)}, bf16[2,32,256]{2,1,0:T(8,128)(2,1)S(1)}, u32[]{:S(2)}, u32[]{:S(2)}) collective-permute-start(bf16[2,32,256]{2,1,0:T(8,128)(2,1)S(1)} %bitcast.13), channel_id=1, source_target_pairs={{0,4},{2,6},{4,0},{6,2},{1,5},{3,7},{5,1},{7,3},{8,12},{10,14},{12... | collective-permute-start | bytes 98312 | tf_op jit(solution)/shard_map/ppermute | solution.py:237
  84.5 0.0 collective-permute-done.19
  84.5 1.1 %collective-permute-start.20 = (f32[64,256]{1,0:T(8,128)S(1)}, f32[64,256]{1,0:T(8,128)S(1)}, u32[]{:S(2)}, u32[]{:S(2)}) collective-permute-start(f32[64,256]{1,0:T(8,128)S(1)} %add.60), channel_id=1, source_target_pairs={{0,128},{128,0},{1,129},{129,1},{2,130},{130,2},{3,131},{131,3},{4... | collective-permute-start | bytes 196616 | tf_op jit(solution)/shard_map/ppermute | solution.py:237
  85.6 2.9 %collective-permute-done.25 = bf16[2,32,256]{2,1,0:T(8,128)(2,1)S(1)} collective-permute-done((bf16[2,32,256]{2,1,0:T(8,128)(2,1)S(1)}, bf16[2,32,256]{2,1,0:T(8,128)(2,1)S(1)}, u32[]{:S(2)}, u32[]{:S(2)}) %collective-permute-start.25) | collective-permute-done | bytes 32800 | tf_op jit(solution)/shard_map/ppermute | solution.py:237
  88.5 0.6 convert_add_fusion
  89.2 0.6 add.61
  (24 shorter events, 0.1 us)
Async XLA Ops:
  0.6 12.2 %copy-start = (bf16[256,256]{1,0:T(8,128)(2,1)S(1)}, bf16[256,256]{1,0:T(8,128)(2,1)}, u32[]{:S(2)}) copy-start(bf16[256,256]{1,0:T(8,128)(2,1)} %leaf_ref.1) | copy-start | bytes 393220
  1.5 11.4 %copy-start.5 = (s32[1,256]{1,0:T(1,128)S(1)}, s32[1,256]{1,0:T(1,128)}, u32[]{:S(2)}) copy-start(s32[1,256]{1,0:T(1,128)} %seg_ref.1) | copy-start | bytes 3076
  1.5 11.4 %copy-start.6 = (s32[1,8]{1,0:T(1,128)S(1)}, s32[1,8]{1,0:T(1,128)}, u32[]{:S(2)}) copy-start(s32[1,8]{1,0:T(1,128)} %seg_branch.1) | copy-start | bytes 100
  1.5 17.4 %collective-permute-start.2 = (bf16[128,256]{1,0:T(8,128)(2,1)S(1)}, bf16[128,256]{1,0:T(8,128)(2,1)S(1)}, u32[]{:S(2)}, u32[]{:S(2)}) collective-permute-start(bf16[128,256]{1,0:T(8,128)(2,1)S(1)} %pad_maximum_fusion.z0), channel_id=1, source_target_pairs={{0,2},{2,4},{4,6},{6,0},{1,3},{3,5},{5,7},{7,1},{8,10},{10,12},{12... | collective-permute-start | bytes 196616 | tf_op jit(solution)/shard_map/ppermute | solution.py:237
  4.8 14.1 %collective-permute-start.1 = (bf16[128,256]{1,0:T(8,128)(2,1)S(1)}, bf16[128,256]{1,0:T(8,128)(2,1)S(1)}, u32[]{:S(2)}, u32[]{:S(2)}) collective-permute-start(bf16[128,256]{1,0:T(8,128)(2,1)S(1)} %pad_maximum_fusion.z0), channel_id=1, source_target_pairs={{0,4},{2,6},{4,0},{6,2},{1,5},{3,7},{5,1},{7,3},{8,12},{10,14},{12... | collective-permute-start | bytes 196616 | tf_op jit(solution)/shard_map/ppermute | solution.py:237
  10.2 8.7 %collective-permute-start = (bf16[128,256]{1,0:T(8,128)(2,1)S(1)}, bf16[128,256]{1,0:T(8,128)(2,1)S(1)}, u32[]{:S(2)}, u32[]{:S(2)}) collective-permute-start(bf16[128,256]{1,0:T(8,128)(2,1)S(1)} %pad_maximum_fusion.z0), channel_id=1, source_target_pairs={{0,6},{2,0},{4,2},{6,4},{1,7},{3,1},{5,3},{7,5},{8,14},{10,8},{12,... | collective-permute-start | bytes 196616 | tf_op jit(solution)/shard_map/ppermute | solution.py:237
  12.9 0.7 copy-start.4
  18.8 0.6 copy-start.1
  18.9 12.3 %collective-permute-start.6 = (bf16[4096,128]{1,0:T(8,128)(2,1)S(1)}, bf16[4096,128]{1,0:T(8,128)(2,1)S(1)}, u32[]{:S(2)}, u32[]{:S(2)}) collective-permute-start(bf16[4096,128]{1,0:T(8,128)(2,1)S(1)} %get-tuple-element.56.qg0.qg_ref), channel_id=1, source_target_pairs={{0,1},{1,0},{2,3},{3,2},{4,5},{5,4},{6,7},{7,6},{8,9},{9,8},{10,11... | collective-permute-start | bytes 3145736 | tf_op jit(solution)/shard_map/ppermute | solution.py:237
  19.5 8.1 %collective-permute-start.5 = (bf16[256,256]{1,0:T(8,128)(2,1)S(1)}, bf16[256,256]{1,0:T(8,128)(2,1)}, u32[]{:S(2)}, u32[]{:S(2)}) collective-permute-start(bf16[256,256]{1,0:T(8,128)(2,1)S(1)} %get-tuple-element.55.kv0), channel_id=1, source_target_pairs={{0,8},{8,16},{16,24},{24,0},{1,9},{9,17},{17,25},{25,1},{2,10},{10... | collective-permute-start | bytes 393224 | tf_op jit(solution)/shard_map/ppermute | solution.py:237
  21.0 10.1 %collective-permute-start.4 = (bf16[256,256]{1,0:T(8,128)(2,1)S(1)}, bf16[256,256]{1,0:T(8,128)(2,1)}, u32[]{:S(2)}, u32[]{:S(2)}) collective-permute-start(bf16[256,256]{1,0:T(8,128)(2,1)S(1)} %get-tuple-element.55.kv0), channel_id=1, source_target_pairs={{0,16},{8,24},{16,0},{24,8},{1,17},{9,25},{17,1},{25,9},{2,18},{10... | collective-permute-start | bytes 393224 | tf_op jit(solution)/shard_map/ppermute | solution.py:237
  23.9 7.2 %collective-permute-start.3 = (bf16[256,256]{1,0:T(8,128)(2,1)S(1)}, bf16[256,256]{1,0:T(8,128)(2,1)}, u32[]{:S(2)}, u32[]{:S(2)}) collective-permute-start(bf16[256,256]{1,0:T(8,128)(2,1)S(1)} %get-tuple-element.55.kv0), channel_id=1, source_target_pairs={{0,24},{8,0},{16,8},{24,16},{1,25},{9,1},{17,9},{25,17},{2,26},{10... | collective-permute-start | bytes 393224 | tf_op jit(solution)/shard_map/ppermute | solution.py:237
  25.3 1.6 %collective-permute-start.7 = (f32[4,2048]{1,0:T(4,128)}, f32[4,2048]{1,0:T(4,128)}, u32[]{:S(2)}, u32[]{:S(2)}) collective-permute-start(f32[4,2048]{1,0:T(4,128)} %copy-done.1), channel_id=1, source_target_pairs={{0,1},{1,0},{2,3},{3,2},{4,5},{5,4},{6,7},{7,6},{8,9},{9,8},{10,11... | collective-permute-start | bytes 98312 | tf_op jit(solution)/shard_map/ppermute | solution.py:237
  25.4 0.7 copy-start.7
  26.8 20.1 %collective-permute-start.13 = (bf16[256,256]{1,0:T(8,128)(2,1)S(1)}, bf16[256,256]{1,0:T(8,128)(2,1)S(1)}, u32[]{:S(2)}, u32[]{:S(2)}) collective-permute-start(bf16[256,256]{1,0:T(8,128)(2,1)S(1)} %get-tuple-element.62.kv0), channel_id=1, source_target_pairs={{0,8},{8,16},{16,24},{24,0},{1,9},{9,17},{17,25},{25,1},{2,10},{10... | collective-permute-start | bytes 393224 | tf_op jit(solution)/shard_map/ppermute | solution.py:237
  27.5 21.4 %collective-permute-start.12 = (bf16[256,256]{1,0:T(8,128)(2,1)S(1)}, bf16[256,256]{1,0:T(8,128)(2,1)S(1)}, u32[]{:S(2)}, u32[]{:S(2)}) collective-permute-start(bf16[256,256]{1,0:T(8,128)(2,1)S(1)} %get-tuple-element.62.kv0), channel_id=1, source_target_pairs={{0,16},{8,24},{16,0},{24,8},{1,17},{9,25},{17,1},{25,9},{2,18},{10... | collective-permute-start | bytes 393224 | tf_op jit(solution)/shard_map/ppermute | solution.py:237
  31.2 17.7 %collective-permute-start.11 = (bf16[256,256]{1,0:T(8,128)(2,1)S(1)}, bf16[256,256]{1,0:T(8,128)(2,1)S(1)}, u32[]{:S(2)}, u32[]{:S(2)}) collective-permute-start(bf16[256,256]{1,0:T(8,128)(2,1)S(1)} %get-tuple-element.62.kv0), channel_id=1, source_target_pairs={{0,24},{8,0},{16,8},{24,16},{1,25},{9,1},{17,9},{25,17},{2,26},{10... | collective-permute-start | bytes 393224 | tf_op jit(solution)/shard_map/ppermute | solution.py:237
  31.2 0.8 copy-start.2
  44.0 10.9 %collective-permute-start.8 = (bf16[256,256]{1,0:T(8,128)(2,1)S(1)}, bf16[256,256]{1,0:T(8,128)(2,1)S(1)}, u32[]{:S(2)}, u32[]{:S(2)}) collective-permute-start(bf16[256,256]{1,0:T(8,128)(2,1)S(1)} %get-tuple-element.59), channel_id=1, source_target_pairs={{0,8},{8,16},{16,24},{24,0},{1,9},{9,17},{17,25},{25,1},{2,10},{10... | collective-permute-start | bytes 393224 | tf_op jit(solution)/shard_map/ppermute | solution.py:237
  46.1 8.8 %collective-permute-start.9 = (bf16[256,256]{1,0:T(8,128)(2,1)S(1)}, bf16[256,256]{1,0:T(8,128)(2,1)S(1)}, u32[]{:S(2)}, u32[]{:S(2)}) collective-permute-start(bf16[256,256]{1,0:T(8,128)(2,1)S(1)} %get-tuple-element.60), channel_id=1, source_target_pairs={{0,16},{8,24},{16,0},{24,8},{1,17},{9,25},{17,1},{25,9},{2,18},{10... | collective-permute-start | bytes 393224 | tf_op jit(solution)/shard_map/ppermute | solution.py:237
  46.9 8.1 %collective-permute-start.10 = (bf16[256,256]{1,0:T(8,128)(2,1)S(1)}, bf16[256,256]{1,0:T(8,128)(2,1)S(1)}, u32[]{:S(2)}, u32[]{:S(2)}) collective-permute-start(bf16[256,256]{1,0:T(8,128)(2,1)S(1)} %get-tuple-element.61), channel_id=1, source_target_pairs={{0,24},{8,0},{16,8},{24,16},{1,25},{9,1},{17,9},{25,17},{2,26},{10... | collective-permute-start | bytes 393224 | tf_op jit(solution)/shard_map/ppermute | solution.py:237
  55.0 11.5 %collective-permute-start.17 = (f32[128,2048]{1,0:T(8,128)S(1)}, f32[128,2048]{1,0:T(8,128)S(1)}, u32[]{:S(2)}, u32[]{:S(2)}) collective-permute-start(f32[128,2048]{1,0:T(8,128)S(1)} %get-tuple-element.70), channel_id=1, source_target_pairs={{0,1},{1,0},{2,3},{3,2},{4,5},{5,4},{6,7},{7,6},{8,9},{9,8},{10,11... | collective-permute-start | bytes 3145736 | tf_op jit(solution)/shard_map/ppermute | solution.py:237
  55.2 5.6 %copy-start.3 = (f32[4,2048]{1,0:T(4,128)S(1)}, f32[4,2048]{1,0:T(4,128)}, u32[]{:S(2)}) copy-start(f32[4,2048]{1,0:T(4,128)} %copy-done.1) | copy-start | bytes 98308
  55.2 11.3 %collective-permute-start.16 = (bf16[64,256]{1,0:T(8,128)(2,1)S(1)}, bf16[64,256]{1,0:T(8,128)(2,1)S(1)}, u32[]{:S(2)}, u32[]{:S(2)}) collective-permute-start(bf16[64,256]{1,0:T(8,128)(2,1)S(1)} %get-tuple-element.98), channel_id=1, source_target_pairs={{0,6},{2,0},{4,2},{6,4},{1,7},{3,1},{5,3},{7,5},{8,14},{10,8},{12,... | collective-permute-start | bytes 98312 | tf_op jit(solution)/shard_map/ppermute | solution.py:237
  57.3 9.1 %collective-permute-start.15 = (bf16[64,256]{1,0:T(8,128)(2,1)S(1)}, bf16[64,256]{1,0:T(8,128)(2,1)S(1)}, u32[]{:S(2)}, u32[]{:S(2)}) collective-permute-start(bf16[64,256]{1,0:T(8,128)(2,1)S(1)} %get-tuple-element.99), channel_id=1, source_target_pairs={{0,4},{2,6},{4,0},{6,2},{1,5},{3,7},{5,1},{7,3},{8,12},{10,14},{12... | collective-permute-start | bytes 98312 | tf_op jit(solution)/shard_map/ppermute | solution.py:237
  59.3 7.2 %collective-permute-start.14 = (bf16[64,256]{1,0:T(8,128)(2,1)S(1)}, bf16[64,256]{1,0:T(8,128)(2,1)S(1)}, u32[]{:S(2)}, u32[]{:S(2)}) collective-permute-start(bf16[64,256]{1,0:T(8,128)(2,1)S(1)} %get-tuple-element.100), channel_id=1, source_target_pairs={{0,2},{2,4},{4,6},{6,0},{1,3},{3,5},{5,7},{7,1},{8,10},{10,12},{12... | collective-permute-start | bytes 98312 | tf_op jit(solution)/shard_map/ppermute | solution.py:237
  66.5 9.7 %collective-permute-start.21 = (bf16[256,256]{1,0:T(8,128)(2,1)S(1)}, bf16[256,256]{1,0:T(8,128)(2,1)S(1)}, u32[]{:S(2)}, u32[]{:S(2)}) collective-permute-start(bf16[256,256]{1,0:T(8,128)(2,1)S(1)} %get-tuple-element.90), channel_id=1, source_target_pairs={{0,8},{8,16},{16,24},{24,0},{1,9},{9,17},{17,25},{25,1},{2,10},{10... | collective-permute-start | bytes 393224 | tf_op jit(solution)/shard_map/ppermute | solution.py:237
  66.6 9.6 %collective-permute-start.22 = (bf16[256,256]{1,0:T(8,128)(2,1)S(1)}, bf16[256,256]{1,0:T(8,128)(2,1)S(1)}, u32[]{:S(2)}, u32[]{:S(2)}) collective-permute-start(bf16[256,256]{1,0:T(8,128)(2,1)S(1)} %get-tuple-element.91), channel_id=1, source_target_pairs={{0,16},{8,24},{16,0},{24,8},{1,17},{9,25},{17,1},{25,9},{2,18},{10... | collective-permute-start | bytes 393224 | tf_op jit(solution)/shard_map/ppermute | solution.py:237
  69.0 7.3 %collective-permute-start.23 = (bf16[256,256]{1,0:T(8,128)(2,1)S(1)}, bf16[256,256]{1,0:T(8,128)(2,1)S(1)}, u32[]{:S(2)}, u32[]{:S(2)}) collective-permute-start(bf16[256,256]{1,0:T(8,128)(2,1)S(1)} %get-tuple-element.92), channel_id=1, source_target_pairs={{0,24},{8,0},{16,8},{24,16},{1,25},{9,1},{17,9},{25,17},{2,26},{10... | collective-permute-start | bytes 393224 | tf_op jit(solution)/shard_map/ppermute | solution.py:237
  70.3 4.4 %collective-permute-start.18 = (f32[64,256]{1,0:T(8,128)S(1)}, f32[64,256]{1,0:T(8,128)S(1)}, u32[]{:S(2)}, u32[]{:S(2)}) collective-permute-start(f32[64,256]{1,0:T(8,128)S(1)} %convert_add_fusion.1), channel_id=1, source_target_pairs={{0,32},{32,0},{64,96},{96,64},{1,33},{33,1},{65,97},{97,65},{2,34}... | collective-permute-start | bytes 196616 | tf_op jit(solution)/shard_map/ppermute | solution.py:349
  74.6 9.8 %collective-permute-start.19 = (f32[64,256]{1,0:T(8,128)S(1)}, f32[64,256]{1,0:T(8,128)S(1)}, u32[]{:S(2)}, u32[]{:S(2)}) collective-permute-start(f32[64,256]{1,0:T(8,128)S(1)} %add.59), channel_id=1, source_target_pairs={{0,96},{96,0},{32,64},{64,32},{1,97},{97,1},{33,65},{65,33},{2,98}... | collective-permute-start | bytes 196616 | tf_op jit(solution)/shard_map/ppermute | solution.py:352
  76.4 9.2 %collective-permute-start.24 = (bf16[2,32,256]{2,1,0:T(8,128)(2,1)S(1)}, bf16[2,32,256]{2,1,0:T(8,128)(2,1)S(1)}, u32[]{:S(2)}, u32[]{:S(2)}) collective-permute-start(bf16[2,32,256]{2,1,0:T(8,128)(2,1)S(1)} %bitcast.15), channel_id=1, source_target_pairs={{0,2},{2,4},{4,6},{6,0},{1,3},{3,5},{5,7},{7,1},{8,10},{10,12},{12... | collective-permute-start | bytes 98312 | tf_op jit(solution)/shard_map/ppermute | solution.py:237
  79.5 6.1 %collective-permute-start.26 = (bf16[2,32,256]{2,1,0:T(8,128)(2,1)S(1)}, bf16[2,32,256]{2,1,0:T(8,128)(2,1)S(1)}, u32[]{:S(2)}, u32[]{:S(2)}) collective-permute-start(bf16[2,32,256]{2,1,0:T(8,128)(2,1)S(1)} %bitcast.14), channel_id=1, source_target_pairs={{0,6},{2,0},{4,2},{6,4},{1,7},{3,1},{5,3},{7,5},{8,14},{10,8},{12,... | collective-permute-start | bytes 98312 | tf_op jit(solution)/shard_map/ppermute | solution.py:237
  80.6 7.9 %collective-permute-start.25 = (bf16[2,32,256]{2,1,0:T(8,128)(2,1)S(1)}, bf16[2,32,256]{2,1,0:T(8,128)(2,1)S(1)}, u32[]{:S(2)}, u32[]{:S(2)}) collective-permute-start(bf16[2,32,256]{2,1,0:T(8,128)(2,1)S(1)} %bitcast.13), channel_id=1, source_target_pairs={{0,4},{2,6},{4,0},{6,2},{1,5},{3,7},{5,1},{7,3},{8,12},{10,14},{12... | collective-permute-start | bytes 98312 | tf_op jit(solution)/shard_map/ppermute | solution.py:237
  84.5 4.7 %collective-permute-start.20 = (f32[64,256]{1,0:T(8,128)S(1)}, f32[64,256]{1,0:T(8,128)S(1)}, u32[]{:S(2)}, u32[]{:S(2)}) collective-permute-start(f32[64,256]{1,0:T(8,128)S(1)} %add.60), channel_id=1, source_target_pairs={{0,128},{128,0},{1,129},{129,1},{2,130},{130,2},{3,131},{131,3},{4... | collective-permute-start | bytes 196616 | tf_op jit(solution)/shard_map/ppermute | solution.py:237

commit v5 on v4

--- a/solution.py
+++ b/solution.py
@@ -186,7 +186,7 @@
     y = lax.rem(place[0] + dy, NY)
     z = lax.rem(place[1] + dz, NZ)
     start = ((y * NZ + z) * 2 + place[2]) * BR_SH
-    return lax.broadcasted_iota(jnp.int32, (BR_SH, 1), 0) + start < lengths[b]
+    return lax.broadcasted_iota(jnp.int32, (BR_SH, 1), 0) + start < lengths[place[3] + b]
 
 
 def branch_other_kernel(place, lengths, kv0, kv1, kv2, kv3, qg_ref, stat_ref, dq_in, dq_ref, kv_ref, total):
@@ -242,7 +242,7 @@
 
 
 def exchange(blocks, axis, size):
-    return [blocks[0]] + [shift(blocks[k], axis, size, k) for k in range(1, size)]
+    return [blocks[0]] + [shift(blocks[k], axis, size, k) for k in (2, 1, 3)]
 
 
 def added(terms):
@@ -252,9 +252,8 @@
 def shards(
     queries, attn_out, out_grad, log_norm, leaf_kv, root_kv, branch_kv, branch_len, segment_ids, segment_branch
 ):
-    row_index = lax.axis_index("zl") * 4 + lax.axis_index("x")
-    lengths = lax.dynamic_slice_in_dim(branch_len, row_index * 2, 2, 0)
-    place = jnp.stack([lax.axis_index("y"), lax.axis_index("zh"), lax.axis_index("c")]).astype(jnp.int32)
+    first_branch = (lax.axis_index("zl") * 4 + lax.axis_index("x")) * 2
+    place = jnp.stack([lax.axis_index("y"), lax.axis_index("zh"), lax.axis_index("c"), first_branch]).astype(jnp.int32)
 
     shard = jnp.concatenate([root_kv, branch_kv.reshape(2 * BR_SH, 2 * HD)], axis=0)
     block = shape((NZ * ROOT_SH, 2 * HD), BF)
@@ -316,7 +315,7 @@
         compiler_params=PARAMS,
         cost_estimate=branch_cost,
         name="branch_other",
-    )(place, lengths, *branches, qg1, s1, dq1)
+    )(place, branch_len, *branches, qg1, s1, dq1)
     root_y, dq1, branch_total = lax.optimization_barrier((root_y, dq1, branch_total))
     other = shift(dq1, "c", 2, 1)
     root_y = added(root_y).astype(BF).reshape(NZ, ROOT_SH, 2 * HD)
@@ -332,7 +331,7 @@
         compiler_params=PARAMS,
         cost_estimate=branch_cost,
         name="branch_own",
-    )(place, lengths, branch_kv_all, branch_total, qg0, s0, dq0)
+    )(place, branch_len, branch_kv_all, branch_total, qg0, s0, dq0)
     root_z, other, branch_terms, dq0 = lax.optimization_barrier((root_z, other, branch_terms, dq0))
 
     branch_y = exchange(branch_terms, "y", NY)

time: 90.8 us -> 91.8 us (1.011)
  waiting for transfers between devices: 6.01 us -> 8.82 us
    ppermute x25, waiting for transfers between devices: 3.84 us -> 6.14 us  [shift(): lax.ppermute(value, axis, [(i, (i + by) % size) for i in range(size)])]
  transfers between devices with their start and end apart: 27 -> 27, of which waited for: 5 -> 6; matrix products, arithmetic and copies ran while one was open for 1% -> 1% of each run, Pallas kernels for 34% -> 33%
where the time goes in v5:
time: 91.8 us; the launch traced here: 91.5 us
  starting transfers between devices  47 us (51%)
  Pallas kernels  30.5 us (33%)
  waiting for transfers between devices  8.82 us (10%)
  other arithmetic  2.36 us (3%)
  local copies, waits for them, and re-layouts  1.94 us (2%)
    ppermute x25, starting transfers between devices, shift(): lax.ppermute(value, axis, [(i, (i + by) % size) for i in range(size)])  45.3 us
    pallas_call x1, Pallas kernels, shards(): pl.pallas_call(root_kernel, out_shape=(dq_shape, dq_shape, block, block,...  12.1 us
    ppermute x25, waiting for transfers between devices, shift(): lax.ppermute(value, axis, [(i, (i + by) % size) for i in range(size)])  6.14 us
    pallas_call x1, Pallas kernels, shards(): pl.pallas_call(branch_other_kernel, out_shape=(dq_shape, shape((2 * KB, 2...  5.81 us
    pallas_call x1, Pallas kernels, shards(): pl.pallas_call(branch_own_kernel, out_shape=(dq_shape, block, block, bloc...  5.74 us
    pallas_call x1, Pallas kernels, shards(): pl.pallas_call(prepare_kernel, out_shape=(shape((2 * ROWS, HD), BF), shap...  5.26 us
    ppermute x1, waiting for transfers between devices, shards(): pair = lax.ppermute(root_part, 'x', [(0, 1), (1, 0), (2, 3), (3, 2)])  2.68 us
    unnamed x16, local copies, waits for them, and re-layouts  1.92 us
  transfers between devices with their start and end apart: 27, of which 6 were waited for; matrix products, arithmetic and copies ran while one was open for 1% of the time, Pallas kernels for 33%

profile of v5, /device:TPU:2, one launch (start us, length us, event | category | flops | bytes accessed | tf_op | source)
XLA Modules:
  0.0 91.5 jit_solution(5043279454803021151)
XLA Ops:
  0.6 0.8 pad_maximum_fusion.z0
  1.5 3.3 %collective-permute-start.2 = (bf16[128,256]{1,0:T(8,128)(2,1)S(1)}, bf16[128,256]{1,0:T(8,128)(2,1)S(1)}, u32[]{:S(2)}, u32[]{:S(2)}) collective-permute-start(bf16[128,256]{1,0:T(8,128)(2,1)S(1)} %pad_maximum_fusion.z0), channel_id=1, source_target_pairs={{0,2},{2,4},{4,6},{6,0},{1,3},{3,5},{5,7},{7,1},{8,10},{10,12},{12... | collective-permute-start | bytes 196616 | tf_op jit(solution)/shard_map/ppermute | solution.py:237
  4.8 5.4 %collective-permute-start.1 = (bf16[128,256]{1,0:T(8,128)(2,1)S(1)}, bf16[128,256]{1,0:T(8,128)(2,1)S(1)}, u32[]{:S(2)}, u32[]{:S(2)}) collective-permute-start(bf16[128,256]{1,0:T(8,128)(2,1)S(1)} %pad_maximum_fusion.z0), channel_id=1, source_target_pairs={{0,4},{2,6},{4,0},{6,2},{1,5},{3,7},{5,1},{7,3},{8,12},{10,14},{12... | collective-permute-start | bytes 196616 | tf_op jit(solution)/shard_map/ppermute | solution.py:237
  10.2 2.7 %collective-permute-start = (bf16[128,256]{1,0:T(8,128)(2,1)S(1)}, bf16[128,256]{1,0:T(8,128)(2,1)S(1)}, u32[]{:S(2)}, u32[]{:S(2)}) collective-permute-start(bf16[128,256]{1,0:T(8,128)(2,1)S(1)} %pad_maximum_fusion.z0), channel_id=1, source_target_pairs={{0,6},{2,0},{4,2},{6,4},{1,7},{3,1},{5,3},{7,5},{8,14},{10,8},{12,... | collective-permute-start | bytes 196616 | tf_op jit(solution)/shard_map/ppermute | solution.py:237
  12.9 0.7 copy-done.4
  13.6 5.3 %prepare.1 = (bf16[4096,128]{1,0:T(8,128)(2,1)S(1)}, f32[4,2048]{1,0:T(4,128)S(1)}, bf16[256,256]{1,0:T(8,128)(2,1)S(1)}, f32[256,256]{1,0:T(8,128)}, f32[128,2048]{1,0:T(8,128)S(1)}) custom-call(s32[1,8]{1,0:T(1,128)S(1)} %copy-done.6, bf16[256,1024]{1,0:T(8,128)(2,1)} %q_hbm.1, bf16[256,1024]{1,0:T(8,128)(2,1)} %o_hbm.1, bf16[256,1024]{1,0:T(8,128)(2,1)} %g_hbm.1, ...), custom_call_target="tpu_custom_call" | custom-call | flops 4000000000 | bytes 5000000 | tf_op jit(solution)/shard_map/prepare/pallas_call | solution.py:260
  18.8 0.0 copy-start.1
  18.9 0.0 collective-permute-done.2.z3
  18.9 0.0 collective-permute-done.1.z2
  18.9 0.0 collective-permute-done.z1
  18.9 0.1 collective-permute-start.6
  19.0 0.4 copy-done.1
  19.5 1.6 %collective-permute-start.5 = (bf16[256,256]{1,0:T(8,128)(2,1)S(1)}, bf16[256,256]{1,0:T(8,128)(2,1)}, u32[]{:S(2)}, u32[]{:S(2)}) collective-permute-start(bf16[256,256]{1,0:T(8,128)(2,1)S(1)} %get-tuple-element.55.kv0), channel_id=1, source_target_pairs={{0,8},{8,16},{16,24},{24,0},{1,9},{9,17},{17,25},{25,1},{2,10},{10... | collective-permute-start | bytes 393224 | tf_op jit(solution)/shard_map/ppermute | solution.py:237
  21.0 2.9 %collective-permute-start.4 = (bf16[256,256]{1,0:T(8,128)(2,1)S(1)}, bf16[256,256]{1,0:T(8,128)(2,1)}, u32[]{:S(2)}, u32[]{:S(2)}) collective-permute-start(bf16[256,256]{1,0:T(8,128)(2,1)S(1)} %get-tuple-element.55.kv0), channel_id=1, source_target_pairs={{0,16},{8,24},{16,0},{24,8},{1,17},{9,25},{17,1},{25,9},{2,18},{10... | collective-permute-start | bytes 393224 | tf_op jit(solution)/shard_map/ppermute | solution.py:237
  23.9 1.3 %collective-permute-start.3 = (bf16[256,256]{1,0:T(8,128)(2,1)S(1)}, bf16[256,256]{1,0:T(8,128)(2,1)}, u32[]{:S(2)}, u32[]{:S(2)}) collective-permute-start(bf16[256,256]{1,0:T(8,128)(2,1)S(1)} %get-tuple-element.55.kv0), channel_id=1, source_target_pairs={{0,24},{8,0},{16,8},{24,16},{1,25},{9,1},{17,9},{25,17},{2,26},{10... | collective-permute-start | bytes 393224 | tf_op jit(solution)/shard_map/ppermute | solution.py:237
  25.3 0.0 collective-permute-start.7
  25.3 0.1 pad_add_fusion.place
  25.4 1.3 %collective-permute-done.7.s1.stat_ref = f32[4,2048]{1,0:T(4,128)S(1)} collective-permute-done((f32[4,2048]{1,0:T(4,128)}, f32[4,2048]{1,0:T(4,128)S(1)}, u32[]{:S(2)}, u32[]{:S(2)}) %collective-permute-start.7) | collective-permute-done | bytes 32800 | tf_op jit(solution)/shard_map/ppermute | solution.py:237
  26.7 0.7 collective-permute-start.13
  27.4 0.0 collective-permute-done.5.kv3
  27.4 3.7 %collective-permute-start.12 = (bf16[256,256]{1,0:T(8,128)(2,1)S(1)}, bf16[256,256]{1,0:T(8,128)(2,1)S(1)}, u32[]{:S(2)}, u32[]{:S(2)}) collective-permute-start(bf16[256,256]{1,0:T(8,128)(2,1)S(1)} %get-tuple-element.62.kv0), channel_id=1, source_target_pairs={{0,16},{8,24},{16,0},{24,8},{1,17},{9,25},{17,1},{25,9},{2,18},{10... | collective-permute-start | bytes 393224 | tf_op jit(solution)/shard_map/ppermute | solution.py:237
  31.1 0.1 collective-permute-done.4.kv2
  31.2 0.0 collective-permute-start.11
  31.2 0.0 copy-start.2
  31.2 0.7 copy-done.2
  31.9 12.1 %root.1 = (f32[128,2048]{1,0:T(8,128)S(1)}, f32[128,2048]{1,0:T(8,128)S(1)}, bf16[256,256]{1,0:T(8,128)(2,1)S(1)}, bf16[256,256]{1,0:T(8,128)(2,1)S(1)}, bf16[25...) custom-call(bf16[256,256]{1,0:T(8,128)(2,1)S(1)} %get-tuple-element.55.kv0, ...), custom_call_target="tpu_custom_call" | custom-call | flops 10000000000 | bytes 8000000 | tf_op jit(solution)/shard_map/root/pallas_call | solution.py:296
  44.1 2.4 %collective-permute-start.8 = (bf16[256,256]{1,0:T(8,128)(2,1)S(1)}, bf16[256,256]{1,0:T(8,128)(2,1)S(1)}, u32[]{:S(2)}, u32[]{:S(2)}) collective-permute-start(bf16[256,256]{1,0:T(8,128)(2,1)S(1)} %get-tuple-element.59), channel_id=1, source_target_pairs={{0,16},{8,24},{16,0},{24,8},{1,17},{9,25},{17,1},{25,9},{2,18},{10... | collective-permute-start | bytes 393224 | tf_op jit(solution)/shard_map/ppermute | solution.py:237
  46.4 0.0 collective-permute-start.9
  46.4 0.0 collective-permute-done.13.kv3
  46.5 3.2 %collective-permute-start.10 = (bf16[256,256]{1,0:T(8,128)(2,1)S(1)}, bf16[256,256]{1,0:T(8,128)(2,1)S(1)}, u32[]{:S(2)}, u32[]{:S(2)}) collective-permute-start(bf16[256,256]{1,0:T(8,128)(2,1)S(1)} %get-tuple-element.61), channel_id=1, source_target_pairs={{0,24},{8,0},{16,8},{24,16},{1,25},{9,1},{17,9},{25,17},{2,26},{10... | collective-permute-start | bytes 393224 | tf_op jit(solution)/shard_map/ppermute | solution.py:237
  49.7 0.0 collective-permute-done.12.kv2
  49.7 0.0 collective-permute-done.11.kv1
  49.7 5.8 %branch_other.1 = (f32[128,2048]{1,0:T(8,128)S(1)}, bf16[1024,256]{1,0:T(8,128)(2,1)S(1)}, f32[1024,256]{1,0:T(8,128)S(1)}) custom-call(s32[4]{0:T(128)S(1)} %pad_add_fusion.place, s32[16]{0:T(128)S(1)} %copy-done.7, bf16[256,256]{1,0:T(8,128)(2,1)S(1)} %get-tuple-element.62.kv0, ...), custom_call_target="tpu_custom_call", output_to_operand_aliasing={{0}: (8, {})} | custom-call | flops 4499999744 | bytes 5000000 | tf_op jit(solution)/shard_map/branch_other/pallas_call | solution.py:309
  55.5 0.0 collective-permute-done.9
  55.5 0.0 collective-permute-done.10
  55.5 0.1 collective-permute-start.17
  55.6 0.1 add_convert_fusion.1
  55.7 0.0 copy-start.3
  55.8 2.0 %collective-permute-start.16 = (bf16[64,256]{1,0:T(8,128)(2,1)S(1)}, bf16[64,256]{1,0:T(8,128)(2,1)S(1)}, u32[]{:S(2)}, u32[]{:S(2)}) collective-permute-start(bf16[64,256]{1,0:T(8,128)(2,1)S(1)} %get-tuple-element.98), channel_id=1, source_target_pairs={{0,6},{2,0},{4,2},{6,4},{1,7},{3,1},{5,3},{7,5},{8,14},{10,8},{12,... | collective-permute-start | bytes 98312 | tf_op jit(solution)/shard_map/ppermute | solution.py:237
  57.8 1.2 %collective-permute-start.15 = (bf16[64,256]{1,0:T(8,128)(2,1)S(1)}, bf16[64,256]{1,0:T(8,128)(2,1)S(1)}, u32[]{:S(2)}, u32[]{:S(2)}) collective-permute-start(bf16[64,256]{1,0:T(8,128)(2,1)S(1)} %get-tuple-element.99), channel_id=1, source_target_pairs={{0,2},{2,4},{4,6},{6,0},{1,3},{3,5},{5,7},{7,1},{8,10},{10,12},{12... | collective-permute-start | bytes 98312 | tf_op jit(solution)/shard_map/ppermute | solution.py:237
  59.0 2.2 %collective-permute-start.14 = (bf16[64,256]{1,0:T(8,128)(2,1)S(1)}, bf16[64,256]{1,0:T(8,128)(2,1)S(1)}, u32[]{:S(2)}, u32[]{:S(2)}) collective-permute-start(bf16[64,256]{1,0:T(8,128)(2,1)S(1)} %get-tuple-element.100), channel_id=1, source_target_pairs={{0,4},{2,6},{4,0},{6,2},{1,5},{3,7},{5,1},{7,3},{8,12},{10,14},{12... | collective-permute-start | bytes 98312 | tf_op jit(solution)/shard_map/ppermute | solution.py:237
  61.2 5.7 %branch_own.1 = (f32[128,2048]{1,0:T(8,128)S(1)}, bf16[256,256]{1,0:T(8,128)(2,1)S(1)}, bf16[256,256]{1,0:T(8,128)(2,1)S(1)}, bf16[256,256]{1,0:T(8,128)(2,1)S(1)}, bf16[256,256]{1,0:T(8,128)(2,1)S(1)}) custom-call(s32[4]{0:T(128)S(1)} %pad_add_fusion.place, s32[16]{0:T(128)S(1)} %copy-done.7, ...), custom_call_target="tpu_custom_call", output_to_operand_aliasing={{0}: (6, {})} | custom-call | flops 4499999744 | bytes 5000000 | tf_op jit(solution)/shard_map/branch_own/pallas_call | solution.py:324
  67.0 0.0 collective-permute-done.15
  67.0 0.0 collective-permute-done.14
  67.0 1.1 %collective-permute-start.21 = (bf16[256,256]{1,0:T(8,128)(2,1)S(1)}, bf16[256,256]{1,0:T(8,128)(2,1)S(1)}, u32[]{:S(2)}, u32[]{:S(2)}) collective-permute-start(bf16[256,256]{1,0:T(8,128)(2,1)S(1)} %get-tuple-element.90), channel_id=1, source_target_pairs={{0,16},{8,24},{16,0},{24,8},{1,17},{9,25},{17,1},{25,9},{2,18},{10... | collective-permute-start | bytes 393224 | tf_op jit(solution)/shard_map/ppermute | solution.py:237
  68.1 0.8 collective-permute-start.22
  68.9 2.5 %collective-permute-start.23 = (bf16[256,256]{1,0:T(8,128)(2,1)S(1)}, bf16[256,256]{1,0:T(8,128)(2,1)S(1)}, u32[]{:S(2)}, u32[]{:S(2)}) collective-permute-start(bf16[256,256]{1,0:T(8,128)(2,1)S(1)} %get-tuple-element.92), channel_id=1, source_target_pairs={{0,24},{8,0},{16,8},{24,16},{1,25},{9,1},{17,9},{25,17},{2,26},{10... | collective-permute-start | bytes 393224 | tf_op jit(solution)/shard_map/ppermute | solution.py:237
  71.4 0.1 collective-permute-start.18
  71.5 1.6 %finish.1 = bf16[256,1024]{1,0:T(8,128)(2,1)} custom-call(bf16[256,256]{1,0:T(8,128)(2,1)S(1)} %get-tuple-element.83.onehot_ref, f32[128,2048]{1,0:T(8,128)S(1)} %get-tuple-element.84.leaf, f32[128,2048]{1,0:T(8,128)S(1)} %get-tuple-element.85.mine, f32[128,2048]{1,0:T(8,128)S(1)} %collective-permute-done.17.other), custom_call_target="tpu_custom_call" | custom-call | flops 200000000 | bytes 3000000 | tf_op jit(solution)/shard_map/finish/pallas_call | solution.py:338
  73.1 2.7 %collective-permute-done.18 = f32[64,256]{1,0:T(8,128)S(1)} collective-permute-done((f32[64,256]{1,0:T(8,128)S(1)}, f32[64,256]{1,0:T(8,128)S(1)}, u32[]{:S(2)}, u32[]{:S(2)}) %collective-permute-start.18) | collective-permute-done | bytes 65568 | tf_op jit(solution)/shard_map/ppermute | solution.py:348
  75.8 1.6 %collective-permute-start.19 = (f32[64,256]{1,0:T(8,128)S(1)}, f32[64,256]{1,0:T(8,128)S(1)}, u32[]{:S(2)}, u32[]{:S(2)}) collective-permute-start(f32[64,256]{1,0:T(8,128)S(1)} %add.55), channel_id=1, source_target_pairs={{0,96},{96,0},{32,64},{64,32},{1,97},{97,1},{33,65},{65,33},{2,98}... | collective-permute-start | bytes 196616 | tf_op jit(solution)/shard_map/ppermute | solution.py:351
  77.3 0.0 collective-permute-done.23
  77.3 0.1 add_convert_fusion
  77.4 4.0 %collective-permute-start.24 = (bf16[2,32,256]{2,1,0:T(8,128)(2,1)S(1)}, bf16[2,32,256]{2,1,0:T(8,128)(2,1)S(1)}, u32[]{:S(2)}, u32[]{:S(2)}) collective-permute-start(bf16[2,32,256]{2,1,0:T(8,128)(2,1)S(1)} %bitcast.16), channel_id=1, source_target_pairs={{0,4},{2,6},{4,0},{6,2},{1,5},{3,7},{5,1},{7,3},{8,12},{10,14},{12... | collective-permute-start | bytes 98312 | tf_op jit(solution)/shard_map/ppermute | solution.py:237
  81.5 2.7 %collective-permute-start.26 = (bf16[2,32,256]{2,1,0:T(8,128)(2,1)S(1)}, bf16[2,32,256]{2,1,0:T(8,128)(2,1)S(1)}, u32[]{:S(2)}, u32[]{:S(2)}) collective-permute-start(bf16[2,32,256]{2,1,0:T(8,128)(2,1)S(1)} %bitcast.15), channel_id=1, source_target_pairs={{0,6},{2,0},{4,2},{6,4},{1,7},{3,1},{5,3},{7,5},{8,14},{10,8},{12,... | collective-permute-start | bytes 98312 | tf_op jit(solution)/shard_map/ppermute | solution.py:237
  84.2 0.2 collective-permute-start.25
  84.4 0.0 collective-permute-done.19
  84.4 1.1 %collective-permute-start.20 = (f32[64,256]{1,0:T(8,128)S(1)}, f32[64,256]{1,0:T(8,128)S(1)}, u32[]{:S(2)}, u32[]{:S(2)}) collective-permute-start(f32[64,256]{1,0:T(8,128)S(1)} %add.56), channel_id=1, source_target_pairs={{0,128},{128,0},{1,129},{129,1},{2,130},{130,2},{3,131},{131,3},{4... | collective-permute-start | bytes 196616 | tf_op jit(solution)/shard_map/ppermute | solution.py:237
  85.5 0.3 collective-permute-done.24
  85.8 1.1 %collective-permute-done.26 = bf16[2,32,256]{2,1,0:T(8,128)(2,1)S(1)} collective-permute-done((bf16[2,32,256]{2,1,0:T(8,128)(2,1)S(1)}, bf16[2,32,256]{2,1,0:T(8,128)(2,1)S(1)}, u32[]{:S(2)}, u32[]{:S(2)}) %collective-permute-start.26) | collective-permute-done | bytes 32800 | tf_op jit(solution)/shard_map/ppermute | solution.py:237
  86.9 3.3 %collective-permute-done.25 = bf16[2,32,256]{2,1,0:T(8,128)(2,1)S(1)} collective-permute-done((bf16[2,32,256]{2,1,0:T(8,128)(2,1)S(1)}, bf16[2,32,256]{2,1,0:T(8,128)(2,1)S(1)}, u32[]{:S(2)}, u32[]{:S(2)}) %collective-permute-start.25) | collective-permute-done | bytes 32800 | tf_op jit(solution)/shard_map/ppermute | solution.py:237
  90.2 0.6 convert_add_fusion
  90.9 0.0 collective-permute-done.20
  90.9 0.6 add.57
  (23 shorter events, 0.1 us)
Async XLA Ops:
  0.6 12.2 %copy-start = (bf16[256,256]{1,0:T(8,128)(2,1)S(1)}, bf16[256,256]{1,0:T(8,128)(2,1)}, u32[]{:S(2)}) copy-start(bf16[256,256]{1,0:T(8,128)(2,1)} %leaf_ref.1) | copy-start | bytes 393220
  1.5 11.4 %copy-start.5 = (s32[1,256]{1,0:T(1,128)S(1)}, s32[1,256]{1,0:T(1,128)}, u32[]{:S(2)}) copy-start(s32[1,256]{1,0:T(1,128)} %seg_ref.1) | copy-start | bytes 3076
  1.5 11.4 %copy-start.6 = (s32[1,8]{1,0:T(1,128)S(1)}, s32[1,8]{1,0:T(1,128)}, u32[]{:S(2)}) copy-start(s32[1,8]{1,0:T(1,128)} %seg_branch.1) | copy-start | bytes 100
  1.5 17.4 %collective-permute-start.2 = (bf16[128,256]{1,0:T(8,128)(2,1)S(1)}, bf16[128,256]{1,0:T(8,128)(2,1)S(1)}, u32[]{:S(2)}, u32[]{:S(2)}) collective-permute-start(bf16[128,256]{1,0:T(8,128)(2,1)S(1)} %pad_maximum_fusion.z0), channel_id=1, source_target_pairs={{0,2},{2,4},{4,6},{6,0},{1,3},{3,5},{5,7},{7,1},{8,10},{10,12},{12... | collective-permute-start | bytes 196616 | tf_op jit(solution)/shard_map/ppermute | solution.py:237
  4.8 14.1 %collective-permute-start.1 = (bf16[128,256]{1,0:T(8,128)(2,1)S(1)}, bf16[128,256]{1,0:T(8,128)(2,1)S(1)}, u32[]{:S(2)}, u32[]{:S(2)}) collective-permute-start(bf16[128,256]{1,0:T(8,128)(2,1)S(1)} %pad_maximum_fusion.z0), channel_id=1, source_target_pairs={{0,4},{2,6},{4,0},{6,2},{1,5},{3,7},{5,1},{7,3},{8,12},{10,14},{12... | collective-permute-start | bytes 196616 | tf_op jit(solution)/shard_map/ppermute | solution.py:237
  10.2 8.7 %collective-permute-start = (bf16[128,256]{1,0:T(8,128)(2,1)S(1)}, bf16[128,256]{1,0:T(8,128)(2,1)S(1)}, u32[]{:S(2)}, u32[]{:S(2)}) collective-permute-start(bf16[128,256]{1,0:T(8,128)(2,1)S(1)} %pad_maximum_fusion.z0), channel_id=1, source_target_pairs={{0,6},{2,0},{4,2},{6,4},{1,7},{3,1},{5,3},{7,5},{8,14},{10,8},{12,... | collective-permute-start | bytes 196616 | tf_op jit(solution)/shard_map/ppermute | solution.py:237
  12.9 0.7 copy-start.4
  18.8 0.6 copy-start.1
  18.9 12.3 %collective-permute-start.6 = (bf16[4096,128]{1,0:T(8,128)(2,1)S(1)}, bf16[4096,128]{1,0:T(8,128)(2,1)S(1)}, u32[]{:S(2)}, u32[]{:S(2)}) collective-permute-start(bf16[4096,128]{1,0:T(8,128)(2,1)S(1)} %get-tuple-element.56.qg0.qg_ref), channel_id=1, source_target_pairs={{0,1},{1,0},{2,3},{3,2},{4,5},{5,4},{6,7},{7,6},{8,9},{9,8},{10,11... | collective-permute-start | bytes 3145736 | tf_op jit(solution)/shard_map/ppermute | solution.py:237
  19.5 7.9 %collective-permute-start.5 = (bf16[256,256]{1,0:T(8,128)(2,1)S(1)}, bf16[256,256]{1,0:T(8,128)(2,1)}, u32[]{:S(2)}, u32[]{:S(2)}) collective-permute-start(bf16[256,256]{1,0:T(8,128)(2,1)S(1)} %get-tuple-element.55.kv0), channel_id=1, source_target_pairs={{0,8},{8,16},{16,24},{24,0},{1,9},{9,17},{17,25},{25,1},{2,10},{10... | collective-permute-start | bytes 393224 | tf_op jit(solution)/shard_map/ppermute | solution.py:237
  21.0 10.1 %collective-permute-start.4 = (bf16[256,256]{1,0:T(8,128)(2,1)S(1)}, bf16[256,256]{1,0:T(8,128)(2,1)}, u32[]{:S(2)}, u32[]{:S(2)}) collective-permute-start(bf16[256,256]{1,0:T(8,128)(2,1)S(1)} %get-tuple-element.55.kv0), channel_id=1, source_target_pairs={{0,16},{8,24},{16,0},{24,8},{1,17},{9,25},{17,1},{25,9},{2,18},{10... | collective-permute-start | bytes 393224 | tf_op jit(solution)/shard_map/ppermute | solution.py:237
  23.9 7.2 %collective-permute-start.3 = (bf16[256,256]{1,0:T(8,128)(2,1)S(1)}, bf16[256,256]{1,0:T(8,128)(2,1)}, u32[]{:S(2)}, u32[]{:S(2)}) collective-permute-start(bf16[256,256]{1,0:T(8,128)(2,1)S(1)} %get-tuple-element.55.kv0), channel_id=1, source_target_pairs={{0,24},{8,0},{16,8},{24,16},{1,25},{9,1},{17,9},{25,17},{2,26},{10... | collective-permute-start | bytes 393224 | tf_op jit(solution)/shard_map/ppermute | solution.py:237
  25.3 1.4 %collective-permute-start.7 = (f32[4,2048]{1,0:T(4,128)}, f32[4,2048]{1,0:T(4,128)S(1)}, u32[]{:S(2)}, u32[]{:S(2)}) collective-permute-start(f32[4,2048]{1,0:T(4,128)} %copy-done.1), channel_id=1, source_target_pairs={{0,1},{1,0},{2,3},{3,2},{4,5},{5,4},{6,7},{7,6},{8,9},{9,8},{10,11... | collective-permute-start | bytes 98312 | tf_op jit(solution)/shard_map/ppermute | solution.py:237
  26.7 19.7 %collective-permute-start.13 = (bf16[256,256]{1,0:T(8,128)(2,1)S(1)}, bf16[256,256]{1,0:T(8,128)(2,1)S(1)}, u32[]{:S(2)}, u32[]{:S(2)}) collective-permute-start(bf16[256,256]{1,0:T(8,128)(2,1)S(1)} %get-tuple-element.62.kv0), channel_id=1, source_target_pairs={{0,8},{8,16},{16,24},{24,0},{1,9},{9,17},{17,25},{25,1},{2,10},{10... | collective-permute-start | bytes 393224 | tf_op jit(solution)/shard_map/ppermute | solution.py:237
  27.4 22.3 %collective-permute-start.12 = (bf16[256,256]{1,0:T(8,128)(2,1)S(1)}, bf16[256,256]{1,0:T(8,128)(2,1)S(1)}, u32[]{:S(2)}, u32[]{:S(2)}) collective-permute-start(bf16[256,256]{1,0:T(8,128)(2,1)S(1)} %get-tuple-element.62.kv0), channel_id=1, source_target_pairs={{0,16},{8,24},{16,0},{24,8},{1,17},{9,25},{17,1},{25,9},{2,18},{10... | collective-permute-start | bytes 393224 | tf_op jit(solution)/shard_map/ppermute | solution.py:237
  31.2 18.5 %collective-permute-start.11 = (bf16[256,256]{1,0:T(8,128)(2,1)S(1)}, bf16[256,256]{1,0:T(8,128)(2,1)S(1)}, u32[]{:S(2)}, u32[]{:S(2)}) collective-permute-start(bf16[256,256]{1,0:T(8,128)(2,1)S(1)} %get-tuple-element.62.kv0), channel_id=1, source_target_pairs={{0,24},{8,0},{16,8},{24,16},{1,25},{9,1},{17,9},{25,17},{2,26},{10... | collective-permute-start | bytes 393224 | tf_op jit(solution)/shard_map/ppermute | solution.py:237
  31.2 0.8 copy-start.2
  44.1 11.4 %collective-permute-start.8 = (bf16[256,256]{1,0:T(8,128)(2,1)S(1)}, bf16[256,256]{1,0:T(8,128)(2,1)S(1)}, u32[]{:S(2)}, u32[]{:S(2)}) collective-permute-start(bf16[256,256]{1,0:T(8,128)(2,1)S(1)} %get-tuple-element.59), channel_id=1, source_target_pairs={{0,16},{8,24},{16,0},{24,8},{1,17},{9,25},{17,1},{25,9},{2,18},{10... | collective-permute-start | bytes 393224 | tf_op jit(solution)/shard_map/ppermute | solution.py:237
  46.4 9.1 %collective-permute-start.9 = (bf16[256,256]{1,0:T(8,128)(2,1)S(1)}, bf16[256,256]{1,0:T(8,128)(2,1)S(1)}, u32[]{:S(2)}, u32[]{:S(2)}) collective-permute-start(bf16[256,256]{1,0:T(8,128)(2,1)S(1)} %get-tuple-element.60), channel_id=1, source_target_pairs={{0,8},{8,16},{16,24},{24,0},{1,9},{9,17},{17,25},{25,1},{2,10},{10... | collective-permute-start | bytes 393224 | tf_op jit(solution)/shard_map/ppermute | solution.py:237
  46.4 3.2 %copy-start.7 = (s32[16]{0:T(128)S(1)}, s32[16]{0:T(128)}, u32[]{:S(2)}) copy-start(s32[16]{0:T(128)} %lengths.3) | copy-start | bytes 196
  46.5 9.1 %collective-permute-start.10 = (bf16[256,256]{1,0:T(8,128)(2,1)S(1)}, bf16[256,256]{1,0:T(8,128)(2,1)S(1)}, u32[]{:S(2)}, u32[]{:S(2)}) collective-permute-start(bf16[256,256]{1,0:T(8,128)(2,1)S(1)} %get-tuple-element.61), channel_id=1, source_target_pairs={{0,24},{8,0},{16,8},{24,16},{1,25},{9,1},{17,9},{25,17},{2,26},{10... | collective-permute-start | bytes 393224 | tf_op jit(solution)/shard_map/ppermute | solution.py:237
  55.5 11.5 %collective-permute-start.17 = (f32[128,2048]{1,0:T(8,128)S(1)}, f32[128,2048]{1,0:T(8,128)S(1)}, u32[]{:S(2)}, u32[]{:S(2)}) collective-permute-start(f32[128,2048]{1,0:T(8,128)S(1)} %get-tuple-element.70), channel_id=1, source_target_pairs={{0,1},{1,0},{2,3},{3,2},{4,5},{5,4},{6,7},{7,6},{8,9},{9,8},{10,11... | collective-permute-start | bytes 3145736 | tf_op jit(solution)/shard_map/ppermute | solution.py:237
  55.7 5.5 %copy-start.3 = (f32[4,2048]{1,0:T(4,128)S(1)}, f32[4,2048]{1,0:T(4,128)}, u32[]{:S(2)}) copy-start(f32[4,2048]{1,0:T(4,128)} %copy-done.1) | copy-start | bytes 98308
  55.8 11.2 %collective-permute-start.16 = (bf16[64,256]{1,0:T(8,128)(2,1)S(1)}, bf16[64,256]{1,0:T(8,128)(2,1)S(1)}, u32[]{:S(2)}, u32[]{:S(2)}) collective-permute-start(bf16[64,256]{1,0:T(8,128)(2,1)S(1)} %get-tuple-element.98), channel_id=1, source_target_pairs={{0,6},{2,0},{4,2},{6,4},{1,7},{3,1},{5,3},{7,5},{8,14},{10,8},{12,... | collective-permute-start | bytes 98312 | tf_op jit(solution)/shard_map/ppermute | solution.py:237
  57.8 9.2 %collective-permute-start.15 = (bf16[64,256]{1,0:T(8,128)(2,1)S(1)}, bf16[64,256]{1,0:T(8,128)(2,1)S(1)}, u32[]{:S(2)}, u32[]{:S(2)}) collective-permute-start(bf16[64,256]{1,0:T(8,128)(2,1)S(1)} %get-tuple-element.99), channel_id=1, source_target_pairs={{0,2},{2,4},{4,6},{6,0},{1,3},{3,5},{5,7},{7,1},{8,10},{10,12},{12... | collective-permute-start | bytes 98312 | tf_op jit(solution)/shard_map/ppermute | solution.py:237
  59.0 8.0 %collective-permute-start.14 = (bf16[64,256]{1,0:T(8,128)(2,1)S(1)}, bf16[64,256]{1,0:T(8,128)(2,1)S(1)}, u32[]{:S(2)}, u32[]{:S(2)}) collective-permute-start(bf16[64,256]{1,0:T(8,128)(2,1)S(1)} %get-tuple-element.100), channel_id=1, source_target_pairs={{0,4},{2,6},{4,0},{6,2},{1,5},{3,7},{5,1},{7,3},{8,12},{10,14},{12... | collective-permute-start | bytes 98312 | tf_op jit(solution)/shard_map/ppermute | solution.py:237
  67.0 10.3 %collective-permute-start.21 = (bf16[256,256]{1,0:T(8,128)(2,1)S(1)}, bf16[256,256]{1,0:T(8,128)(2,1)S(1)}, u32[]{:S(2)}, u32[]{:S(2)}) collective-permute-start(bf16[256,256]{1,0:T(8,128)(2,1)S(1)} %get-tuple-element.90), channel_id=1, source_target_pairs={{0,16},{8,24},{16,0},{24,8},{1,17},{9,25},{17,1},{25,9},{2,18},{10... | collective-permute-start | bytes 393224 | tf_op jit(solution)/shard_map/ppermute | solution.py:237
  68.1 9.2 %collective-permute-start.22 = (bf16[256,256]{1,0:T(8,128)(2,1)S(1)}, bf16[256,256]{1,0:T(8,128)(2,1)S(1)}, u32[]{:S(2)}, u32[]{:S(2)}) collective-permute-start(bf16[256,256]{1,0:T(8,128)(2,1)S(1)} %get-tuple-element.91), channel_id=1, source_target_pairs={{0,8},{8,16},{16,24},{24,0},{1,9},{9,17},{17,25},{25,1},{2,10},{10... | collective-permute-start | bytes 393224 | tf_op jit(solution)/shard_map/ppermute | solution.py:237
  68.9 8.4 %collective-permute-start.23 = (bf16[256,256]{1,0:T(8,128)(2,1)S(1)}, bf16[256,256]{1,0:T(8,128)(2,1)S(1)}, u32[]{:S(2)}, u32[]{:S(2)}) collective-permute-start(bf16[256,256]{1,0:T(8,128)(2,1)S(1)} %get-tuple-element.92), channel_id=1, source_target_pairs={{0,24},{8,0},{16,8},{24,16},{1,25},{9,1},{17,9},{25,17},{2,26},{10... | collective-permute-start | bytes 393224 | tf_op jit(solution)/shard_map/ppermute | solution.py:237
  71.4 4.4 %collective-permute-start.18 = (f32[64,256]{1,0:T(8,128)S(1)}, f32[64,256]{1,0:T(8,128)S(1)}, u32[]{:S(2)}, u32[]{:S(2)}) collective-permute-start(f32[64,256]{1,0:T(8,128)S(1)} %convert_add_fusion.1), channel_id=1, source_target_pairs={{0,32},{32,0},{64,96},{96,64},{1,33},{33,1},{65,97},{97,65},{2,34}... | collective-permute-start | bytes 196616 | tf_op jit(solution)/shard_map/ppermute | solution.py:348
  75.8 8.7 %collective-permute-start.19 = (f32[64,256]{1,0:T(8,128)S(1)}, f32[64,256]{1,0:T(8,128)S(1)}, u32[]{:S(2)}, u32[]{:S(2)}) collective-permute-start(f32[64,256]{1,0:T(8,128)S(1)} %add.55), channel_id=1, source_target_pairs={{0,96},{96,0},{32,64},{64,32},{1,97},{97,1},{33,65},{65,33},{2,98}... | collective-permute-start | bytes 196616 | tf_op jit(solution)/shard_map/ppermute | solution.py:351
  77.4 8.4 %collective-permute-start.24 = (bf16[2,32,256]{2,1,0:T(8,128)(2,1)S(1)}, bf16[2,32,256]{2,1,0:T(8,128)(2,1)S(1)}, u32[]{:S(2)}, u32[]{:S(2)}) collective-permute-start(bf16[2,32,256]{2,1,0:T(8,128)(2,1)S(1)} %bitcast.16), channel_id=1, source_target_pairs={{0,4},{2,6},{4,0},{6,2},{1,5},{3,7},{5,1},{7,3},{8,12},{10,14},{12... | collective-permute-start | bytes 98312 | tf_op jit(solution)/shard_map/ppermute | solution.py:237
  81.5 5.5 %collective-permute-start.26 = (bf16[2,32,256]{2,1,0:T(8,128)(2,1)S(1)}, bf16[2,32,256]{2,1,0:T(8,128)(2,1)S(1)}, u32[]{:S(2)}, u32[]{:S(2)}) collective-permute-start(bf16[2,32,256]{2,1,0:T(8,128)(2,1)S(1)} %bitcast.15), channel_id=1, source_target_pairs={{0,6},{2,0},{4,2},{6,4},{1,7},{3,1},{5,3},{7,5},{8,14},{10,8},{12,... | collective-permute-start | bytes 98312 | tf_op jit(solution)/shard_map/ppermute | solution.py:237
  84.2 6.0 %collective-permute-start.25 = (bf16[2,32,256]{2,1,0:T(8,128)(2,1)S(1)}, bf16[2,32,256]{2,1,0:T(8,128)(2,1)S(1)}, u32[]{:S(2)}, u32[]{:S(2)}) collective-permute-start(bf16[2,32,256]{2,1,0:T(8,128)(2,1)S(1)} %bitcast.14), channel_id=1, source_target_pairs={{0,2},{2,4},{4,6},{6,0},{1,3},{3,5},{5,7},{7,1},{8,10},{10,12},{12... | collective-permute-start | bytes 98312 | tf_op jit(solution)/shard_map/ppermute | solution.py:237
  84.4 6.4 %collective-permute-start.20 = (f32[64,256]{1,0:T(8,128)S(1)}, f32[64,256]{1,0:T(8,128)S(1)}, u32[]{:S(2)}, u32[]{:S(2)}) collective-permute-start(f32[64,256]{1,0:T(8,128)S(1)} %add.56), channel_id=1, source_target_pairs={{0,128},{128,0},{1,129},{129,1},{2,130},{130,2},{3,131},{131,3},{4... | collective-permute-start | bytes 196616 | tf_op jit(solution)/shard_map/ppermute | solution.py:237

commit v6 on v5

--- a/solution.py
+++ b/solution.py
@@ -16,6 +16,8 @@
 TILES = TOK // TILE
 TROWS = TILE * HEADS
 ROWS = TOK * HEADS
+STATS = TILES * HEADS * 8
+PARTS = 3
 ROOT_SH = 64
 BR_SH = 32
 NY = 4
@@ -36,14 +38,32 @@
     return lax.dot_general(a, b, (((ca,), (cb,)), ((), ())), preferred_element_type=F32)
 
 
+def split(rows):
+    parts = []
+    for _ in range(PARTS):
+        parts.append(rows.astype(BF))
+        rows = rows - parts[-1].astype(F32)
+    return parts
+
+
 def move(rows, onehot):
-    total = None
-    for _ in range(3):
-        part = rows.astype(BF)
-        rows = rows - part.astype(F32)
-        term = dot(part, onehot, 1, 1)
-        total = term if total is None else total + term
-    return total
+    return [dot(part, onehot, 1, 1) for part in split(rows)]
+
+
+def read_stats(qg_ref, stat_ref):
+    for t in range(TILES):
+        terms = []
+        for j in range(4):
+            pair = qg_ref[pl.ds(2 * ROWS + (t * 4 + j) * 16, 16), :].astype(F32)
+            terms += [pair[:HEADS], pair[HEADS:]]
+        norm = (terms[0] + terms[1]) + terms[2]
+        delta = (terms[3] + terms[4]) + terms[5]
+        norm0 = jnp.where(terms[6] < 0.5, norm, BIG)
+        norm1 = jnp.where(terms[6] < 0.5, BIG, norm)
+        for h in range(HEADS):
+            at = pl.ds((t * HEADS + h) * TILE, TILE)
+            for r, value in enumerate((norm, norm0, norm1, delta)):
+                stat_ref[r : r + 1, at] = value[h : h + 1]
 
 
 def pair_terms(keys, values, q, g, norm, delta, mask=None):
@@ -56,7 +76,7 @@
 
 def prepare_kernel(
     seg_branch, q_hbm, o_hbm, g_hbm, norm_ref, leaf_ref, seg_ref,
-    qg_ref, stat_ref, onehot_ref, grad_ref, dq_ref, q_ref, o_ref, g_ref, sems,
+    qg_ref, onehot_ref, grad_ref, dq_ref, q_ref, o_ref, g_ref, stat_ref, sems,
 ):
     copies = [
         pltpu.make_async_copy(source, target, sems.at[i])
@@ -98,17 +118,18 @@
             jnp.sum(g_ref[:, at].astype(F32) * o_ref[:, at].astype(F32), axis=1, keepdims=True)
         )
     delta = move(jnp.concatenate(columns, axis=1).T, onehot)
-    norm = move(norm_ref[...], onehot) * LOG2E
+    norm = move(norm_ref[...] * LOG2E, onehot)
     place = jnp.concatenate([lane, first, branch, lane, lane, lane, lane, lane], axis=0)
-    place = dot(place.astype(F32).astype(BF), onehot, 1, 1).astype(jnp.int32)
-    norm0 = jnp.where(place[2:3] == 0, norm, BIG)
-    norm1 = jnp.where(place[2:3] == 0, BIG, norm)
+    place = dot(place.astype(F32).astype(BF), onehot, 1, 1)
+    flag = jnp.broadcast_to(place[2:3], (HEADS, TOK))
+    terms = norm + delta + [flag, flag]
     for t in range(TILES):
-        for h in range(HEADS):
-            at = pl.ds((t * HEADS + h) * TILE, TILE)
-            tok = slice(t * TILE, (t + 1) * TILE)
-            for r, value in enumerate((norm, norm0, norm1, delta)):
-                stat_ref[r : r + 1, at] = value[h : h + 1, tok]
+        tok = slice(t * TILE, (t + 1) * TILE)
+        for j in range(4):
+            pair = jnp.concatenate([terms[2 * j][:, tok], terms[2 * j + 1][:, tok]], axis=0)
+            qg_ref[pl.ds(2 * ROWS + (t * 4 + j) * 16, 16), :] = pair.astype(BF)
+    read_stats(qg_ref, stat_ref)
+    place = place.astype(jnp.int32)
 
     keys = leaf_ref[:, :HD]
     values = leaf_ref[:, HD:]
@@ -166,9 +187,11 @@
         lax.fori_loop(0, TILES, visit, 0)
 
 
-def root_kernel(kv0, kv1, kv2, kv3, qg0, s0, qg1, s1, dq0, dq1, to0, to1, to2, to3, kv_ref, total):
+def root_kernel(kv0, kv1, kv2, kv3, qg0, qg1, dq0, dq1, to0, to1, to2, to3, kv_ref, total, s0, s1):
     dq0[...] = jnp.zeros_like(dq0)
     dq1[...] = jnp.zeros_like(dq1)
+    read_stats(qg0, s0)
+    read_stats(qg1, s1)
     sources = ((qg0, s0, dq0), (qg1, s1, dq1))
     pieces, targets = (kv0, kv1, kv2, kv3), (to0, to1, to2, to3)
     each = NZ * ROOT_SH
@@ -189,7 +212,8 @@
     return lax.broadcasted_iota(jnp.int32, (BR_SH, 1), 0) + start < lengths[place[3] + b]
 
 
-def branch_other_kernel(place, lengths, kv0, kv1, kv2, kv3, qg_ref, stat_ref, dq_in, dq_ref, kv_ref, total):
+def branch_other_kernel(place, lengths, kv0, kv1, kv2, kv3, qg_ref, dq_in, dq_ref, kv_ref, total, stat_ref):
+    read_stats(qg_ref, stat_ref)
     dq_ref[...] = dq_in[...]
     total[...] = jnp.zeros_like(total)
     for b in range(2):
@@ -203,8 +227,9 @@
 
 
 def branch_own_kernel(
-    place, lengths, kv_ref, total_in, qg_ref, stat_ref, dq_in, dq_ref, to0, to1, to2, to3, total
+    place, lengths, kv_ref, total_in, qg_ref, dq_in, dq_ref, to0, to1, to2, to3, total, stat_ref
 ):
+    read_stats(qg_ref, stat_ref)
     dq_ref[...] = dq_in[...]
     for b in range(2):
         whole = pl.ds(b * KB, KB)
@@ -242,7 +267,7 @@
 
 
 def exchange(blocks, axis, size):
-    return [blocks[0]] + [shift(blocks[k], axis, size, k) for k in (2, 1, 3)]
+    return [blocks[0]] + [shift(blocks[k], axis, size, k) for k in range(1, size)]
 
 
 def added(terms):
@@ -257,23 +282,24 @@
 
     shard = jnp.concatenate([root_kv, branch_kv.reshape(2 * BR_SH, 2 * HD)], axis=0)
     block = shape((NZ * ROOT_SH, 2 * HD), BF)
-    qg0, s0, onehot, leaf_grad, dq_leaf = pl.pallas_call(
+    stats = pltpu.VMEM((4, ROWS), F32)
+
+    qg0, onehot, leaf_grad, dq_leaf = pl.pallas_call(
         prepare_kernel,
         out_shape=(
-            shape((2 * ROWS, HD), BF),
-            shape((4, ROWS), F32),
+            shape((2 * ROWS + STATS, HD), BF),
             shape((TOK, TOK), BF),
             shape((TOK, 2 * HD), F32),
             shape((HD, ROWS), F32),
         ),
         in_specs=[SMEM] + [HBM] * 3 + [VMEM] * 3,
-        out_specs=(VMEM,) * 5,
-        scratch_shapes=[pltpu.VMEM((TOK, HEADS * HD), BF)] * 3 + [pltpu.SemaphoreType.DMA((3,))],
+        out_specs=(VMEM,) * 4,
+        scratch_shapes=[pltpu.VMEM((TOK, HEADS * HD), BF)] * 3 + [stats, pltpu.SemaphoreType.DMA((3,))],
         compiler_params=PARAMS,
         cost_estimate=pl.CostEstimate(flops=4_000_000_000, bytes_accessed=5_000_000, transcendentals=0),
         name="prepare",
     )(segment_branch, *(pltpu.with_memory_space_constraint(x, pltpu.HBM) for x in (queries, attn_out, out_grad)), log_norm.T, leaf_kv, segment_ids)
-    pieces, qg0, s0 = lax.optimization_barrier((gather(shard, "zh", NZ), qg0, s0))
+    pieces, qg0 = lax.optimization_barrier((gather(shard, "zh", NZ), qg0))
     root_z, branch_z = pl.pallas_call(
         pack_kernel,
         out_shape=(block, block),
@@ -286,8 +312,6 @@
     roots = gather(root_z, "y", NY)
     branches = gather(branch_z, "y", NY)
     qg1 = shift(qg0, "c", 2, 1)
-    s1 = shift(s0, "c", 2, 1)
-    tokens = (qg0, s0, qg1, s1)
     dq_shape = shape((HD, ROWS), F32)
 
 
@@ -296,26 +320,27 @@
     dq0, dq1, *root_terms = pl.pallas_call(
         root_kernel,
         out_shape=(dq_shape, dq_shape, block, block, block, block),
-        in_specs=[VMEM] * 8,
+        in_specs=[VMEM] * 6,
         out_specs=(VMEM,) * 6,
-        scratch_shapes=scratch,
+        scratch_shapes=scratch + [stats, stats],
         compiler_params=PARAMS,
         cost_estimate=pl.CostEstimate(flops=10_000_000_000, bytes_accessed=8_000_000, transcendentals=0),
         name="root",
-    )(*roots, *tokens)
+    )(*roots, qg0, qg1)
     root_y = exchange(root_terms, "y", NY)
 
     branch_cost = pl.CostEstimate(flops=4_500_000_000, bytes_accessed=5_000_000, transcendentals=0)
     dq1, branch_kv_all, branch_total = pl.pallas_call(
         branch_other_kernel,
         out_shape=(dq_shape, shape((2 * KB, 2 * HD), BF), shape((2 * KB, 2 * HD), F32)),
-        in_specs=[SMEM] * 2 + [VMEM] * 7,
+        in_specs=[SMEM] * 2 + [VMEM] * 6,
         out_specs=(VMEM,) * 3,
-        input_output_aliases={8: 0},
+        scratch_shapes=[stats],
+        input_output_aliases={7: 0},
         compiler_params=PARAMS,
         cost_estimate=branch_cost,
         name="branch_other",
-    )(place, branch_len, *branches, qg1, s1, dq1)
+    )(place, branch_len, *branches, qg1, dq1)
     root_y, dq1, branch_total = lax.optimization_barrier((root_y, dq1, branch_total))
     other = shift(dq1, "c", 2, 1)
     root_y = added(root_y).astype(BF).reshape(NZ, ROOT_SH, 2 * HD)
@@ -324,14 +349,14 @@
     dq0, *branch_terms = pl.pallas_call(
         branch_own_kernel,
         out_shape=(dq_shape, block, block, block, block),
-        in_specs=[SMEM] * 2 + [VMEM] * 5,
+        in_specs=[SMEM] * 2 + [VMEM] * 4,
         out_specs=(VMEM,) * 5,
-        scratch_shapes=[pltpu.VMEM((KB, 2 * HD), F32)],
-        input_output_aliases={6: 0},
+        scratch_shapes=[pltpu.VMEM((KB, 2 * HD), F32), stats],
+        input_output_aliases={5: 0},
         compiler_params=PARAMS,
         cost_estimate=branch_cost,
         name="branch_own",
-    )(place, branch_len, branch_kv_all, branch_total, qg0, s0, dq0)
+    )(place, branch_len, branch_kv_all, branch_total, qg0, dq0)
     root_z, other, branch_terms, dq0 = lax.optimization_barrier((root_z, other, branch_terms, dq0))
 
     branch_y = exchange(branch_terms, "y", NY)

time: 91.8 us -> 92.4 us (level)
  waiting for transfers between devices: 8.82 us -> 6.35 us
  local copies, waits for them, and re-layouts: 1.94 us -> 2.96 us
    ppermute x25 -> x24, waiting for transfers between devices: 6.14 us -> 4.16 us  [shift(): lax.ppermute(value, axis, [(i, (i + by) % size) for i in range(size)])]
    unnamed x16 -> x10, local copies, waits for them, and re-layouts: 1.92 us -> 2.94 us
    ppermute x25 -> x24, starting transfers between devices: 45.3 us -> 45.7 us  [shift(): lax.ppermute(value, axis, [(i, (i + by) % size) for i in range(size)])]
  transfers between devices with their start and end apart: 27 -> 26, of which waited for: 6 -> 6; matrix products, arithmetic and copies ran while one was open for 1% -> 1% of each run, Pallas kernels for 33% -> 34%
where the time goes in v6:
time: 92.4 us; the launch traced here: 91.6 us
  starting transfers between devices  47.8 us (52%)
  Pallas kernels  31.3 us (34%)
  waiting for transfers between devices  6.35 us (7%)
  local copies, waits for them, and re-layouts  2.96 us (3%)
  other arithmetic  2.33 us (3%)
    ppermute x24, starting transfers between devices, shift(): lax.ppermute(value, axis, [(i, (i + by) % size) for i in range(size)])  45.7 us
    pallas_call x1, Pallas kernels, shards(): pl.pallas_call(root_kernel, out_shape=(dq_shape, dq_shape, block, block,...  12.2 us
    pallas_call x1, Pallas kernels, shards(): pl.pallas_call(branch_other_kernel, out_shape=(dq_shape, shape((2 * KB, 2...  5.84 us
    pallas_call x1, Pallas kernels, shards(): pl.pallas_call(branch_own_kernel, out_shape=(dq_shape, block, block, bloc...  5.73 us
    pallas_call x1, Pallas kernels, shards(): pl.pallas_call(prepare_kernel, out_shape=(shape((2 * ROWS + STATS, HD), B...  5.32 us
    ppermute x24, waiting for transfers between devices, shift(): lax.ppermute(value, axis, [(i, (i + by) % size) for i in range(size)])  4.16 us
    unnamed x10, local copies, waits for them, and re-layouts  2.94 us
    ppermute x1, waiting for transfers between devices, shards(): pair = lax.ppermute(root_part, 'x', [(0, 1), (1, 0), (2, 3), (3, 2)])  2.19 us
  transfers between devices with their start and end apart: 26, of which 6 were waited for; matrix products, arithmetic and copies ran while one was open for 1% of the time, Pallas kernels for 34%

profile of v6, /device:TPU:2, one launch (start us, length us, event | category | flops | bytes accessed | tf_op | source)
XLA Modules:
  0.0 91.6 jit_solution(12438284006331627805)
XLA Ops:
  0.6 0.8 pad_maximum_fusion.z0
  1.4 3.3 %collective-permute-start.2 = (bf16[128,256]{1,0:T(8,128)(2,1)S(1)}, bf16[128,256]{1,0:T(8,128)(2,1)S(1)}, u32[]{:S(2)}, u32[]{:S(2)}) collective-permute-start(bf16[128,256]{1,0:T(8,128)(2,1)S(1)} %pad_maximum_fusion.z0), channel_id=1, source_target_pairs={{0,2},{2,4},{4,6},{6,0},{1,3},{3,5},{5,7},{7,1},{8,10},{10,12},{12... | collective-permute-start | bytes 196616 | tf_op jit(solution)/shard_map/ppermute | solution.py:262
  4.7 5.4 %collective-permute-start.1 = (bf16[128,256]{1,0:T(8,128)(2,1)S(1)}, bf16[128,256]{1,0:T(8,128)(2,1)S(1)}, u32[]{:S(2)}, u32[]{:S(2)}) collective-permute-start(bf16[128,256]{1,0:T(8,128)(2,1)S(1)} %pad_maximum_fusion.z0), channel_id=1, source_target_pairs={{0,4},{2,6},{4,0},{6,2},{1,5},{3,7},{5,1},{7,3},{8,12},{10,14},{12... | collective-permute-start | bytes 196616 | tf_op jit(solution)/shard_map/ppermute | solution.py:262
  10.1 2.7 %collective-permute-start = (bf16[128,256]{1,0:T(8,128)(2,1)S(1)}, bf16[128,256]{1,0:T(8,128)(2,1)S(1)}, u32[]{:S(2)}, u32[]{:S(2)}) collective-permute-start(bf16[128,256]{1,0:T(8,128)(2,1)S(1)} %pad_maximum_fusion.z0), channel_id=1, source_target_pairs={{0,6},{2,0},{4,2},{6,4},{1,7},{3,1},{5,3},{7,5},{8,14},{10,8},{12,... | collective-permute-start | bytes 196616 | tf_op jit(solution)/shard_map/ppermute | solution.py:262
  12.7 0.9 copy-done
  13.6 0.7 copy-done.1
  14.3 0.7 copy-done.2
  15.0 0.7 copy-done.3
  15.7 5.3 %prepare.1 = (bf16[4224,128]{1,0:T(8,128)(2,1)S(1)}, bf16[256,256]{1,0:T(8,128)(2,1)S(1)}, f32[256,256]{1,0:T(8,128)}, f32[128,2048]{1,0:T(8,128)S(1)}) custom-call(s32[1,8]{1,0:T(1,128)S(1)} %copy-done.3, bf16[256,1024]{1,0:T(8,128)(2,1)} %q_hbm.1, bf16[256,1024]{1,0:T(8,128)(2,1)} %o_hbm.1, bf16[256,1024]{1,0:T(8,128)(2,1)} %g_hbm.1, ...), custom_call_target="tpu_custom_call" | custom-call | flops 4000000000 | bytes 5000000 | tf_op jit(solution)/shard_map/prepare/pallas_call | solution.py:287
  21.0 0.0 collective-permute-done.2.z3
  21.0 0.0 collective-permute-done.1.z2
  21.0 0.0 collective-permute-done.z1
  21.0 0.1 collective-permute-start.6
  21.1 0.7 pack.1
  21.8 1.6 %collective-permute-start.5 = (bf16[256,256]{1,0:T(8,128)(2,1)}, bf16[256,256]{1,0:T(8,128)(2,1)}, u32[]{:S(2)}, u32[]{:S(2)}) collective-permute-start(bf16[256,256]{1,0:T(8,128)(2,1)} %get-tuple-element.52.kv0), channel_id=1, source_target_pairs={{0,8},{8,16},{16,24},{24,0},{1,9},{9,17},{17,25},{25,1},{2,10},{10... | collective-permute-start | bytes 393224 | tf_op jit(solution)/shard_map/ppermute | solution.py:262
  23.4 2.9 %collective-permute-start.4 = (bf16[256,256]{1,0:T(8,128)(2,1)}, bf16[256,256]{1,0:T(8,128)(2,1)}, u32[]{:S(2)}, u32[]{:S(2)}) collective-permute-start(bf16[256,256]{1,0:T(8,128)(2,1)} %get-tuple-element.52.kv0), channel_id=1, source_target_pairs={{0,16},{8,24},{16,0},{24,8},{1,17},{9,25},{17,1},{25,9},{2,18},{10... | collective-permute-start | bytes 393224 | tf_op jit(solution)/shard_map/ppermute | solution.py:262
  26.3 1.3 %collective-permute-start.3 = (bf16[256,256]{1,0:T(8,128)(2,1)}, bf16[256,256]{1,0:T(8,128)(2,1)}, u32[]{:S(2)}, u32[]{:S(2)}) collective-permute-start(bf16[256,256]{1,0:T(8,128)(2,1)} %get-tuple-element.52.kv0), channel_id=1, source_target_pairs={{0,24},{8,0},{16,8},{24,16},{1,25},{9,1},{17,9},{25,17},{2,26},{10... | collective-permute-start | bytes 393224 | tf_op jit(solution)/shard_map/ppermute | solution.py:262
  27.6 0.1 pad_add_fusion.place
  27.7 0.7 collective-permute-start.12
  28.4 0.9 collective-permute-done.5.kv3
  29.3 4.5 %collective-permute-start.11 = (bf16[256,256]{1,0:T(8,128)(2,1)S(1)}, bf16[256,256]{1,0:T(8,128)(2,1)S(1)}, u32[]{:S(2)}, u32[]{:S(2)}) collective-permute-start(bf16[256,256]{1,0:T(8,128)(2,1)S(1)} %get-tuple-element.58.kv0), channel_id=1, source_target_pairs={{0,16},{8,24},{16,0},{24,8},{1,17},{9,25},{17,1},{25,9},{2,18},{10... | collective-permute-start | bytes 393224 | tf_op jit(solution)/shard_map/ppermute | solution.py:262
  33.8 0.0 collective-permute-done.4.kv2
  33.8 0.0 collective-permute-start.10
  33.8 0.0 collective-permute-done.3.kv1
  33.8 0.0 collective-permute-done.6.qg1.qg_ref
  33.8 12.2 %root.1 = (f32[128,2048]{1,0:T(8,128)S(1)}, f32[128,2048]{1,0:T(8,128)S(1)}, bf16[256,256]{1,0:T(8,128)(2,1)S(1)}, bf16[256,256]{1,0:T(8,128)(2,1)S(1)}, bf16[25...) custom-call(bf16[256,256]{1,0:T(8,128)(2,1)} %get-tuple-element.52.kv0, bf16[256,256]{1,0:T(8,128)(2,1)} %collective-permute-done.3.kv1, ...), custom_call_target="tpu_custom_call" | custom-call | flops 10000000000 | bytes 8000000 | tf_op jit(solution)/shard_map/root/pallas_call | solution.py:320
  46.0 2.1 %collective-permute-start.7 = (bf16[256,256]{1,0:T(8,128)(2,1)S(1)}, bf16[256,256]{1,0:T(8,128)(2,1)S(1)}, u32[]{:S(2)}, u32[]{:S(2)}) collective-permute-start(bf16[256,256]{1,0:T(8,128)(2,1)S(1)} %get-tuple-element.55), channel_id=1, source_target_pairs={{0,8},{8,16},{16,24},{24,0},{1,9},{9,17},{17,25},{25,1},{2,10},{10... | collective-permute-start | bytes 393224 | tf_op jit(solution)/shard_map/ppermute | solution.py:262
  48.1 1.3 %collective-permute-start.8 = (bf16[256,256]{1,0:T(8,128)(2,1)S(1)}, bf16[256,256]{1,0:T(8,128)(2,1)S(1)}, u32[]{:S(2)}, u32[]{:S(2)}) collective-permute-start(bf16[256,256]{1,0:T(8,128)(2,1)S(1)} %get-tuple-element.56), channel_id=1, source_target_pairs={{0,16},{8,24},{16,0},{24,8},{1,17},{9,25},{17,1},{25,9},{2,18},{10... | collective-permute-start | bytes 393224 | tf_op jit(solution)/shard_map/ppermute | solution.py:262
  49.4 0.0 collective-permute-done.12.kv3
  49.4 2.1 %collective-permute-start.9 = (bf16[256,256]{1,0:T(8,128)(2,1)S(1)}, bf16[256,256]{1,0:T(8,128)(2,1)S(1)}, u32[]{:S(2)}, u32[]{:S(2)}) collective-permute-start(bf16[256,256]{1,0:T(8,128)(2,1)S(1)} %get-tuple-element.57), channel_id=1, source_target_pairs={{0,24},{8,0},{16,8},{24,16},{1,25},{9,1},{17,9},{25,17},{2,26},{10... | collective-permute-start | bytes 393224 | tf_op jit(solution)/shard_map/ppermute | solution.py:262
  51.5 0.0 collective-permute-done.11.kv2
  51.5 0.0 collective-permute-done.10.kv1
  51.5 5.8 %branch_other.1 = (f32[128,2048]{1,0:T(8,128)S(1)}, bf16[1024,256]{1,0:T(8,128)(2,1)S(1)}, f32[1024,256]{1,0:T(8,128)S(1)}) custom-call(s32[4]{0:T(128)S(1)} %pad_add_fusion.place, s32[16]{0:T(128)S(1)} %copy-done.4, bf16[256,256]{1,0:T(8,128)(2,1)S(1)} %get-tuple-element.58.kv0, ...), custom_call_target="tpu_custom_call", output_to_operand_aliasing={{0}: (7, {})} | custom-call | flops 4499999744 | bytes 5000000 | tf_op jit(solution)/shard_map/branch_other/pallas_call | solution.py:333
  57.4 0.0 collective-permute-done.7
  57.4 0.0 collective-permute-done.8
  57.4 0.0 collective-permute-done.9
  57.4 0.1 collective-permute-start.16
  57.5 0.1 add_convert_fusion.1
  57.6 0.3 collective-permute-start.15
  57.9 3.8 %collective-permute-start.14 = (bf16[64,256]{1,0:T(8,128)(2,1)S(1)}, bf16[64,256]{1,0:T(8,128)(2,1)S(1)}, u32[]{:S(2)}, u32[]{:S(2)}) collective-permute-start(bf16[64,256]{1,0:T(8,128)(2,1)S(1)} %get-tuple-element.95), channel_id=1, source_target_pairs={{0,4},{2,6},{4,0},{6,2},{1,5},{3,7},{5,1},{7,3},{8,12},{10,14},{12... | collective-permute-start | bytes 98312 | tf_op jit(solution)/shard_map/ppermute | solution.py:262
  61.7 0.1 collective-permute-start.13
  61.8 5.7 %branch_own.1 = (f32[128,2048]{1,0:T(8,128)S(1)}, bf16[256,256]{1,0:T(8,128)(2,1)S(1)}, bf16[256,256]{1,0:T(8,128)(2,1)S(1)}, bf16[256,256]{1,0:T(8,128)(2,1)S(1)}, bf16[256,256]{1,0:T(8,128)(2,1)S(1)}) custom-call(s32[4]{0:T(128)S(1)} %pad_add_fusion.place, s32[16]{0:T(128)S(1)} %copy-done.4, ...), custom_call_target="tpu_custom_call", output_to_operand_aliasing={{0}: (5, {})} | custom-call | flops 4499999744 | bytes 5000000 | tf_op jit(solution)/shard_map/branch_own/pallas_call | solution.py:349
  67.6 0.2 collective-permute-done.13
  67.7 0.0 collective-permute-done.16.other
  67.7 0.0 collective-permute-start.20
  67.7 2.2 %collective-permute-start.21 = (bf16[256,256]{1,0:T(8,128)(2,1)S(1)}, bf16[256,256]{1,0:T(8,128)(2,1)S(1)}, u32[]{:S(2)}, u32[]{:S(2)}) collective-permute-start(bf16[256,256]{1,0:T(8,128)(2,1)S(1)} %get-tuple-element.87), channel_id=1, source_target_pairs={{0,16},{8,24},{16,0},{24,8},{1,17},{9,25},{17,1},{25,9},{2,18},{10... | collective-permute-start | bytes 393224 | tf_op jit(solution)/shard_map/ppermute | solution.py:262
  69.9 1.2 %collective-permute-start.22 = (bf16[256,256]{1,0:T(8,128)(2,1)S(1)}, bf16[256,256]{1,0:T(8,128)(2,1)S(1)}, u32[]{:S(2)}, u32[]{:S(2)}) collective-permute-start(bf16[256,256]{1,0:T(8,128)(2,1)S(1)} %get-tuple-element.88), channel_id=1, source_target_pairs={{0,24},{8,0},{16,8},{24,16},{1,25},{9,1},{17,9},{25,17},{2,26},{10... | collective-permute-start | bytes 393224 | tf_op jit(solution)/shard_map/ppermute | solution.py:262
  71.2 0.6 collective-permute-start.17
  71.8 1.6 %finish.1 = bf16[256,1024]{1,0:T(8,128)(2,1)} custom-call(bf16[256,256]{1,0:T(8,128)(2,1)S(1)} %get-tuple-element.79.onehot_ref, f32[128,2048]{1,0:T(8,128)S(1)} %get-tuple-element.80.leaf, f32[128,2048]{1,0:T(8,128)S(1)} %get-tuple-element.81.mine, f32[128,2048]{1,0:T(8,128)S(1)} %collective-permute-done.16.other), custom_call_target="tpu_custom_call" | custom-call | flops 200000000 | bytes 3000000 | tf_op jit(solution)/shard_map/finish/pallas_call | solution.py:363
  73.3 2.2 %collective-permute-done.17 = f32[64,256]{1,0:T(8,128)S(1)} collective-permute-done((f32[64,256]{1,0:T(8,128)S(1)}, f32[64,256]{1,0:T(8,128)S(1)}, u32[]{:S(2)}, u32[]{:S(2)}) %collective-permute-start.17) | collective-permute-done | bytes 65568 | tf_op jit(solution)/shard_map/ppermute | solution.py:373
  75.5 1.6 %collective-permute-start.18 = (f32[64,256]{1,0:T(8,128)S(1)}, f32[64,256]{1,0:T(8,128)S(1)}, u32[]{:S(2)}, u32[]{:S(2)}) collective-permute-start(f32[64,256]{1,0:T(8,128)S(1)} %add.55), channel_id=1, source_target_pairs={{0,96},{96,0},{32,64},{64,32},{1,97},{97,1},{33,65},{65,33},{2,98}... | collective-permute-start | bytes 196616 | tf_op jit(solution)/shard_map/ppermute | solution.py:376
  77.1 0.0 collective-permute-done.20
  77.1 0.4 collective-permute-done.22
  77.6 0.1 add_convert_fusion
  77.7 2.8 %collective-permute-start.23 = (bf16[2,32,256]{2,1,0:T(8,128)(2,1)S(1)}, bf16[2,32,256]{2,1,0:T(8,128)(2,1)S(1)}, u32[]{:S(2)}, u32[]{:S(2)}) collective-permute-start(bf16[2,32,256]{2,1,0:T(8,128)(2,1)S(1)} %bitcast.16), channel_id=1, source_target_pairs={{0,2},{2,4},{4,6},{6,0},{1,3},{3,5},{5,7},{7,1},{8,10},{10,12},{12... | collective-permute-start | bytes 98312 | tf_op jit(solution)/shard_map/ppermute | solution.py:262
  80.5 1.4 %collective-permute-start.25 = (bf16[2,32,256]{2,1,0:T(8,128)(2,1)S(1)}, bf16[2,32,256]{2,1,0:T(8,128)(2,1)S(1)}, u32[]{:S(2)}, u32[]{:S(2)}) collective-permute-start(bf16[2,32,256]{2,1,0:T(8,128)(2,1)S(1)} %bitcast.15), channel_id=1, source_target_pairs={{0,6},{2,0},{4,2},{6,4},{1,7},{3,1},{5,3},{7,5},{8,14},{10,8},{12,... | collective-permute-start | bytes 98312 | tf_op jit(solution)/shard_map/ppermute | solution.py:262
  81.9 4.7 %collective-permute-start.24 = (bf16[2,32,256]{2,1,0:T(8,128)(2,1)S(1)}, bf16[2,32,256]{2,1,0:T(8,128)(2,1)S(1)}, u32[]{:S(2)}, u32[]{:S(2)}) collective-permute-start(bf16[2,32,256]{2,1,0:T(8,128)(2,1)S(1)} %bitcast.14), channel_id=1, source_target_pairs={{0,4},{2,6},{4,0},{6,2},{1,5},{3,7},{5,1},{7,3},{8,12},{10,14},{12... | collective-permute-start | bytes 98312 | tf_op jit(solution)/shard_map/ppermute | solution.py:262
  86.6 1.1 %collective-permute-start.19 = (f32[64,256]{1,0:T(8,128)S(1)}, f32[64,256]{1,0:T(8,128)S(1)}, u32[]{:S(2)}, u32[]{:S(2)}) collective-permute-start(f32[64,256]{1,0:T(8,128)S(1)} %add.56), channel_id=1, source_target_pairs={{0,128},{128,0},{1,129},{129,1},{2,130},{130,2},{3,131},{131,3},{4... | collective-permute-start | bytes 196616 | tf_op jit(solution)/shard_map/ppermute | solution.py:262
  87.7 0.0 collective-permute-done.23
  87.7 0.0 collective-permute-done.25
  87.7 2.0 %collective-permute-done.24 = bf16[2,32,256]{2,1,0:T(8,128)(2,1)S(1)} collective-permute-done((bf16[2,32,256]{2,1,0:T(8,128)(2,1)S(1)}, bf16[2,32,256]{2,1,0:T(8,128)(2,1)S(1)}, u32[]{:S(2)}, u32[]{:S(2)}) %collective-permute-start.24) | collective-permute-done | bytes 32800 | tf_op jit(solution)/shard_map/ppermute | solution.py:262
  89.7 0.6 convert_add_fusion
  90.3 0.6 collective-permute-done.19
  91.0 0.6 add.57
  (15 shorter events, 0.1 us)
Async XLA Ops:
  1.4 19.6 %collective-permute-start.2 = (bf16[128,256]{1,0:T(8,128)(2,1)S(1)}, bf16[128,256]{1,0:T(8,128)(2,1)S(1)}, u32[]{:S(2)}, u32[]{:S(2)}) collective-permute-start(bf16[128,256]{1,0:T(8,128)(2,1)S(1)} %pad_maximum_fusion.z0), channel_id=1, source_target_pairs={{0,2},{2,4},{4,6},{6,0},{1,3},{3,5},{5,7},{7,1},{8,10},{10,12},{12... | collective-permute-start | bytes 196616 | tf_op jit(solution)/shard_map/ppermute | solution.py:262
  4.7 16.3 %collective-permute-start.1 = (bf16[128,256]{1,0:T(8,128)(2,1)S(1)}, bf16[128,256]{1,0:T(8,128)(2,1)S(1)}, u32[]{:S(2)}, u32[]{:S(2)}) collective-permute-start(bf16[128,256]{1,0:T(8,128)(2,1)S(1)} %pad_maximum_fusion.z0), channel_id=1, source_target_pairs={{0,4},{2,6},{4,0},{6,2},{1,5},{3,7},{5,1},{7,3},{8,12},{10,14},{12... | collective-permute-start | bytes 196616 | tf_op jit(solution)/shard_map/ppermute | solution.py:262
  10.1 11.0 %collective-permute-start = (bf16[128,256]{1,0:T(8,128)(2,1)S(1)}, bf16[128,256]{1,0:T(8,128)(2,1)S(1)}, u32[]{:S(2)}, u32[]{:S(2)}) collective-permute-start(bf16[128,256]{1,0:T(8,128)(2,1)S(1)} %pad_maximum_fusion.z0), channel_id=1, source_target_pairs={{0,6},{2,0},{4,2},{6,4},{1,7},{3,1},{5,3},{7,5},{8,14},{10,8},{12,... | collective-permute-start | bytes 196616 | tf_op jit(solution)/shard_map/ppermute | solution.py:262
  12.7 0.9 copy-start
  13.6 0.7 copy-start.1
  14.3 0.7 copy-start.2
  15.0 0.7 copy-start.3
  21.0 12.8 %collective-permute-start.6 = (bf16[4224,128]{1,0:T(8,128)(2,1)S(1)}, bf16[4224,128]{1,0:T(8,128)(2,1)S(1)}, u32[]{:S(2)}, u32[]{:S(2)}) collective-permute-start(bf16[4224,128]{1,0:T(8,128)(2,1)S(1)} %get-tuple-element.53.qg0.qg_ref), channel_id=1, source_target_pairs={{0,1},{1,0},{2,3},{3,2},{4,5},{5,4},{6,7},{7,6},{8,9},{9,8},{10,11... | collective-permute-start | bytes 3244040 | tf_op jit(solution)/shard_map/ppermute | solution.py:262
  21.8 7.5 %collective-permute-start.5 = (bf16[256,256]{1,0:T(8,128)(2,1)}, bf16[256,256]{1,0:T(8,128)(2,1)}, u32[]{:S(2)}, u32[]{:S(2)}) collective-permute-start(bf16[256,256]{1,0:T(8,128)(2,1)} %get-tuple-element.52.kv0), channel_id=1, source_target_pairs={{0,8},{8,16},{16,24},{24,0},{1,9},{9,17},{17,25},{25,1},{2,10},{10... | collective-permute-start | bytes 393224 | tf_op jit(solution)/shard_map/ppermute | solution.py:262
  23.4 10.4 %collective-permute-start.4 = (bf16[256,256]{1,0:T(8,128)(2,1)}, bf16[256,256]{1,0:T(8,128)(2,1)}, u32[]{:S(2)}, u32[]{:S(2)}) collective-permute-start(bf16[256,256]{1,0:T(8,128)(2,1)} %get-tuple-element.52.kv0), channel_id=1, source_target_pairs={{0,16},{8,24},{16,0},{24,8},{1,17},{9,25},{17,1},{25,9},{2,18},{10... | collective-permute-start | bytes 393224 | tf_op jit(solution)/shard_map/ppermute | solution.py:262
  26.3 7.5 %collective-permute-start.3 = (bf16[256,256]{1,0:T(8,128)(2,1)}, bf16[256,256]{1,0:T(8,128)(2,1)}, u32[]{:S(2)}, u32[]{:S(2)}) collective-permute-start(bf16[256,256]{1,0:T(8,128)(2,1)} %get-tuple-element.52.kv0), channel_id=1, source_target_pairs={{0,24},{8,0},{16,8},{24,16},{1,25},{9,1},{17,9},{25,17},{2,26},{10... | collective-permute-start | bytes 393224 | tf_op jit(solution)/shard_map/ppermute | solution.py:262
  27.7 23.8 %copy-start.4 = (s32[16]{0:T(128)S(1)}, s32[16]{0:T(128)}, u32[]{:S(2)}) copy-start(s32[16]{0:T(128)} %lengths.3) | copy-start | bytes 196
  27.7 21.7 %collective-permute-start.12 = (bf16[256,256]{1,0:T(8,128)(2,1)S(1)}, bf16[256,256]{1,0:T(8,128)(2,1)S(1)}, u32[]{:S(2)}, u32[]{:S(2)}) collective-permute-start(bf16[256,256]{1,0:T(8,128)(2,1)S(1)} %get-tuple-element.58.kv0), channel_id=1, source_target_pairs={{0,8},{8,16},{16,24},{24,0},{1,9},{9,17},{17,25},{25,1},{2,10},{10... | collective-permute-start | bytes 393224 | tf_op jit(solution)/shard_map/ppermute | solution.py:262
  29.3 22.2 %collective-permute-start.11 = (bf16[256,256]{1,0:T(8,128)(2,1)S(1)}, bf16[256,256]{1,0:T(8,128)(2,1)S(1)}, u32[]{:S(2)}, u32[]{:S(2)}) collective-permute-start(bf16[256,256]{1,0:T(8,128)(2,1)S(1)} %get-tuple-element.58.kv0), channel_id=1, source_target_pairs={{0,16},{8,24},{16,0},{24,8},{1,17},{9,25},{17,1},{25,9},{2,18},{10... | collective-permute-start | bytes 393224 | tf_op jit(solution)/shard_map/ppermute | solution.py:262
  33.8 17.7 %collective-permute-start.10 = (bf16[256,256]{1,0:T(8,128)(2,1)S(1)}, bf16[256,256]{1,0:T(8,128)(2,1)S(1)}, u32[]{:S(2)}, u32[]{:S(2)}) collective-permute-start(bf16[256,256]{1,0:T(8,128)(2,1)S(1)} %get-tuple-element.58.kv0), channel_id=1, source_target_pairs={{0,24},{8,0},{16,8},{24,16},{1,25},{9,1},{17,9},{25,17},{2,26},{10... | collective-permute-start | bytes 393224 | tf_op jit(solution)/shard_map/ppermute | solution.py:262
  46.0 11.3 %collective-permute-start.7 = (bf16[256,256]{1,0:T(8,128)(2,1)S(1)}, bf16[256,256]{1,0:T(8,128)(2,1)S(1)}, u32[]{:S(2)}, u32[]{:S(2)}) collective-permute-start(bf16[256,256]{1,0:T(8,128)(2,1)S(1)} %get-tuple-element.55), channel_id=1, source_target_pairs={{0,8},{8,16},{16,24},{24,0},{1,9},{9,17},{17,25},{25,1},{2,10},{10... | collective-permute-start | bytes 393224 | tf_op jit(solution)/shard_map/ppermute | solution.py:262
  48.1 9.3 %collective-permute-start.8 = (bf16[256,256]{1,0:T(8,128)(2,1)S(1)}, bf16[256,256]{1,0:T(8,128)(2,1)S(1)}, u32[]{:S(2)}, u32[]{:S(2)}) collective-permute-start(bf16[256,256]{1,0:T(8,128)(2,1)S(1)} %get-tuple-element.56), channel_id=1, source_target_pairs={{0,16},{8,24},{16,0},{24,8},{1,17},{9,25},{17,1},{25,9},{2,18},{10... | collective-permute-start | bytes 393224 | tf_op jit(solution)/shard_map/ppermute | solution.py:262
  49.4 7.9 %collective-permute-start.9 = (bf16[256,256]{1,0:T(8,128)(2,1)S(1)}, bf16[256,256]{1,0:T(8,128)(2,1)S(1)}, u32[]{:S(2)}, u32[]{:S(2)}) collective-permute-start(bf16[256,256]{1,0:T(8,128)(2,1)S(1)} %get-tuple-element.57), channel_id=1, source_target_pairs={{0,24},{8,0},{16,8},{24,16},{1,25},{9,1},{17,9},{25,17},{2,26},{10... | collective-permute-start | bytes 393224 | tf_op jit(solution)/shard_map/ppermute | solution.py:262
  57.4 10.4 %collective-permute-start.16 = (f32[128,2048]{1,0:T(8,128)S(1)}, f32[128,2048]{1,0:T(8,128)S(1)}, u32[]{:S(2)}, u32[]{:S(2)}) collective-permute-start(f32[128,2048]{1,0:T(8,128)S(1)} %get-tuple-element.66), channel_id=1, source_target_pairs={{0,1},{1,0},{2,3},{3,2},{4,5},{5,4},{6,7},{7,6},{8,9},{9,8},{10,11... | collective-permute-start | bytes 3145736 | tf_op jit(solution)/shard_map/ppermute | solution.py:262
  57.6 10.0 %collective-permute-start.15 = (bf16[64,256]{1,0:T(8,128)(2,1)S(1)}, bf16[64,256]{1,0:T(8,128)(2,1)S(1)}, u32[]{:S(2)}, u32[]{:S(2)}) collective-permute-start(bf16[64,256]{1,0:T(8,128)(2,1)S(1)} %get-tuple-element.94), channel_id=1, source_target_pairs={{0,6},{2,0},{4,2},{6,4},{1,7},{3,1},{5,3},{7,5},{8,14},{10,8},{12,... | collective-permute-start | bytes 98312 | tf_op jit(solution)/shard_map/ppermute | solution.py:262
  57.9 9.7 %collective-permute-start.14 = (bf16[64,256]{1,0:T(8,128)(2,1)S(1)}, bf16[64,256]{1,0:T(8,128)(2,1)S(1)}, u32[]{:S(2)}, u32[]{:S(2)}) collective-permute-start(bf16[64,256]{1,0:T(8,128)(2,1)S(1)} %get-tuple-element.95), channel_id=1, source_target_pairs={{0,4},{2,6},{4,0},{6,2},{1,5},{3,7},{5,1},{7,3},{8,12},{10,14},{12... | collective-permute-start | bytes 98312 | tf_op jit(solution)/shard_map/ppermute | solution.py:262
  61.7 6.0 %collective-permute-start.13 = (bf16[64,256]{1,0:T(8,128)(2,1)S(1)}, bf16[64,256]{1,0:T(8,128)(2,1)S(1)}, u32[]{:S(2)}, u32[]{:S(2)}) collective-permute-start(bf16[64,256]{1,0:T(8,128)(2,1)S(1)} %get-tuple-element.96), channel_id=1, source_target_pairs={{0,2},{2,4},{4,6},{6,0},{1,3},{3,5},{5,7},{7,1},{8,10},{10,12},{12... | collective-permute-start | bytes 98312 | tf_op jit(solution)/shard_map/ppermute | solution.py:262
  67.7 9.4 %collective-permute-start.20 = (bf16[256,256]{1,0:T(8,128)(2,1)S(1)}, bf16[256,256]{1,0:T(8,128)(2,1)S(1)}, u32[]{:S(2)}, u32[]{:S(2)}) collective-permute-start(bf16[256,256]{1,0:T(8,128)(2,1)S(1)} %get-tuple-element.86), channel_id=1, source_target_pairs={{0,8},{8,16},{16,24},{24,0},{1,9},{9,17},{17,25},{25,1},{2,10},{10... | collective-permute-start | bytes 393224 | tf_op jit(solution)/shard_map/ppermute | solution.py:262
  67.7 9.4 %collective-permute-start.21 = (bf16[256,256]{1,0:T(8,128)(2,1)S(1)}, bf16[256,256]{1,0:T(8,128)(2,1)S(1)}, u32[]{:S(2)}, u32[]{:S(2)}) collective-permute-start(bf16[256,256]{1,0:T(8,128)(2,1)S(1)} %get-tuple-element.87), channel_id=1, source_target_pairs={{0,16},{8,24},{16,0},{24,8},{1,17},{9,25},{17,1},{25,9},{2,18},{10... | collective-permute-start | bytes 393224 | tf_op jit(solution)/shard_map/ppermute | solution.py:262
  69.9 7.6 %collective-permute-start.22 = (bf16[256,256]{1,0:T(8,128)(2,1)S(1)}, bf16[256,256]{1,0:T(8,128)(2,1)S(1)}, u32[]{:S(2)}, u32[]{:S(2)}) collective-permute-start(bf16[256,256]{1,0:T(8,128)(2,1)S(1)} %get-tuple-element.88), channel_id=1, source_target_pairs={{0,24},{8,0},{16,8},{24,16},{1,25},{9,1},{17,9},{25,17},{2,26},{10... | collective-permute-start | bytes 393224 | tf_op jit(solution)/shard_map/ppermute | solution.py:262
  71.2 4.4 %collective-permute-start.17 = (f32[64,256]{1,0:T(8,128)S(1)}, f32[64,256]{1,0:T(8,128)S(1)}, u32[]{:S(2)}, u32[]{:S(2)}) collective-permute-start(f32[64,256]{1,0:T(8,128)S(1)} %convert_add_fusion.1), channel_id=1, source_target_pairs={{0,32},{32,0},{64,96},{96,64},{1,33},{33,1},{65,97},{97,65},{2,34}... | collective-permute-start | bytes 196616 | tf_op jit(solution)/shard_map/ppermute | solution.py:373
  75.5 11.1 %collective-permute-start.18 = (f32[64,256]{1,0:T(8,128)S(1)}, f32[64,256]{1,0:T(8,128)S(1)}, u32[]{:S(2)}, u32[]{:S(2)}) collective-permute-start(f32[64,256]{1,0:T(8,128)S(1)} %add.55), channel_id=1, source_target_pairs={{0,96},{96,0},{32,64},{64,32},{1,97},{97,1},{33,65},{65,33},{2,98}... | collective-permute-start | bytes 196616 | tf_op jit(solution)/shard_map/ppermute | solution.py:376
  77.7 10.1 %collective-permute-start.23 = (bf16[2,32,256]{2,1,0:T(8,128)(2,1)S(1)}, bf16[2,32,256]{2,1,0:T(8,128)(2,1)S(1)}, u32[]{:S(2)}, u32[]{:S(2)}) collective-permute-start(bf16[2,32,256]{2,1,0:T(8,128)(2,1)S(1)} %bitcast.16), channel_id=1, source_target_pairs={{0,2},{2,4},{4,6},{6,0},{1,3},{3,5},{5,7},{7,1},{8,10},{10,12},{12... | collective-permute-start | bytes 98312 | tf_op jit(solution)/shard_map/ppermute | solution.py:262
  80.5 7.2 %collective-permute-start.25 = (bf16[2,32,256]{2,1,0:T(8,128)(2,1)S(1)}, bf16[2,32,256]{2,1,0:T(8,128)(2,1)S(1)}, u32[]{:S(2)}, u32[]{:S(2)}) collective-permute-start(bf16[2,32,256]{2,1,0:T(8,128)(2,1)S(1)} %bitcast.15), channel_id=1, source_target_pairs={{0,6},{2,0},{4,2},{6,4},{1,7},{3,1},{5,3},{7,5},{8,14},{10,8},{12,... | collective-permute-start | bytes 98312 | tf_op jit(solution)/shard_map/ppermute | solution.py:262
  81.9 7.8 %collective-permute-start.24 = (bf16[2,32,256]{2,1,0:T(8,128)(2,1)S(1)}, bf16[2,32,256]{2,1,0:T(8,128)(2,1)S(1)}, u32[]{:S(2)}, u32[]{:S(2)}) collective-permute-start(bf16[2,32,256]{2,1,0:T(8,128)(2,1)S(1)} %bitcast.14), channel_id=1, source_target_pairs={{0,4},{2,6},{4,0},{6,2},{1,5},{3,7},{5,1},{7,3},{8,12},{10,14},{12... | collective-permute-start | bytes 98312 | tf_op jit(solution)/shard_map/ppermute | solution.py:262
  86.6 4.4 %collective-permute-start.19 = (f32[64,256]{1,0:T(8,128)S(1)}, f32[64,256]{1,0:T(8,128)S(1)}, u32[]{:S(2)}, u32[]{:S(2)}) collective-permute-start(f32[64,256]{1,0:T(8,128)S(1)} %add.56), channel_id=1, source_target_pairs={{0,128},{128,0},{1,129},{129,1},{2,130},{130,2},{3,131},{131,3},{4... | collective-permute-start | bytes 196616 | tf_op jit(solution)/shard_map/ppermute | solution.py:262

commit v7 on v6

--- a/solution.py
+++ b/solution.py
@@ -75,12 +75,14 @@
 
 
 def prepare_kernel(
-    seg_branch, q_hbm, o_hbm, g_hbm, norm_ref, leaf_ref, seg_ref,
-    qg_ref, onehot_ref, grad_ref, dq_ref, q_ref, o_ref, g_ref, stat_ref, sems,
+    seg_branch, q_hbm, o_hbm, g_hbm, leaf_hbm, norm_ref, seg_ref,
+    qg_ref, onehot_ref, grad_ref, dq_ref, q_ref, o_ref, g_ref, leaf_ref, stat_ref, sems,
 ):
     copies = [
         pltpu.make_async_copy(source, target, sems.at[i])
-        for i, (source, target) in enumerate(((q_hbm, q_ref), (g_hbm, g_ref), (o_hbm, o_ref)))
+        for i, (source, target) in enumerate(
+            ((q_hbm, q_ref), (g_hbm, g_ref), (o_hbm, o_ref), (leaf_hbm, leaf_ref))
+        )
     ]
     for copy in copies:
         copy.start()
@@ -131,6 +133,7 @@
     read_stats(qg_ref, stat_ref)
     place = place.astype(jnp.int32)
 
+    copies[3].wait()
     keys = leaf_ref[:, :HD]
     values = leaf_ref[:, HD:]
     keys_t = keys.T
@@ -254,6 +257,10 @@
         out_ref[:, h * HD : (h + 1) * HD] = dot(onehot_ref[...], column, 0, 0).astype(BF)
 
 
+def in_hbm(value):
+    return pltpu.with_memory_space_constraint(value, pltpu.HBM)
+
+
 def shape(dims, dtype):
     return jax.ShapeDtypeStruct(dims, dtype)
 
@@ -292,13 +299,14 @@
             shape((TOK, 2 * HD), F32),
             shape((HD, ROWS), F32),
         ),
-        in_specs=[SMEM] + [HBM] * 3 + [VMEM] * 3,
+        in_specs=[SMEM] + [HBM] * 4 + [VMEM] * 2,
         out_specs=(VMEM,) * 4,
-        scratch_shapes=[pltpu.VMEM((TOK, HEADS * HD), BF)] * 3 + [stats, pltpu.SemaphoreType.DMA((3,))],
+        scratch_shapes=[pltpu.VMEM((TOK, HEADS * HD), BF)] * 3
+        + [pltpu.VMEM((TOK, 2 * HD), BF), stats, pltpu.SemaphoreType.DMA((4,))],
         compiler_params=PARAMS,
         cost_estimate=pl.CostEstimate(flops=4_000_000_000, bytes_accessed=5_000_000, transcendentals=0),
         name="prepare",
-    )(segment_branch, *(pltpu.with_memory_space_constraint(x, pltpu.HBM) for x in (queries, attn_out, out_grad)), log_norm.T, leaf_kv, segment_ids)
+    )(in_hbm(segment_branch), *(in_hbm(x) for x in (queries, attn_out, out_grad, leaf_kv, log_norm.T, segment_ids)))
     pieces, qg0 = lax.optimization_barrier((gather(shard, "zh", NZ), qg0))
     root_z, branch_z = pl.pallas_call(
         pack_kernel,

time: 92.4 us -> 90.4 us (0.978)
  local copies, waits for them, and re-layouts: 2.96 us -> 0.03 us
    unnamed x10 -> x2, local copies, waits for them, and re-layouts: 2.94 us -> 0.01 us
  transfers between devices with their start and end apart: 26 -> 26, of which waited for: 6 -> 4; matrix products, arithmetic and copies ran while one was open for 1% -> 1% of each run, Pallas kernels for 34% -> 35%
where the time goes in v7:
time: 90.4 us; the launch traced here: 89.6 us
  starting transfers between devices  48.1 us (53%)
  Pallas kernels  31.6 us (35%)
  waiting for transfers between devices  6.71 us (7%)
  other arithmetic  2.33 us (3%)
    ppermute x24, starting transfers between devices, shift(): lax.ppermute(value, axis, [(i, (i + by) % size) for i in range(size)])  45.9 us
    pallas_call x1, Pallas kernels, shards(): pl.pallas_call(root_kernel, out_shape=(dq_shape, dq_shape, block, block,...  12.2 us
    pallas_call x1, Pallas kernels, shards(): pl.pallas_call(branch_other_kernel, out_shape=(dq_shape, shape((2 * KB, 2...  5.83 us
    pallas_call x1, Pallas kernels, shards(): pl.pallas_call(branch_own_kernel, out_shape=(dq_shape, block, block, bloc...  5.73 us
    pallas_call x1, Pallas kernels, shards(): pl.pallas_call(prepare_kernel, out_shape=(shape((2 * ROWS + STATS, HD), B...  5.61 us
    ppermute x24, waiting for transfers between devices, shift(): lax.ppermute(value, axis, [(i, (i + by) % size) for i in range(size)])  4.53 us
    ppermute x1, waiting for transfers between devices, shards(): pair = lax.ppermute(root_part, 'x', [(0, 1), (1, 0), (2, 3), (3, 2)])  2.17 us
  transfers between devices with their start and end apart: 26, of which 4 were waited for; matrix products, arithmetic and copies ran while one was open for 1% of the time, Pallas kernels for 35%

profile of v7, /device:TPU:2, one launch (start us, length us, event | category | flops | bytes accessed | tf_op | source)
XLA Modules:
  0.0 89.6 jit_solution(1136957859236295524)
XLA Ops:
  0.6 0.8 pad_maximum_fusion.z0
  1.4 3.3 %collective-permute-start.2 = (bf16[128,256]{1,0:T(8,128)(2,1)S(1)}, bf16[128,256]{1,0:T(8,128)(2,1)S(1)}, u32[]{:S(2)}, u32[]{:S(2)}) collective-permute-start(bf16[128,256]{1,0:T(8,128)(2,1)S(1)} %pad_maximum_fusion.z0), channel_id=1, source_target_pairs={{0,2},{2,4},{4,6},{6,0},{1,3},{3,5},{5,7},{7,1},{8,10},{10,12},{12... | collective-permute-start | bytes 196616 | tf_op jit(solution)/shard_map/ppermute | solution.py:269
  4.7 5.4 %collective-permute-start.1 = (bf16[128,256]{1,0:T(8,128)(2,1)S(1)}, bf16[128,256]{1,0:T(8,128)(2,1)S(1)}, u32[]{:S(2)}, u32[]{:S(2)}) collective-permute-start(bf16[128,256]{1,0:T(8,128)(2,1)S(1)} %pad_maximum_fusion.z0), channel_id=1, source_target_pairs={{0,4},{2,6},{4,0},{6,2},{1,5},{3,7},{5,1},{7,3},{8,12},{10,14},{12... | collective-permute-start | bytes 196616 | tf_op jit(solution)/shard_map/ppermute | solution.py:269
  10.1 2.7 %collective-permute-start = (bf16[128,256]{1,0:T(8,128)(2,1)S(1)}, bf16[128,256]{1,0:T(8,128)(2,1)S(1)}, u32[]{:S(2)}, u32[]{:S(2)}) collective-permute-start(bf16[128,256]{1,0:T(8,128)(2,1)S(1)} %pad_maximum_fusion.z0), channel_id=1, source_target_pairs={{0,6},{2,0},{4,2},{6,4},{1,7},{3,1},{5,3},{7,5},{8,14},{10,8},{12,... | collective-permute-start | bytes 196616 | tf_op jit(solution)/shard_map/ppermute | solution.py:269
  12.7 5.6 %prepare.1 = (bf16[4224,128]{1,0:T(8,128)(2,1)S(1)}, bf16[256,256]{1,0:T(8,128)(2,1)S(1)}, f32[256,256]{1,0:T(8,128)}, f32[128,2048]{1,0:T(8,128)S(1)}) custom-call(s32[1,8]{1,0:T(1,128)} %seg_branch.1, bf16[256,1024]{1,0:T(8,128)(2,1)} %q_hbm.1, bf16[256,1024]{1,0:T(8,128)(2,1)} %o_hbm.1, bf16[256,1024]{1,0:T(8,128)(2,1)} %g_hbm.1, ...), custom_call_target="tpu_custom_call" | custom-call | flops 4000000000 | bytes 5000000 | tf_op jit(solution)/shard_map/prepare/pallas_call | solution.py:294
  18.4 0.0 collective-permute-done.2.z3
  18.4 0.0 collective-permute-done.1.z2
  18.4 0.0 collective-permute-done.z1
  18.4 0.1 collective-permute-start.6
  18.5 0.7 pack.1
  19.2 1.6 %collective-permute-start.5 = (bf16[256,256]{1,0:T(8,128)(2,1)}, bf16[256,256]{1,0:T(8,128)(2,1)}, u32[]{:S(2)}, u32[]{:S(2)}) collective-permute-start(bf16[256,256]{1,0:T(8,128)(2,1)} %get-tuple-element.52.kv0), channel_id=1, source_target_pairs={{0,8},{8,16},{16,24},{24,0},{1,9},{9,17},{17,25},{25,1},{2,10},{10... | collective-permute-start | bytes 393224 | tf_op jit(solution)/shard_map/ppermute | solution.py:269
  20.7 2.9 %collective-permute-start.4 = (bf16[256,256]{1,0:T(8,128)(2,1)}, bf16[256,256]{1,0:T(8,128)(2,1)}, u32[]{:S(2)}, u32[]{:S(2)}) collective-permute-start(bf16[256,256]{1,0:T(8,128)(2,1)} %get-tuple-element.52.kv0), channel_id=1, source_target_pairs={{0,16},{8,24},{16,0},{24,8},{1,17},{9,25},{17,1},{25,9},{2,18},{10... | collective-permute-start | bytes 393224 | tf_op jit(solution)/shard_map/ppermute | solution.py:269
  23.6 1.3 %collective-permute-start.3 = (bf16[256,256]{1,0:T(8,128)(2,1)}, bf16[256,256]{1,0:T(8,128)(2,1)}, u32[]{:S(2)}, u32[]{:S(2)}) collective-permute-start(bf16[256,256]{1,0:T(8,128)(2,1)} %get-tuple-element.52.kv0), channel_id=1, source_target_pairs={{0,24},{8,0},{16,8},{24,16},{1,25},{9,1},{17,9},{25,17},{2,26},{10... | collective-permute-start | bytes 393224 | tf_op jit(solution)/shard_map/ppermute | solution.py:269
  25.0 0.1 pad_add_fusion.place
  25.1 0.7 collective-permute-start.12
  25.8 0.9 collective-permute-done.5.kv3
  26.6 4.5 %collective-permute-start.11 = (bf16[256,256]{1,0:T(8,128)(2,1)S(1)}, bf16[256,256]{1,0:T(8,128)(2,1)S(1)}, u32[]{:S(2)}, u32[]{:S(2)}) collective-permute-start(bf16[256,256]{1,0:T(8,128)(2,1)S(1)} %get-tuple-element.58.kv0), channel_id=1, source_target_pairs={{0,16},{8,24},{16,0},{24,8},{1,17},{9,25},{17,1},{25,9},{2,18},{10... | collective-permute-start | bytes 393224 | tf_op jit(solution)/shard_map/ppermute | solution.py:269
  31.1 0.0 collective-permute-done.4.kv2
  31.1 0.0 collective-permute-start.10
  31.1 0.0 collective-permute-done.3.kv1
  31.1 0.0 collective-permute-done.6.qg1.qg_ref
  31.2 12.2 %root.1 = (f32[128,2048]{1,0:T(8,128)S(1)}, f32[128,2048]{1,0:T(8,128)S(1)}, bf16[256,256]{1,0:T(8,128)(2,1)S(1)}, bf16[256,256]{1,0:T(8,128)(2,1)S(1)}, bf16[25...) custom-call(bf16[256,256]{1,0:T(8,128)(2,1)} %get-tuple-element.52.kv0, bf16[256,256]{1,0:T(8,128)(2,1)} %collective-permute-done.3.kv1, ...), custom_call_target="tpu_custom_call" | custom-call | flops 10000000000 | bytes 8000000 | tf_op jit(solution)/shard_map/root/pallas_call | solution.py:328
  43.4 2.1 %collective-permute-start.7 = (bf16[256,256]{1,0:T(8,128)(2,1)S(1)}, bf16[256,256]{1,0:T(8,128)(2,1)S(1)}, u32[]{:S(2)}, u32[]{:S(2)}) collective-permute-start(bf16[256,256]{1,0:T(8,128)(2,1)S(1)} %get-tuple-element.55), channel_id=1, source_target_pairs={{0,8},{8,16},{16,24},{24,0},{1,9},{9,17},{17,25},{25,1},{2,10},{10... | collective-permute-start | bytes 393224 | tf_op jit(solution)/shard_map/ppermute | solution.py:269
  45.4 1.3 %collective-permute-start.8 = (bf16[256,256]{1,0:T(8,128)(2,1)S(1)}, bf16[256,256]{1,0:T(8,128)(2,1)S(1)}, u32[]{:S(2)}, u32[]{:S(2)}) collective-permute-start(bf16[256,256]{1,0:T(8,128)(2,1)S(1)} %get-tuple-element.56), channel_id=1, source_target_pairs={{0,16},{8,24},{16,0},{24,8},{1,17},{9,25},{17,1},{25,9},{2,18},{10... | collective-permute-start | bytes 393224 | tf_op jit(solution)/shard_map/ppermute | solution.py:269
  46.8 0.0 collective-permute-done.12.kv3
  46.8 2.1 %collective-permute-start.9 = (bf16[256,256]{1,0:T(8,128)(2,1)S(1)}, bf16[256,256]{1,0:T(8,128)(2,1)S(1)}, u32[]{:S(2)}, u32[]{:S(2)}) collective-permute-start(bf16[256,256]{1,0:T(8,128)(2,1)S(1)} %get-tuple-element.57), channel_id=1, source_target_pairs={{0,24},{8,0},{16,8},{24,16},{1,25},{9,1},{17,9},{25,17},{2,26},{10... | collective-permute-start | bytes 393224 | tf_op jit(solution)/shard_map/ppermute | solution.py:269
  48.8 0.0 collective-permute-done.11.kv2
  48.8 0.0 collective-permute-done.10.kv1
  48.9 5.8 %branch_other.1 = (f32[128,2048]{1,0:T(8,128)S(1)}, bf16[1024,256]{1,0:T(8,128)(2,1)S(1)}, f32[1024,256]{1,0:T(8,128)S(1)}) custom-call(s32[4]{0:T(128)S(1)} %pad_add_fusion.place, s32[16]{0:T(128)S(1)} %copy-done, bf16[256,256]{1,0:T(8,128)(2,1)S(1)} %get-tuple-element.58.kv0, ...), custom_call_target="tpu_custom_call", output_to_operand_aliasing={{0}: (7, {})} | custom-call | flops 4499999744 | bytes 5000000 | tf_op jit(solution)/shard_map/branch_other/pallas_call | solution.py:341
  54.7 0.0 collective-permute-done.7
  54.7 0.0 collective-permute-done.8
  54.7 0.0 collective-permute-done.9
  54.7 0.1 collective-permute-start.16
  54.8 0.1 add_convert_fusion.1
  54.9 2.2 %collective-permute-start.15 = (bf16[64,256]{1,0:T(8,128)(2,1)S(1)}, bf16[64,256]{1,0:T(8,128)(2,1)S(1)}, u32[]{:S(2)}, u32[]{:S(2)}) collective-permute-start(bf16[64,256]{1,0:T(8,128)(2,1)S(1)} %get-tuple-element.94), channel_id=1, source_target_pairs={{0,6},{2,0},{4,2},{6,4},{1,7},{3,1},{5,3},{7,5},{8,14},{10,8},{12,... | collective-permute-start | bytes 98312 | tf_op jit(solution)/shard_map/ppermute | solution.py:269
  57.1 2.2 %collective-permute-start.14 = (bf16[64,256]{1,0:T(8,128)(2,1)S(1)}, bf16[64,256]{1,0:T(8,128)(2,1)S(1)}, u32[]{:S(2)}, u32[]{:S(2)}) collective-permute-start(bf16[64,256]{1,0:T(8,128)(2,1)S(1)} %get-tuple-element.95), channel_id=1, source_target_pairs={{0,4},{2,6},{4,0},{6,2},{1,5},{3,7},{5,1},{7,3},{8,12},{10,14},{12... | collective-permute-start | bytes 98312 | tf_op jit(solution)/shard_map/ppermute | solution.py:269
  59.3 1.3 %collective-permute-start.13 = (bf16[64,256]{1,0:T(8,128)(2,1)S(1)}, bf16[64,256]{1,0:T(8,128)(2,1)S(1)}, u32[]{:S(2)}, u32[]{:S(2)}) collective-permute-start(bf16[64,256]{1,0:T(8,128)(2,1)S(1)} %get-tuple-element.96), channel_id=1, source_target_pairs={{0,2},{2,4},{4,6},{6,0},{1,3},{3,5},{5,7},{7,1},{8,10},{10,12},{12... | collective-permute-start | bytes 98312 | tf_op jit(solution)/shard_map/ppermute | solution.py:269
  60.6 5.7 %branch_own.1 = (f32[128,2048]{1,0:T(8,128)S(1)}, bf16[256,256]{1,0:T(8,128)(2,1)S(1)}, bf16[256,256]{1,0:T(8,128)(2,1)S(1)}, bf16[256,256]{1,0:T(8,128)(2,1)S(1)}, bf16[256,256]{1,0:T(8,128)(2,1)S(1)}) custom-call(s32[4]{0:T(128)S(1)} %pad_add_fusion.place, s32[16]{0:T(128)S(1)} %copy-done, ...), custom_call_target="tpu_custom_call", output_to_operand_aliasing={{0}: (5, {})} | custom-call | flops 4499999744 | bytes 5000000 | tf_op jit(solution)/shard_map/branch_own/pallas_call | solution.py:357
  66.3 0.0 collective-permute-done.15
  66.3 0.0 collective-permute-done.14
  66.3 0.0 collective-permute-done.13
  66.3 0.0 collective-permute-done.16.other
  66.3 0.1 collective-permute-start.20
  66.4 2.2 %collective-permute-start.21 = (bf16[256,256]{1,0:T(8,128)(2,1)S(1)}, bf16[256,256]{1,0:T(8,128)(2,1)S(1)}, u32[]{:S(2)}, u32[]{:S(2)}) collective-permute-start(bf16[256,256]{1,0:T(8,128)(2,1)S(1)} %get-tuple-element.87), channel_id=1, source_target_pairs={{0,16},{8,24},{16,0},{24,8},{1,17},{9,25},{17,1},{25,9},{2,18},{10... | collective-permute-start | bytes 393224 | tf_op jit(solution)/shard_map/ppermute | solution.py:269
  68.6 1.2 %collective-permute-start.22 = (bf16[256,256]{1,0:T(8,128)(2,1)S(1)}, bf16[256,256]{1,0:T(8,128)(2,1)S(1)}, u32[]{:S(2)}, u32[]{:S(2)}) collective-permute-start(bf16[256,256]{1,0:T(8,128)(2,1)S(1)} %get-tuple-element.88), channel_id=1, source_target_pairs={{0,24},{8,0},{16,8},{24,16},{1,25},{9,1},{17,9},{25,17},{2,26},{10... | collective-permute-start | bytes 393224 | tf_op jit(solution)/shard_map/ppermute | solution.py:269
  69.9 0.6 collective-permute-start.17
  70.5 1.6 %finish.1 = bf16[256,1024]{1,0:T(8,128)(2,1)} custom-call(bf16[256,256]{1,0:T(8,128)(2,1)S(1)} %get-tuple-element.79.onehot_ref, f32[128,2048]{1,0:T(8,128)S(1)} %get-tuple-element.80.leaf, f32[128,2048]{1,0:T(8,128)S(1)} %get-tuple-element.81.mine, f32[128,2048]{1,0:T(8,128)S(1)} %collective-permute-done.16.other), custom_call_target="tpu_custom_call" | custom-call | flops 200000000 | bytes 3000000 | tf_op jit(solution)/shard_map/finish/pallas_call | solution.py:371
  72.0 2.2 %collective-permute-done.17 = f32[64,256]{1,0:T(8,128)S(1)} collective-permute-done((f32[64,256]{1,0:T(8,128)S(1)}, f32[64,256]{1,0:T(8,128)S(1)}, u32[]{:S(2)}, u32[]{:S(2)}) %collective-permute-start.17) | collective-permute-done | bytes 65568 | tf_op jit(solution)/shard_map/ppermute | solution.py:381
  74.2 1.6 %collective-permute-start.18 = (f32[64,256]{1,0:T(8,128)S(1)}, f32[64,256]{1,0:T(8,128)S(1)}, u32[]{:S(2)}, u32[]{:S(2)}) collective-permute-start(f32[64,256]{1,0:T(8,128)S(1)} %add.55), channel_id=1, source_target_pairs={{0,96},{96,0},{32,64},{64,32},{1,97},{97,1},{33,65},{65,33},{2,98}... | collective-permute-start | bytes 196616 | tf_op jit(solution)/shard_map/ppermute | solution.py:384
  75.8 0.0 collective-permute-done.20
  75.8 0.0 collective-permute-done.21
  75.8 0.3 collective-permute-done.22
  76.1 0.1 add_convert_fusion
  76.2 3.2 %collective-permute-start.23 = (bf16[2,32,256]{2,1,0:T(8,128)(2,1)S(1)}, bf16[2,32,256]{2,1,0:T(8,128)(2,1)S(1)}, u32[]{:S(2)}, u32[]{:S(2)}) collective-permute-start(bf16[2,32,256]{2,1,0:T(8,128)(2,1)S(1)} %bitcast.15), channel_id=1, source_target_pairs={{0,2},{2,4},{4,6},{6,0},{1,3},{3,5},{5,7},{7,1},{8,10},{10,12},{12... | collective-permute-start | bytes 98312 | tf_op jit(solution)/shard_map/ppermute | solution.py:269
  79.4 1.1 %collective-permute-start.25 = (bf16[2,32,256]{2,1,0:T(8,128)(2,1)S(1)}, bf16[2,32,256]{2,1,0:T(8,128)(2,1)S(1)}, u32[]{:S(2)}, u32[]{:S(2)}) collective-permute-start(bf16[2,32,256]{2,1,0:T(8,128)(2,1)S(1)} %bitcast.14), channel_id=1, source_target_pairs={{0,6},{2,0},{4,2},{6,4},{1,7},{3,1},{5,3},{7,5},{8,14},{10,8},{12,... | collective-permute-start | bytes 98312 | tf_op jit(solution)/shard_map/ppermute | solution.py:269
  80.4 3.5 %collective-permute-start.24 = (bf16[2,32,256]{2,1,0:T(8,128)(2,1)S(1)}, bf16[2,32,256]{2,1,0:T(8,128)(2,1)S(1)}, u32[]{:S(2)}, u32[]{:S(2)}) collective-permute-start(bf16[2,32,256]{2,1,0:T(8,128)(2,1)S(1)} %bitcast.13), channel_id=1, source_target_pairs={{0,4},{2,6},{4,0},{6,2},{1,5},{3,7},{5,1},{7,3},{8,12},{10,14},{12... | collective-permute-start | bytes 98312 | tf_op jit(solution)/shard_map/ppermute | solution.py:269
  83.9 0.0 collective-permute-done.18
  84.0 1.1 %collective-permute-start.19 = (f32[64,256]{1,0:T(8,128)S(1)}, f32[64,256]{1,0:T(8,128)S(1)}, u32[]{:S(2)}, u32[]{:S(2)}) collective-permute-start(f32[64,256]{1,0:T(8,128)S(1)} %add.56), channel_id=1, source_target_pairs={{0,128},{128,0},{1,129},{129,1},{2,130},{130,2},{3,131},{131,3},{4... | collective-permute-start | bytes 196616 | tf_op jit(solution)/shard_map/ppermute | solution.py:269
  85.1 0.0 collective-permute-done.23
  85.1 0.0 collective-permute-done.25
  85.1 3.3 %collective-permute-done.24 = bf16[2,32,256]{2,1,0:T(8,128)(2,1)S(1)} collective-permute-done((bf16[2,32,256]{2,1,0:T(8,128)(2,1)S(1)}, bf16[2,32,256]{2,1,0:T(8,128)(2,1)S(1)}, u32[]{:S(2)}, u32[]{:S(2)}) %collective-permute-start.24) | collective-permute-done | bytes 32800 | tf_op jit(solution)/shard_map/ppermute | solution.py:269
  88.4 0.6 convert_add_fusion
  89.0 0.0 collective-permute-done.19
  89.0 0.6 add.57
  (7 shorter events, 0.1 us)
Async XLA Ops:
  1.4 16.9 %collective-permute-start.2 = (bf16[128,256]{1,0:T(8,128)(2,1)S(1)}, bf16[128,256]{1,0:T(8,128)(2,1)S(1)}, u32[]{:S(2)}, u32[]{:S(2)}) collective-permute-start(bf16[128,256]{1,0:T(8,128)(2,1)S(1)} %pad_maximum_fusion.z0), channel_id=1, source_target_pairs={{0,2},{2,4},{4,6},{6,0},{1,3},{3,5},{5,7},{7,1},{8,10},{10,12},{12... | collective-permute-start | bytes 196616 | tf_op jit(solution)/shard_map/ppermute | solution.py:269
  4.7 13.7 %collective-permute-start.1 = (bf16[128,256]{1,0:T(8,128)(2,1)S(1)}, bf16[128,256]{1,0:T(8,128)(2,1)S(1)}, u32[]{:S(2)}, u32[]{:S(2)}) collective-permute-start(bf16[128,256]{1,0:T(8,128)(2,1)S(1)} %pad_maximum_fusion.z0), channel_id=1, source_target_pairs={{0,4},{2,6},{4,0},{6,2},{1,5},{3,7},{5,1},{7,3},{8,12},{10,14},{12... | collective-permute-start | bytes 196616 | tf_op jit(solution)/shard_map/ppermute | solution.py:269
  10.1 8.3 %collective-permute-start = (bf16[128,256]{1,0:T(8,128)(2,1)S(1)}, bf16[128,256]{1,0:T(8,128)(2,1)S(1)}, u32[]{:S(2)}, u32[]{:S(2)}) collective-permute-start(bf16[128,256]{1,0:T(8,128)(2,1)S(1)} %pad_maximum_fusion.z0), channel_id=1, source_target_pairs={{0,6},{2,0},{4,2},{6,4},{1,7},{3,1},{5,3},{7,5},{8,14},{10,8},{12,... | collective-permute-start | bytes 196616 | tf_op jit(solution)/shard_map/ppermute | solution.py:269
  18.4 12.8 %collective-permute-start.6 = (bf16[4224,128]{1,0:T(8,128)(2,1)S(1)}, bf16[4224,128]{1,0:T(8,128)(2,1)S(1)}, u32[]{:S(2)}, u32[]{:S(2)}) collective-permute-start(bf16[4224,128]{1,0:T(8,128)(2,1)S(1)} %get-tuple-element.53.qg0.qg_ref), channel_id=1, source_target_pairs={{0,1},{1,0},{2,3},{3,2},{4,5},{5,4},{6,7},{7,6},{8,9},{9,8},{10,11... | collective-permute-start | bytes 3244040 | tf_op jit(solution)/shard_map/ppermute | solution.py:269
  19.2 7.5 %collective-permute-start.5 = (bf16[256,256]{1,0:T(8,128)(2,1)}, bf16[256,256]{1,0:T(8,128)(2,1)}, u32[]{:S(2)}, u32[]{:S(2)}) collective-permute-start(bf16[256,256]{1,0:T(8,128)(2,1)} %get-tuple-element.52.kv0), channel_id=1, source_target_pairs={{0,8},{8,16},{16,24},{24,0},{1,9},{9,17},{17,25},{25,1},{2,10},{10... | collective-permute-start | bytes 393224 | tf_op jit(solution)/shard_map/ppermute | solution.py:269
  20.7 10.4 %collective-permute-start.4 = (bf16[256,256]{1,0:T(8,128)(2,1)}, bf16[256,256]{1,0:T(8,128)(2,1)}, u32[]{:S(2)}, u32[]{:S(2)}) collective-permute-start(bf16[256,256]{1,0:T(8,128)(2,1)} %get-tuple-element.52.kv0), channel_id=1, source_target_pairs={{0,16},{8,24},{16,0},{24,8},{1,17},{9,25},{17,1},{25,9},{2,18},{10... | collective-permute-start | bytes 393224 | tf_op jit(solution)/shard_map/ppermute | solution.py:269
  23.6 7.5 %collective-permute-start.3 = (bf16[256,256]{1,0:T(8,128)(2,1)}, bf16[256,256]{1,0:T(8,128)(2,1)}, u32[]{:S(2)}, u32[]{:S(2)}) collective-permute-start(bf16[256,256]{1,0:T(8,128)(2,1)} %get-tuple-element.52.kv0), channel_id=1, source_target_pairs={{0,24},{8,0},{16,8},{24,16},{1,25},{9,1},{17,9},{25,17},{2,26},{10... | collective-permute-start | bytes 393224 | tf_op jit(solution)/shard_map/ppermute | solution.py:269
  25.1 23.8 %copy-start = (s32[16]{0:T(128)S(1)}, s32[16]{0:T(128)}, u32[]{:S(2)}) copy-start(s32[16]{0:T(128)} %lengths.3) | copy-start | bytes 196
  25.1 21.7 %collective-permute-start.12 = (bf16[256,256]{1,0:T(8,128)(2,1)S(1)}, bf16[256,256]{1,0:T(8,128)(2,1)S(1)}, u32[]{:S(2)}, u32[]{:S(2)}) collective-permute-start(bf16[256,256]{1,0:T(8,128)(2,1)S(1)} %get-tuple-element.58.kv0), channel_id=1, source_target_pairs={{0,8},{8,16},{16,24},{24,0},{1,9},{9,17},{17,25},{25,1},{2,10},{10... | collective-permute-start | bytes 393224 | tf_op jit(solution)/shard_map/ppermute | solution.py:269
  26.6 22.2 %collective-permute-start.11 = (bf16[256,256]{1,0:T(8,128)(2,1)S(1)}, bf16[256,256]{1,0:T(8,128)(2,1)S(1)}, u32[]{:S(2)}, u32[]{:S(2)}) collective-permute-start(bf16[256,256]{1,0:T(8,128)(2,1)S(1)} %get-tuple-element.58.kv0), channel_id=1, source_target_pairs={{0,16},{8,24},{16,0},{24,8},{1,17},{9,25},{17,1},{25,9},{2,18},{10... | collective-permute-start | bytes 393224 | tf_op jit(solution)/shard_map/ppermute | solution.py:269
  31.1 17.7 %collective-permute-start.10 = (bf16[256,256]{1,0:T(8,128)(2,1)S(1)}, bf16[256,256]{1,0:T(8,128)(2,1)S(1)}, u32[]{:S(2)}, u32[]{:S(2)}) collective-permute-start(bf16[256,256]{1,0:T(8,128)(2,1)S(1)} %get-tuple-element.58.kv0), channel_id=1, source_target_pairs={{0,24},{8,0},{16,8},{24,16},{1,25},{9,1},{17,9},{25,17},{2,26},{10... | collective-permute-start | bytes 393224 | tf_op jit(solution)/shard_map/ppermute | solution.py:269
  43.4 11.3 %collective-permute-start.7 = (bf16[256,256]{1,0:T(8,128)(2,1)S(1)}, bf16[256,256]{1,0:T(8,128)(2,1)S(1)}, u32[]{:S(2)}, u32[]{:S(2)}) collective-permute-start(bf16[256,256]{1,0:T(8,128)(2,1)S(1)} %get-tuple-element.55), channel_id=1, source_target_pairs={{0,8},{8,16},{16,24},{24,0},{1,9},{9,17},{17,25},{25,1},{2,10},{10... | collective-permute-start | bytes 393224 | tf_op jit(solution)/shard_map/ppermute | solution.py:269
  45.4 9.3 %collective-permute-start.8 = (bf16[256,256]{1,0:T(8,128)(2,1)S(1)}, bf16[256,256]{1,0:T(8,128)(2,1)S(1)}, u32[]{:S(2)}, u32[]{:S(2)}) collective-permute-start(bf16[256,256]{1,0:T(8,128)(2,1)S(1)} %get-tuple-element.56), channel_id=1, source_target_pairs={{0,16},{8,24},{16,0},{24,8},{1,17},{9,25},{17,1},{25,9},{2,18},{10... | collective-permute-start | bytes 393224 | tf_op jit(solution)/shard_map/ppermute | solution.py:269
  46.8 7.9 %collective-permute-start.9 = (bf16[256,256]{1,0:T(8,128)(2,1)S(1)}, bf16[256,256]{1,0:T(8,128)(2,1)S(1)}, u32[]{:S(2)}, u32[]{:S(2)}) collective-permute-start(bf16[256,256]{1,0:T(8,128)(2,1)S(1)} %get-tuple-element.57), channel_id=1, source_target_pairs={{0,24},{8,0},{16,8},{24,16},{1,25},{9,1},{17,9},{25,17},{2,26},{10... | collective-permute-start | bytes 393224 | tf_op jit(solution)/shard_map/ppermute | solution.py:269
  54.7 11.6 %collective-permute-start.16 = (f32[128,2048]{1,0:T(8,128)S(1)}, f32[128,2048]{1,0:T(8,128)S(1)}, u32[]{:S(2)}, u32[]{:S(2)}) collective-permute-start(f32[128,2048]{1,0:T(8,128)S(1)} %get-tuple-element.66), channel_id=1, source_target_pairs={{0,1},{1,0},{2,3},{3,2},{4,5},{5,4},{6,7},{7,6},{8,9},{9,8},{10,11... | collective-permute-start | bytes 3145736 | tf_op jit(solution)/shard_map/ppermute | solution.py:269
  54.9 11.4 %collective-permute-start.15 = (bf16[64,256]{1,0:T(8,128)(2,1)S(1)}, bf16[64,256]{1,0:T(8,128)(2,1)S(1)}, u32[]{:S(2)}, u32[]{:S(2)}) collective-permute-start(bf16[64,256]{1,0:T(8,128)(2,1)S(1)} %get-tuple-element.94), channel_id=1, source_target_pairs={{0,6},{2,0},{4,2},{6,4},{1,7},{3,1},{5,3},{7,5},{8,14},{10,8},{12,... | collective-permute-start | bytes 98312 | tf_op jit(solution)/shard_map/ppermute | solution.py:269
  57.1 9.2 %collective-permute-start.14 = (bf16[64,256]{1,0:T(8,128)(2,1)S(1)}, bf16[64,256]{1,0:T(8,128)(2,1)S(1)}, u32[]{:S(2)}, u32[]{:S(2)}) collective-permute-start(bf16[64,256]{1,0:T(8,128)(2,1)S(1)} %get-tuple-element.95), channel_id=1, source_target_pairs={{0,4},{2,6},{4,0},{6,2},{1,5},{3,7},{5,1},{7,3},{8,12},{10,14},{12... | collective-permute-start | bytes 98312 | tf_op jit(solution)/shard_map/ppermute | solution.py:269
  59.3 7.0 %collective-permute-start.13 = (bf16[64,256]{1,0:T(8,128)(2,1)S(1)}, bf16[64,256]{1,0:T(8,128)(2,1)S(1)}, u32[]{:S(2)}, u32[]{:S(2)}) collective-permute-start(bf16[64,256]{1,0:T(8,128)(2,1)S(1)} %get-tuple-element.96), channel_id=1, source_target_pairs={{0,2},{2,4},{4,6},{6,0},{1,3},{3,5},{5,7},{7,1},{8,10},{10,12},{12... | collective-permute-start | bytes 98312 | tf_op jit(solution)/shard_map/ppermute | solution.py:269
  66.3 9.5 %collective-permute-start.20 = (bf16[256,256]{1,0:T(8,128)(2,1)S(1)}, bf16[256,256]{1,0:T(8,128)(2,1)S(1)}, u32[]{:S(2)}, u32[]{:S(2)}) collective-permute-start(bf16[256,256]{1,0:T(8,128)(2,1)S(1)} %get-tuple-element.86), channel_id=1, source_target_pairs={{0,8},{8,16},{16,24},{24,0},{1,9},{9,17},{17,25},{25,1},{2,10},{10... | collective-permute-start | bytes 393224 | tf_op jit(solution)/shard_map/ppermute | solution.py:269
  66.4 9.4 %collective-permute-start.21 = (bf16[256,256]{1,0:T(8,128)(2,1)S(1)}, bf16[256,256]{1,0:T(8,128)(2,1)S(1)}, u32[]{:S(2)}, u32[]{:S(2)}) collective-permute-start(bf16[256,256]{1,0:T(8,128)(2,1)S(1)} %get-tuple-element.87), channel_id=1, source_target_pairs={{0,16},{8,24},{16,0},{24,8},{1,17},{9,25},{17,1},{25,9},{2,18},{10... | collective-permute-start | bytes 393224 | tf_op jit(solution)/shard_map/ppermute | solution.py:269
  68.6 7.5 %collective-permute-start.22 = (bf16[256,256]{1,0:T(8,128)(2,1)S(1)}, bf16[256,256]{1,0:T(8,128)(2,1)S(1)}, u32[]{:S(2)}, u32[]{:S(2)}) collective-permute-start(bf16[256,256]{1,0:T(8,128)(2,1)S(1)} %get-tuple-element.88), channel_id=1, source_target_pairs={{0,24},{8,0},{16,8},{24,16},{1,25},{9,1},{17,9},{25,17},{2,26},{10... | collective-permute-start | bytes 393224 | tf_op jit(solution)/shard_map/ppermute | solution.py:269
  69.9 4.4 %collective-permute-start.17 = (f32[64,256]{1,0:T(8,128)S(1)}, f32[64,256]{1,0:T(8,128)S(1)}, u32[]{:S(2)}, u32[]{:S(2)}) collective-permute-start(f32[64,256]{1,0:T(8,128)S(1)} %convert_add_fusion.1), channel_id=1, source_target_pairs={{0,32},{32,0},{64,96},{96,64},{1,33},{33,1},{65,97},{97,65},{2,34}... | collective-permute-start | bytes 196616 | tf_op jit(solution)/shard_map/ppermute | solution.py:381
  74.2 9.7 %collective-permute-start.18 = (f32[64,256]{1,0:T(8,128)S(1)}, f32[64,256]{1,0:T(8,128)S(1)}, u32[]{:S(2)}, u32[]{:S(2)}) collective-permute-start(f32[64,256]{1,0:T(8,128)S(1)} %add.55), channel_id=1, source_target_pairs={{0,96},{96,0},{32,64},{64,32},{1,97},{97,1},{33,65},{65,33},{2,98}... | collective-permute-start | bytes 196616 | tf_op jit(solution)/shard_map/ppermute | solution.py:384
  76.2 8.8 %collective-permute-start.23 = (bf16[2,32,256]{2,1,0:T(8,128)(2,1)S(1)}, bf16[2,32,256]{2,1,0:T(8,128)(2,1)S(1)}, u32[]{:S(2)}, u32[]{:S(2)}) collective-permute-start(bf16[2,32,256]{2,1,0:T(8,128)(2,1)S(1)} %bitcast.15), channel_id=1, source_target_pairs={{0,2},{2,4},{4,6},{6,0},{1,3},{3,5},{5,7},{7,1},{8,10},{10,12},{12... | collective-permute-start | bytes 98312 | tf_op jit(solution)/shard_map/ppermute | solution.py:269
  79.4 5.7 %collective-permute-start.25 = (bf16[2,32,256]{2,1,0:T(8,128)(2,1)S(1)}, bf16[2,32,256]{2,1,0:T(8,128)(2,1)S(1)}, u32[]{:S(2)}, u32[]{:S(2)}) collective-permute-start(bf16[2,32,256]{2,1,0:T(8,128)(2,1)S(1)} %bitcast.14), channel_id=1, source_target_pairs={{0,6},{2,0},{4,2},{6,4},{1,7},{3,1},{5,3},{7,5},{8,14},{10,8},{12,... | collective-permute-start | bytes 98312 | tf_op jit(solution)/shard_map/ppermute | solution.py:269
  80.4 7.9 %collective-permute-start.24 = (bf16[2,32,256]{2,1,0:T(8,128)(2,1)S(1)}, bf16[2,32,256]{2,1,0:T(8,128)(2,1)S(1)}, u32[]{:S(2)}, u32[]{:S(2)}) collective-permute-start(bf16[2,32,256]{2,1,0:T(8,128)(2,1)S(1)} %bitcast.13), channel_id=1, source_target_pairs={{0,4},{2,6},{4,0},{6,2},{1,5},{3,7},{5,1},{7,3},{8,12},{10,14},{12... | collective-permute-start | bytes 98312 | tf_op jit(solution)/shard_map/ppermute | solution.py:269
  84.0 5.0 %collective-permute-start.19 = (f32[64,256]{1,0:T(8,128)S(1)}, f32[64,256]{1,0:T(8,128)S(1)}, u32[]{:S(2)}, u32[]{:S(2)}) collective-permute-start(f32[64,256]{1,0:T(8,128)S(1)} %add.56), channel_id=1, source_target_pairs={{0,128},{128,0},{1,129},{129,1},{2,130},{130,2},{3,131},{131,3},{4... | collective-permute-start | bytes 196616 | tf_op jit(solution)/shard_map/ppermute | solution.py:269

commit v8 on v7

--- a/solution.py
+++ b/solution.py
@@ -318,8 +318,8 @@
         name="pack",
     )(*pieces)
     roots = gather(root_z, "y", NY)
+    qg1, branch_z = lax.optimization_barrier((shift(qg0, "c", 2, 1), branch_z))
     branches = gather(branch_z, "y", NY)
-    qg1 = shift(qg0, "c", 2, 1)
     dq_shape = shape((HD, ROWS), F32)
 
 

time: 90.4 us -> 91.3 us (level)
  waiting for transfers between devices: 6.71 us -> 7.81 us
    ppermute x24, waiting for transfers between devices: 4.53 us -> 5.62 us  [shift(): lax.ppermute(value, axis, [(i, (i + by) % size) for i in range(size)])]
where the time goes in v8:
time: 91.3 us; the launch traced here: 91 us
  starting transfers between devices  48.4 us (53%)
  Pallas kernels  31.6 us (35%)
  waiting for transfers between devices  7.81 us (9%)
  other arithmetic  2.33 us (3%)
    ppermute x24, starting transfers between devices, shift(): lax.ppermute(value, axis, [(i, (i + by) % size) for i in range(size)])  46.2 us
    pallas_call x1, Pallas kernels, shards(): pl.pallas_call(root_kernel, out_shape=(dq_shape, dq_shape, block, block,...  12.2 us
    pallas_call x1, Pallas kernels, shards(): pl.pallas_call(branch_other_kernel, out_shape=(dq_shape, shape((2 * KB, 2...  5.84 us
    pallas_call x1, Pallas kernels, shards(): pl.pallas_call(branch_own_kernel, out_shape=(dq_shape, block, block, bloc...  5.73 us
    ppermute x24, waiting for transfers between devices, shift(): lax.ppermute(value, axis, [(i, (i + by) % size) for i in range(size)])  5.62 us
    pallas_call x1, Pallas kernels, shards(): pl.pallas_call(prepare_kernel, out_shape=(shape((2 * ROWS + STATS, HD), B...  5.61 us
    ppermute x1, waiting for transfers between devices, shards(): pair = lax.ppermute(root_part, 'x', [(0, 1), (1, 0), (2, 3), (3, 2)])  2.18 us
  transfers between devices with their start and end apart: 26, of which 4 were waited for; matrix products, arithmetic and copies ran while one was open for 1% of the time, Pallas kernels for 35%

profile of v8, /device:TPU:2, one launch (start us, length us, event | category | flops | bytes accessed | tf_op | source)
XLA Modules:
  0.0 91.0 jit_solution(13822662583983330619)
XLA Ops:
  0.6 0.8 pad_maximum_fusion.z0
  1.4 3.3 %collective-permute-start.2 = (bf16[128,256]{1,0:T(8,128)(2,1)S(1)}, bf16[128,256]{1,0:T(8,128)(2,1)S(1)}, u32[]{:S(2)}, u32[]{:S(2)}) collective-permute-start(bf16[128,256]{1,0:T(8,128)(2,1)S(1)} %pad_maximum_fusion.z0), channel_id=1, source_target_pairs={{0,2},{2,4},{4,6},{6,0},{1,3},{3,5},{5,7},{7,1},{8,10},{10,12},{12... | collective-permute-start | bytes 196616 | tf_op jit(solution)/shard_map/ppermute | solution.py:269
  4.7 5.4 %collective-permute-start.1 = (bf16[128,256]{1,0:T(8,128)(2,1)S(1)}, bf16[128,256]{1,0:T(8,128)(2,1)S(1)}, u32[]{:S(2)}, u32[]{:S(2)}) collective-permute-start(bf16[128,256]{1,0:T(8,128)(2,1)S(1)} %pad_maximum_fusion.z0), channel_id=1, source_target_pairs={{0,4},{2,6},{4,0},{6,2},{1,5},{3,7},{5,1},{7,3},{8,12},{10,14},{12... | collective-permute-start | bytes 196616 | tf_op jit(solution)/shard_map/ppermute | solution.py:269
  10.1 2.7 %collective-permute-start = (bf16[128,256]{1,0:T(8,128)(2,1)S(1)}, bf16[128,256]{1,0:T(8,128)(2,1)S(1)}, u32[]{:S(2)}, u32[]{:S(2)}) collective-permute-start(bf16[128,256]{1,0:T(8,128)(2,1)S(1)} %pad_maximum_fusion.z0), channel_id=1, source_target_pairs={{0,6},{2,0},{4,2},{6,4},{1,7},{3,1},{5,3},{7,5},{8,14},{10,8},{12,... | collective-permute-start | bytes 196616 | tf_op jit(solution)/shard_map/ppermute | solution.py:269
  12.7 5.6 %prepare.1 = (bf16[4224,128]{1,0:T(8,128)(2,1)S(1)}, bf16[256,256]{1,0:T(8,128)(2,1)S(1)}, f32[256,256]{1,0:T(8,128)}, f32[128,2048]{1,0:T(8,128)S(1)}) custom-call(s32[1,8]{1,0:T(1,128)} %seg_branch.1, bf16[256,1024]{1,0:T(8,128)(2,1)} %q_hbm.1, bf16[256,1024]{1,0:T(8,128)(2,1)} %o_hbm.1, bf16[256,1024]{1,0:T(8,128)(2,1)} %g_hbm.1, ...), custom_call_target="tpu_custom_call" | custom-call | flops 4000000000 | bytes 5000000 | tf_op jit(solution)/shard_map/prepare/pallas_call | solution.py:294
  18.4 0.0 collective-permute-done.2.z3
  18.4 0.0 collective-permute-done.1.z2
  18.4 0.0 collective-permute-done.z1
  18.4 0.1 collective-permute-start.6
  18.5 0.7 pack.1
  19.2 1.6 %collective-permute-start.5 = (bf16[256,256]{1,0:T(8,128)(2,1)}, bf16[256,256]{1,0:T(8,128)(2,1)}, u32[]{:S(2)}, u32[]{:S(2)}) collective-permute-start(bf16[256,256]{1,0:T(8,128)(2,1)} %get-tuple-element.54.kv0), channel_id=1, source_target_pairs={{0,8},{8,16},{16,24},{24,0},{1,9},{9,17},{17,25},{25,1},{2,10},{10... | collective-permute-start | bytes 393224 | tf_op jit(solution)/shard_map/ppermute | solution.py:269
  20.7 2.9 %collective-permute-start.4 = (bf16[256,256]{1,0:T(8,128)(2,1)}, bf16[256,256]{1,0:T(8,128)(2,1)}, u32[]{:S(2)}, u32[]{:S(2)}) collective-permute-start(bf16[256,256]{1,0:T(8,128)(2,1)} %get-tuple-element.54.kv0), channel_id=1, source_target_pairs={{0,16},{8,24},{16,0},{24,8},{1,17},{9,25},{17,1},{25,9},{2,18},{10... | collective-permute-start | bytes 393224 | tf_op jit(solution)/shard_map/ppermute | solution.py:269
  23.6 1.3 %collective-permute-start.3 = (bf16[256,256]{1,0:T(8,128)(2,1)}, bf16[256,256]{1,0:T(8,128)(2,1)}, u32[]{:S(2)}, u32[]{:S(2)}) collective-permute-start(bf16[256,256]{1,0:T(8,128)(2,1)} %get-tuple-element.54.kv0), channel_id=1, source_target_pairs={{0,24},{8,0},{16,8},{24,16},{1,25},{9,1},{17,9},{25,17},{2,26},{10... | collective-permute-start | bytes 393224 | tf_op jit(solution)/shard_map/ppermute | solution.py:269
  25.0 0.1 pad_add_fusion.place
  25.1 0.0 collective-permute-done.6.qg1.qg_ref
  25.1 0.7 collective-permute-start.12
  25.8 0.8 collective-permute-start.11
  26.6 0.1 collective-permute-done.5.kv3
  26.6 2.1 %collective-permute-start.10 = (bf16[256,256]{1,0:T(8,128)(2,1)S(1)}, bf16[256,256]{1,0:T(8,128)(2,1)S(1)}, u32[]{:S(2)}, u32[]{:S(2)}) collective-permute-start(bf16[256,256]{1,0:T(8,128)(2,1)S(1)} %get-tuple-element.62.kv0), channel_id=1, source_target_pairs={{0,24},{8,0},{16,8},{24,16},{1,25},{9,1},{17,9},{25,17},{2,26},{10... | collective-permute-start | bytes 393224 | tf_op jit(solution)/shard_map/ppermute | solution.py:269
  28.8 2.2 %collective-permute-done.4.kv2 = bf16[256,256]{1,0:T(8,128)(2,1)} collective-permute-done((bf16[256,256]{1,0:T(8,128)(2,1)}, bf16[256,256]{1,0:T(8,128)(2,1)}, u32[]{:S(2)}, u32[]{:S(2)}) %collective-permute-start.4) | collective-permute-done | bytes 131104 | tf_op jit(solution)/shard_map/ppermute | solution.py:269
  31.0 0.0 collective-permute-done.3.kv1
  31.0 12.2 %root.1 = (f32[128,2048]{1,0:T(8,128)S(1)}, f32[128,2048]{1,0:T(8,128)S(1)}, bf16[256,256]{1,0:T(8,128)(2,1)S(1)}, bf16[256,256]{1,0:T(8,128)(2,1)S(1)}, bf16[25...) custom-call(bf16[256,256]{1,0:T(8,128)(2,1)} %get-tuple-element.54.kv0, bf16[256,256]{1,0:T(8,128)(2,1)} %collective-permute-done.3.kv1, ...), custom_call_target="tpu_custom_call" | custom-call | flops 10000000000 | bytes 8000000 | tf_op jit(solution)/shard_map/root/pallas_call | solution.py:328
  43.2 2.1 %collective-permute-start.7 = (bf16[256,256]{1,0:T(8,128)(2,1)S(1)}, bf16[256,256]{1,0:T(8,128)(2,1)S(1)}, u32[]{:S(2)}, u32[]{:S(2)}) collective-permute-start(bf16[256,256]{1,0:T(8,128)(2,1)S(1)} %get-tuple-element.59), channel_id=1, source_target_pairs={{0,8},{8,16},{16,24},{24,0},{1,9},{9,17},{17,25},{25,1},{2,10},{10... | collective-permute-start | bytes 393224 | tf_op jit(solution)/shard_map/ppermute | solution.py:269
  45.3 3.8 %collective-permute-start.8 = (bf16[256,256]{1,0:T(8,128)(2,1)S(1)}, bf16[256,256]{1,0:T(8,128)(2,1)S(1)}, u32[]{:S(2)}, u32[]{:S(2)}) collective-permute-start(bf16[256,256]{1,0:T(8,128)(2,1)S(1)} %get-tuple-element.60), channel_id=1, source_target_pairs={{0,16},{8,24},{16,0},{24,8},{1,17},{9,25},{17,1},{25,9},{2,18},{10... | collective-permute-start | bytes 393224 | tf_op jit(solution)/shard_map/ppermute | solution.py:269
  49.1 0.0 collective-permute-done.12.kv3
  49.1 0.0 collective-permute-start.9
  49.1 0.0 collective-permute-done.11.kv2
  49.2 0.0 collective-permute-done.10.kv1
  49.2 5.8 %branch_other.1 = (f32[128,2048]{1,0:T(8,128)S(1)}, bf16[1024,256]{1,0:T(8,128)(2,1)S(1)}, f32[1024,256]{1,0:T(8,128)S(1)}) custom-call(s32[4]{0:T(128)S(1)} %pad_add_fusion.place, s32[16]{0:T(128)S(1)} %copy-done, bf16[256,256]{1,0:T(8,128)(2,1)S(1)} %get-tuple-element.62.kv0, ...), custom_call_target="tpu_custom_call", output_to_operand_aliasing={{0}: (7, {})} | custom-call | flops 4499999744 | bytes 5000000 | tf_op jit(solution)/shard_map/branch_other/pallas_call | solution.py:341
  55.0 0.0 collective-permute-done.7
  55.0 0.0 collective-permute-done.8
  55.0 0.0 collective-permute-done.9
  55.0 0.1 collective-permute-start.16
  55.1 0.1 add_convert_fusion.1
  55.2 2.2 %collective-permute-start.15 = (bf16[64,256]{1,0:T(8,128)(2,1)S(1)}, bf16[64,256]{1,0:T(8,128)(2,1)S(1)}, u32[]{:S(2)}, u32[]{:S(2)}) collective-permute-start(bf16[64,256]{1,0:T(8,128)(2,1)S(1)} %get-tuple-element.98), channel_id=1, source_target_pairs={{0,6},{2,0},{4,2},{6,4},{1,7},{3,1},{5,3},{7,5},{8,14},{10,8},{12,... | collective-permute-start | bytes 98312 | tf_op jit(solution)/shard_map/ppermute | solution.py:269
  57.5 2.2 %collective-permute-start.14 = (bf16[64,256]{1,0:T(8,128)(2,1)S(1)}, bf16[64,256]{1,0:T(8,128)(2,1)S(1)}, u32[]{:S(2)}, u32[]{:S(2)}) collective-permute-start(bf16[64,256]{1,0:T(8,128)(2,1)S(1)} %get-tuple-element.99), channel_id=1, source_target_pairs={{0,4},{2,6},{4,0},{6,2},{1,5},{3,7},{5,1},{7,3},{8,12},{10,14},{12... | collective-permute-start | bytes 98312 | tf_op jit(solution)/shard_map/ppermute | solution.py:269
  59.6 1.3 %collective-permute-start.13 = (bf16[64,256]{1,0:T(8,128)(2,1)S(1)}, bf16[64,256]{1,0:T(8,128)(2,1)S(1)}, u32[]{:S(2)}, u32[]{:S(2)}) collective-permute-start(bf16[64,256]{1,0:T(8,128)(2,1)S(1)} %get-tuple-element.100), channel_id=1, source_target_pairs={{0,2},{2,4},{4,6},{6,0},{1,3},{3,5},{5,7},{7,1},{8,10},{10,12},{12... | collective-permute-start | bytes 98312 | tf_op jit(solution)/shard_map/ppermute | solution.py:269
  60.9 5.7 %branch_own.1 = (f32[128,2048]{1,0:T(8,128)S(1)}, bf16[256,256]{1,0:T(8,128)(2,1)S(1)}, bf16[256,256]{1,0:T(8,128)(2,1)S(1)}, bf16[256,256]{1,0:T(8,128)(2,1)S(1)}, bf16[256,256]{1,0:T(8,128)(2,1)S(1)}) custom-call(s32[4]{0:T(128)S(1)} %pad_add_fusion.place, s32[16]{0:T(128)S(1)} %copy-done, ...), custom_call_target="tpu_custom_call", output_to_operand_aliasing={{0}: (5, {})} | custom-call | flops 4499999744 | bytes 5000000 | tf_op jit(solution)/shard_map/branch_own/pallas_call | solution.py:357
  66.6 0.0 collective-permute-done.15
  66.6 0.0 collective-permute-done.14
  66.6 0.0 collective-permute-done.13
  66.7 0.0 collective-permute-done.16.other
  66.7 2.1 %collective-permute-start.20 = (bf16[256,256]{1,0:T(8,128)(2,1)S(1)}, bf16[256,256]{1,0:T(8,128)(2,1)S(1)}, u32[]{:S(2)}, u32[]{:S(2)}) collective-permute-start(bf16[256,256]{1,0:T(8,128)(2,1)S(1)} %get-tuple-element.90), channel_id=1, source_target_pairs={{0,8},{8,16},{16,24},{24,0},{1,9},{9,17},{17,25},{25,1},{2,10},{10... | collective-permute-start | bytes 393224 | tf_op jit(solution)/shard_map/ppermute | solution.py:269
  68.8 0.0 collective-permute-start.21
  68.8 2.8 %collective-permute-start.22 = (bf16[256,256]{1,0:T(8,128)(2,1)S(1)}, bf16[256,256]{1,0:T(8,128)(2,1)S(1)}, u32[]{:S(2)}, u32[]{:S(2)}) collective-permute-start(bf16[256,256]{1,0:T(8,128)(2,1)S(1)} %get-tuple-element.92), channel_id=1, source_target_pairs={{0,24},{8,0},{16,8},{24,16},{1,25},{9,1},{17,9},{25,17},{2,26},{10... | collective-permute-start | bytes 393224 | tf_op jit(solution)/shard_map/ppermute | solution.py:269
  71.5 0.6 collective-permute-start.17
  72.2 1.6 %finish.1 = bf16[256,1024]{1,0:T(8,128)(2,1)} custom-call(bf16[256,256]{1,0:T(8,128)(2,1)S(1)} %get-tuple-element.83.onehot_ref, f32[128,2048]{1,0:T(8,128)S(1)} %get-tuple-element.84.leaf, f32[128,2048]{1,0:T(8,128)S(1)} %get-tuple-element.85.mine, f32[128,2048]{1,0:T(8,128)S(1)} %collective-permute-done.16.other), custom_call_target="tpu_custom_call" | custom-call | flops 200000000 | bytes 3000000 | tf_op jit(solution)/shard_map/finish/pallas_call | solution.py:371
  73.7 2.2 %collective-permute-done.17 = f32[64,256]{1,0:T(8,128)S(1)} collective-permute-done((f32[64,256]{1,0:T(8,128)S(1)}, f32[64,256]{1,0:T(8,128)S(1)}, u32[]{:S(2)}, u32[]{:S(2)}) %collective-permute-start.17) | collective-permute-done | bytes 65568 | tf_op jit(solution)/shard_map/ppermute | solution.py:381
  75.9 1.6 %collective-permute-start.18 = (f32[64,256]{1,0:T(8,128)S(1)}, f32[64,256]{1,0:T(8,128)S(1)}, u32[]{:S(2)}, u32[]{:S(2)}) collective-permute-start(f32[64,256]{1,0:T(8,128)S(1)} %add.55), channel_id=1, source_target_pairs={{0,96},{96,0},{32,64},{64,32},{1,97},{97,1},{33,65},{65,33},{2,98}... | collective-permute-start | bytes 196616 | tf_op jit(solution)/shard_map/ppermute | solution.py:384
  77.5 0.0 collective-permute-done.20
  77.5 0.0 collective-permute-done.21
  77.5 0.0 collective-permute-done.22
  77.5 0.1 add_convert_fusion
  77.6 2.6 %collective-permute-start.23 = (bf16[2,32,256]{2,1,0:T(8,128)(2,1)S(1)}, bf16[2,32,256]{2,1,0:T(8,128)(2,1)S(1)}, u32[]{:S(2)}, u32[]{:S(2)}) collective-permute-start(bf16[2,32,256]{2,1,0:T(8,128)(2,1)S(1)} %bitcast.15), channel_id=1, source_target_pairs={{0,2},{2,4},{4,6},{6,0},{1,3},{3,5},{5,7},{7,1},{8,10},{10,12},{12... | collective-permute-start | bytes 98312 | tf_op jit(solution)/shard_map/ppermute | solution.py:269
  80.1 1.7 %collective-permute-start.25 = (bf16[2,32,256]{2,1,0:T(8,128)(2,1)S(1)}, bf16[2,32,256]{2,1,0:T(8,128)(2,1)S(1)}, u32[]{:S(2)}, u32[]{:S(2)}) collective-permute-start(bf16[2,32,256]{2,1,0:T(8,128)(2,1)S(1)} %bitcast.14), channel_id=1, source_target_pairs={{0,6},{2,0},{4,2},{6,4},{1,7},{3,1},{5,3},{7,5},{8,14},{10,8},{12,... | collective-permute-start | bytes 98312 | tf_op jit(solution)/shard_map/ppermute | solution.py:269
  81.8 3.5 %collective-permute-start.24 = (bf16[2,32,256]{2,1,0:T(8,128)(2,1)S(1)}, bf16[2,32,256]{2,1,0:T(8,128)(2,1)S(1)}, u32[]{:S(2)}, u32[]{:S(2)}) collective-permute-start(bf16[2,32,256]{2,1,0:T(8,128)(2,1)S(1)} %bitcast.13), channel_id=1, source_target_pairs={{0,4},{2,6},{4,0},{6,2},{1,5},{3,7},{5,1},{7,3},{8,12},{10,14},{12... | collective-permute-start | bytes 98312 | tf_op jit(solution)/shard_map/ppermute | solution.py:269
  85.3 0.0 collective-permute-done.18
  85.4 1.1 %collective-permute-start.19 = (f32[64,256]{1,0:T(8,128)S(1)}, f32[64,256]{1,0:T(8,128)S(1)}, u32[]{:S(2)}, u32[]{:S(2)}) collective-permute-start(f32[64,256]{1,0:T(8,128)S(1)} %add.56), channel_id=1, source_target_pairs={{0,128},{128,0},{1,129},{129,1},{2,130},{130,2},{3,131},{131,3},{4... | collective-permute-start | bytes 196616 | tf_op jit(solution)/shard_map/ppermute | solution.py:269
  86.5 0.0 collective-permute-done.23
  86.5 0.0 collective-permute-done.25
  86.5 3.3 %collective-permute-done.24 = bf16[2,32,256]{2,1,0:T(8,128)(2,1)S(1)} collective-permute-done((bf16[2,32,256]{2,1,0:T(8,128)(2,1)S(1)}, bf16[2,32,256]{2,1,0:T(8,128)(2,1)S(1)}, u32[]{:S(2)}, u32[]{:S(2)}) %collective-permute-start.24) | collective-permute-done | bytes 32800 | tf_op jit(solution)/shard_map/ppermute | solution.py:269
  89.7 0.6 convert_add_fusion
  90.4 0.0 collective-permute-done.19
  90.4 0.6 add.57
  (7 shorter events, 0.1 us)
Async XLA Ops:
  1.4 16.9 %collective-permute-start.2 = (bf16[128,256]{1,0:T(8,128)(2,1)S(1)}, bf16[128,256]{1,0:T(8,128)(2,1)S(1)}, u32[]{:S(2)}, u32[]{:S(2)}) collective-permute-start(bf16[128,256]{1,0:T(8,128)(2,1)S(1)} %pad_maximum_fusion.z0), channel_id=1, source_target_pairs={{0,2},{2,4},{4,6},{6,0},{1,3},{3,5},{5,7},{7,1},{8,10},{10,12},{12... | collective-permute-start | bytes 196616 | tf_op jit(solution)/shard_map/ppermute | solution.py:269
  4.7 13.7 %collective-permute-start.1 = (bf16[128,256]{1,0:T(8,128)(2,1)S(1)}, bf16[128,256]{1,0:T(8,128)(2,1)S(1)}, u32[]{:S(2)}, u32[]{:S(2)}) collective-permute-start(bf16[128,256]{1,0:T(8,128)(2,1)S(1)} %pad_maximum_fusion.z0), channel_id=1, source_target_pairs={{0,4},{2,6},{4,0},{6,2},{1,5},{3,7},{5,1},{7,3},{8,12},{10,14},{12... | collective-permute-start | bytes 196616 | tf_op jit(solution)/shard_map/ppermute | solution.py:269
  10.1 8.3 %collective-permute-start = (bf16[128,256]{1,0:T(8,128)(2,1)S(1)}, bf16[128,256]{1,0:T(8,128)(2,1)S(1)}, u32[]{:S(2)}, u32[]{:S(2)}) collective-permute-start(bf16[128,256]{1,0:T(8,128)(2,1)S(1)} %pad_maximum_fusion.z0), channel_id=1, source_target_pairs={{0,6},{2,0},{4,2},{6,4},{1,7},{3,1},{5,3},{7,5},{8,14},{10,8},{12,... | collective-permute-start | bytes 196616 | tf_op jit(solution)/shard_map/ppermute | solution.py:269
  18.4 6.7 %collective-permute-start.6 = (bf16[4224,128]{1,0:T(8,128)(2,1)S(1)}, bf16[4224,128]{1,0:T(8,128)(2,1)S(1)}, u32[]{:S(2)}, u32[]{:S(2)}) collective-permute-start(bf16[4224,128]{1,0:T(8,128)(2,1)S(1)} %get-tuple-element.55.qg0.qg_ref), channel_id=1, source_target_pairs={{0,1},{1,0},{2,3},{3,2},{4,5},{5,4},{6,7},{7,6},{8,9},{9,8},{10,11... | collective-permute-start | bytes 3244040 | tf_op jit(solution)/shard_map/ppermute | solution.py:269
  19.2 7.5 %collective-permute-start.5 = (bf16[256,256]{1,0:T(8,128)(2,1)}, bf16[256,256]{1,0:T(8,128)(2,1)}, u32[]{:S(2)}, u32[]{:S(2)}) collective-permute-start(bf16[256,256]{1,0:T(8,128)(2,1)} %get-tuple-element.54.kv0), channel_id=1, source_target_pairs={{0,8},{8,16},{16,24},{24,0},{1,9},{9,17},{17,25},{25,1},{2,10},{10... | collective-permute-start | bytes 393224 | tf_op jit(solution)/shard_map/ppermute | solution.py:269
  20.7 10.3 %collective-permute-start.4 = (bf16[256,256]{1,0:T(8,128)(2,1)}, bf16[256,256]{1,0:T(8,128)(2,1)}, u32[]{:S(2)}, u32[]{:S(2)}) collective-permute-start(bf16[256,256]{1,0:T(8,128)(2,1)} %get-tuple-element.54.kv0), channel_id=1, source_target_pairs={{0,16},{8,24},{16,0},{24,8},{1,17},{9,25},{17,1},{25,9},{2,18},{10... | collective-permute-start | bytes 393224 | tf_op jit(solution)/shard_map/ppermute | solution.py:269
  23.6 7.4 %collective-permute-start.3 = (bf16[256,256]{1,0:T(8,128)(2,1)}, bf16[256,256]{1,0:T(8,128)(2,1)}, u32[]{:S(2)}, u32[]{:S(2)}) collective-permute-start(bf16[256,256]{1,0:T(8,128)(2,1)} %get-tuple-element.54.kv0), channel_id=1, source_target_pairs={{0,24},{8,0},{16,8},{24,16},{1,25},{9,1},{17,9},{25,17},{2,26},{10... | collective-permute-start | bytes 393224 | tf_op jit(solution)/shard_map/ppermute | solution.py:269
  25.1 24.1 %copy-start = (s32[16]{0:T(128)S(1)}, s32[16]{0:T(128)}, u32[]{:S(2)}) copy-start(s32[16]{0:T(128)} %lengths.3) | copy-start | bytes 196
  25.1 24.1 %collective-permute-start.12 = (bf16[256,256]{1,0:T(8,128)(2,1)S(1)}, bf16[256,256]{1,0:T(8,128)(2,1)S(1)}, u32[]{:S(2)}, u32[]{:S(2)}) collective-permute-start(bf16[256,256]{1,0:T(8,128)(2,1)S(1)} %get-tuple-element.62.kv0), channel_id=1, source_target_pairs={{0,8},{8,16},{16,24},{24,0},{1,9},{9,17},{17,25},{25,1},{2,10},{10... | collective-permute-start | bytes 393224 | tf_op jit(solution)/shard_map/ppermute | solution.py:269
  25.8 23.4 %collective-permute-start.11 = (bf16[256,256]{1,0:T(8,128)(2,1)S(1)}, bf16[256,256]{1,0:T(8,128)(2,1)S(1)}, u32[]{:S(2)}, u32[]{:S(2)}) collective-permute-start(bf16[256,256]{1,0:T(8,128)(2,1)S(1)} %get-tuple-element.62.kv0), channel_id=1, source_target_pairs={{0,16},{8,24},{16,0},{24,8},{1,17},{9,25},{17,1},{25,9},{2,18},{10... | collective-permute-start | bytes 393224 | tf_op jit(solution)/shard_map/ppermute | solution.py:269
  26.6 22.5 %collective-permute-start.10 = (bf16[256,256]{1,0:T(8,128)(2,1)S(1)}, bf16[256,256]{1,0:T(8,128)(2,1)S(1)}, u32[]{:S(2)}, u32[]{:S(2)}) collective-permute-start(bf16[256,256]{1,0:T(8,128)(2,1)S(1)} %get-tuple-element.62.kv0), channel_id=1, source_target_pairs={{0,24},{8,0},{16,8},{24,16},{1,25},{9,1},{17,9},{25,17},{2,26},{10... | collective-permute-start | bytes 393224 | tf_op jit(solution)/shard_map/ppermute | solution.py:269
  43.2 11.8 %collective-permute-start.7 = (bf16[256,256]{1,0:T(8,128)(2,1)S(1)}, bf16[256,256]{1,0:T(8,128)(2,1)S(1)}, u32[]{:S(2)}, u32[]{:S(2)}) collective-permute-start(bf16[256,256]{1,0:T(8,128)(2,1)S(1)} %get-tuple-element.59), channel_id=1, source_target_pairs={{0,8},{8,16},{16,24},{24,0},{1,9},{9,17},{17,25},{25,1},{2,10},{10... | collective-permute-start | bytes 393224 | tf_op jit(solution)/shard_map/ppermute | solution.py:269
  45.3 9.7 %collective-permute-start.8 = (bf16[256,256]{1,0:T(8,128)(2,1)S(1)}, bf16[256,256]{1,0:T(8,128)(2,1)S(1)}, u32[]{:S(2)}, u32[]{:S(2)}) collective-permute-start(bf16[256,256]{1,0:T(8,128)(2,1)S(1)} %get-tuple-element.60), channel_id=1, source_target_pairs={{0,16},{8,24},{16,0},{24,8},{1,17},{9,25},{17,1},{25,9},{2,18},{10... | collective-permute-start | bytes 393224 | tf_op jit(solution)/shard_map/ppermute | solution.py:269
  49.1 5.9 %collective-permute-start.9 = (bf16[256,256]{1,0:T(8,128)(2,1)S(1)}, bf16[256,256]{1,0:T(8,128)(2,1)S(1)}, u32[]{:S(2)}, u32[]{:S(2)}) collective-permute-start(bf16[256,256]{1,0:T(8,128)(2,1)S(1)} %get-tuple-element.61), channel_id=1, source_target_pairs={{0,24},{8,0},{16,8},{24,16},{1,25},{9,1},{17,9},{25,17},{2,26},{10... | collective-permute-start | bytes 393224 | tf_op jit(solution)/shard_map/ppermute | solution.py:269
  55.0 11.6 %collective-permute-start.16 = (f32[128,2048]{1,0:T(8,128)S(1)}, f32[128,2048]{1,0:T(8,128)S(1)}, u32[]{:S(2)}, u32[]{:S(2)}) collective-permute-start(f32[128,2048]{1,0:T(8,128)S(1)} %get-tuple-element.70), channel_id=1, source_target_pairs={{0,1},{1,0},{2,3},{3,2},{4,5},{5,4},{6,7},{7,6},{8,9},{9,8},{10,11... | collective-permute-start | bytes 3145736 | tf_op jit(solution)/shard_map/ppermute | solution.py:269
  55.2 11.4 %collective-permute-start.15 = (bf16[64,256]{1,0:T(8,128)(2,1)S(1)}, bf16[64,256]{1,0:T(8,128)(2,1)S(1)}, u32[]{:S(2)}, u32[]{:S(2)}) collective-permute-start(bf16[64,256]{1,0:T(8,128)(2,1)S(1)} %get-tuple-element.98), channel_id=1, source_target_pairs={{0,6},{2,0},{4,2},{6,4},{1,7},{3,1},{5,3},{7,5},{8,14},{10,8},{12,... | collective-permute-start | bytes 98312 | tf_op jit(solution)/shard_map/ppermute | solution.py:269
  57.5 9.2 %collective-permute-start.14 = (bf16[64,256]{1,0:T(8,128)(2,1)S(1)}, bf16[64,256]{1,0:T(8,128)(2,1)S(1)}, u32[]{:S(2)}, u32[]{:S(2)}) collective-permute-start(bf16[64,256]{1,0:T(8,128)(2,1)S(1)} %get-tuple-element.99), channel_id=1, source_target_pairs={{0,4},{2,6},{4,0},{6,2},{1,5},{3,7},{5,1},{7,3},{8,12},{10,14},{12... | collective-permute-start | bytes 98312 | tf_op jit(solution)/shard_map/ppermute | solution.py:269
  59.6 7.0 %collective-permute-start.13 = (bf16[64,256]{1,0:T(8,128)(2,1)S(1)}, bf16[64,256]{1,0:T(8,128)(2,1)S(1)}, u32[]{:S(2)}, u32[]{:S(2)}) collective-permute-start(bf16[64,256]{1,0:T(8,128)(2,1)S(1)} %get-tuple-element.100), channel_id=1, source_target_pairs={{0,2},{2,4},{4,6},{6,0},{1,3},{3,5},{5,7},{7,1},{8,10},{10,12},{12... | collective-permute-start | bytes 98312 | tf_op jit(solution)/shard_map/ppermute | solution.py:269
  66.7 10.8 %collective-permute-start.20 = (bf16[256,256]{1,0:T(8,128)(2,1)S(1)}, bf16[256,256]{1,0:T(8,128)(2,1)S(1)}, u32[]{:S(2)}, u32[]{:S(2)}) collective-permute-start(bf16[256,256]{1,0:T(8,128)(2,1)S(1)} %get-tuple-element.90), channel_id=1, source_target_pairs={{0,8},{8,16},{16,24},{24,0},{1,9},{9,17},{17,25},{25,1},{2,10},{10... | collective-permute-start | bytes 393224 | tf_op jit(solution)/shard_map/ppermute | solution.py:269
  68.8 8.7 %collective-permute-start.21 = (bf16[256,256]{1,0:T(8,128)(2,1)S(1)}, bf16[256,256]{1,0:T(8,128)(2,1)S(1)}, u32[]{:S(2)}, u32[]{:S(2)}) collective-permute-start(bf16[256,256]{1,0:T(8,128)(2,1)S(1)} %get-tuple-element.91), channel_id=1, source_target_pairs={{0,16},{8,24},{16,0},{24,8},{1,17},{9,25},{17,1},{25,9},{2,18},{10... | collective-permute-start | bytes 393224 | tf_op jit(solution)/shard_map/ppermute | solution.py:269
  68.8 8.7 %collective-permute-start.22 = (bf16[256,256]{1,0:T(8,128)(2,1)S(1)}, bf16[256,256]{1,0:T(8,128)(2,1)S(1)}, u32[]{:S(2)}, u32[]{:S(2)}) collective-permute-start(bf16[256,256]{1,0:T(8,128)(2,1)S(1)} %get-tuple-element.92), channel_id=1, source_target_pairs={{0,24},{8,0},{16,8},{24,16},{1,25},{9,1},{17,9},{25,17},{2,26},{10... | collective-permute-start | bytes 393224 | tf_op jit(solution)/shard_map/ppermute | solution.py:269
  71.5 4.4 %collective-permute-start.17 = (f32[64,256]{1,0:T(8,128)S(1)}, f32[64,256]{1,0:T(8,128)S(1)}, u32[]{:S(2)}, u32[]{:S(2)}) collective-permute-start(f32[64,256]{1,0:T(8,128)S(1)} %convert_add_fusion.1), channel_id=1, source_target_pairs={{0,32},{32,0},{64,96},{96,64},{1,33},{33,1},{65,97},{97,65},{2,34}... | collective-permute-start | bytes 196616 | tf_op jit(solution)/shard_map/ppermute | solution.py:381
  75.9 9.4 %collective-permute-start.18 = (f32[64,256]{1,0:T(8,128)S(1)}, f32[64,256]{1,0:T(8,128)S(1)}, u32[]{:S(2)}, u32[]{:S(2)}) collective-permute-start(f32[64,256]{1,0:T(8,128)S(1)} %add.55), channel_id=1, source_target_pairs={{0,96},{96,0},{32,64},{64,32},{1,97},{97,1},{33,65},{65,33},{2,98}... | collective-permute-start | bytes 196616 | tf_op jit(solution)/shard_map/ppermute | solution.py:384
  77.6 8.9 %collective-permute-start.23 = (bf16[2,32,256]{2,1,0:T(8,128)(2,1)S(1)}, bf16[2,32,256]{2,1,0:T(8,128)(2,1)S(1)}, u32[]{:S(2)}, u32[]{:S(2)}) collective-permute-start(bf16[2,32,256]{2,1,0:T(8,128)(2,1)S(1)} %bitcast.15), channel_id=1, source_target_pairs={{0,2},{2,4},{4,6},{6,0},{1,3},{3,5},{5,7},{7,1},{8,10},{10,12},{12... | collective-permute-start | bytes 98312 | tf_op jit(solution)/shard_map/ppermute | solution.py:269
  80.1 6.3 %collective-permute-start.25 = (bf16[2,32,256]{2,1,0:T(8,128)(2,1)S(1)}, bf16[2,32,256]{2,1,0:T(8,128)(2,1)S(1)}, u32[]{:S(2)}, u32[]{:S(2)}) collective-permute-start(bf16[2,32,256]{2,1,0:T(8,128)(2,1)S(1)} %bitcast.14), channel_id=1, source_target_pairs={{0,6},{2,0},{4,2},{6,4},{1,7},{3,1},{5,3},{7,5},{8,14},{10,8},{12,... | collective-permute-start | bytes 98312 | tf_op jit(solution)/shard_map/ppermute | solution.py:269
  81.8 7.9 %collective-permute-start.24 = (bf16[2,32,256]{2,1,0:T(8,128)(2,1)S(1)}, bf16[2,32,256]{2,1,0:T(8,128)(2,1)S(1)}, u32[]{:S(2)}, u32[]{:S(2)}) collective-permute-start(bf16[2,32,256]{2,1,0:T(8,128)(2,1)S(1)} %bitcast.13), channel_id=1, source_target_pairs={{0,4},{2,6},{4,0},{6,2},{1,5},{3,7},{5,1},{7,3},{8,12},{10,14},{12... | collective-permute-start | bytes 98312 | tf_op jit(solution)/shard_map/ppermute | solution.py:269
  85.4 5.0 %collective-permute-start.19 = (f32[64,256]{1,0:T(8,128)S(1)}, f32[64,256]{1,0:T(8,128)S(1)}, u32[]{:S(2)}, u32[]{:S(2)}) collective-permute-start(f32[64,256]{1,0:T(8,128)S(1)} %add.56), channel_id=1, source_target_pairs={{0,128},{128,0},{1,129},{129,1},{2,130},{130,2},{3,131},{131,3},{4... | collective-permute-start | bytes 196616 | tf_op jit(solution)/shard_map/ppermute | solution.py:269
